TPU v7x, 32 devices: a whole 2x2x4 slice. The times are simulated.
32 devices in a mesh: wide: 8 (over z, y), narrow: 4 (over x, core).
Axes of the slice: x: 2, y: 2, z: 4, core: 2. Of those that a mesh axis runs over, the one named last changes fastest.
Arguments:
- patches: bfloat16 [16384, 768], P('wide'), may hold values from -6 to 6
- norm_gain_attn: float32 [768], replicated, may hold values from 0.5 to 1.5
- norm_gain_mlp: float32 [768], replicated, may hold values from 0.5 to 1.5
- w_query: bfloat16 [768, 768], P('wide', 'narrow'), may hold values from -0.109375 to 0.109375
- w_key: bfloat16 [768, 768], P('wide', 'narrow'), may hold values from -0.109375 to 0.109375
- w_value: bfloat16 [768, 768], P('wide', 'narrow'), may hold values from -0.21875 to 0.21875
- w_out: bfloat16 [768, 768], P('narrow', 'wide'), may hold values from -0.625 to 0.625
- w_gate: bfloat16 [768, 2048], P('wide', 'narrow'), may hold values from -0.21875 to 0.21875
- w_up: bfloat16 [768, 2048], P('wide', 'narrow'), may hold values from -0.21875 to 0.21875
- w_down: bfloat16 [2048, 768], P('narrow', 'wide'), may hold values from -0.125 to 0.125
- cotangent: bfloat16 [16384, 768], P('wide'), may hold values from -6 to 6
- item_slots: int32 [32], P('wide'), may hold values from 512 to 2048, as said below
- valid_counts: int32 [32], P('wide'), may hold values from 1 to 2048, as said below
Outputs:
- output: bfloat16 [16384, 768], P('wide', 'narrow')
- grad_patches: float32 [16384, 768], P('wide', 'narrow')
- grad_gain_attn: float32 [768], replicated
- grad_gain_mlp: float32 [768], replicated
- grad_w_query: float32 [768, 768], P('wide', 'narrow')
- grad_w_key: float32 [768, 768], P('wide', 'narrow')
- grad_w_value: float32 [768, 768], P('wide', 'narrow')
- grad_w_out: float32 [768, 768], P('narrow', 'wide')
- grad_w_gate: float32 [768, 2048], P('wide', 'narrow')
- grad_w_up: float32 [768, 2048], P('wide', 'narrow')
- grad_w_down: float32 [2048, 768], P('narrow', 'wide')
- rms_values: float32 [3], replicated
Inputs may be any that keep to these rules, and one draw needn't show every extreme that they name: `item_slots`: each block of 512 slots carries the number of slots of its item: 512, 1024 or 2048. An item of b slots occupies b slots starting at a multiple of b, so no item crosses a multiple of 2048. `valid_counts`: each block carries the valid patch count of its item, the same on all the item's blocks and at most the item's slots; the first that many slots of the item are patches, the rest padding.
All inputs are finite; a program needn't handle non-finite values.
Results may differ from a plain program's by a relative error of at most 0.015.
Values may be sent and summed in bfloat16 or wider, within the bound.
No kernel may reach another device: no remote copies, remote signals or barrier semaphores. Data moves between devices by JAX's collectives and lax.ppermute only.
A program may use at most 128 MiB of HBM per device.

v0:
```python
import jax
import jax.numpy as jnp
from jax import lax
from jax.sharding import PartitionSpec as P

HEAD_DIM = 64
UNIT = 512
WINDOW = 2048


epsilon = 1e-06
masked_score = -1e30


def plain_dot(left, right):
    return jnp.dot(left, right, preferred_element_type=jnp.float32)


def contract_rows(left, right):
    return lax.dot_general(
        left, right, (((0,), (0,)), ((), ())), preferred_element_type=jnp.float32
    )


def contract_cols(left, right):
    return lax.dot_general(
        left, right, (((1,), (1,)), ((), ())), preferred_element_type=jnp.float32
    )


def spread_blocks(block_values, block_width):
    return (block_values[:, None] + jnp.zeros((1, block_width), jnp.int32)).reshape(-1)


def token_layout(slot_rows, valid_rows, slot_count):
    block_width = slot_count // slot_rows.shape[0]
    slot_tok = spread_blocks(slot_rows, block_width)
    valid_tok = spread_blocks(valid_rows, block_width)
    position = jnp.arange(slot_count, dtype=jnp.int32)
    item_start = position // slot_tok * slot_tok
    live_mask = position - item_start < valid_tok
    return (item_start, live_mask)


def row_total(row_values):
    return lax.psum(row_values, "narrow")


def block_scores(query_heads, key_heads, item_query, item_key, live_key):
    scores = jnp.einsum("qhe,khe->hqk", query_heads, key_heads, preferred_element_type=jnp.float32)
    allowed = (item_query[:, None] == item_key[None, :]) & live_key[None, :]
    return jnp.where(allowed[None, :, :], scores, masked_score)


def body(
    patches,
    norm_gain_attn,
    norm_gain_mlp,
    w_query,
    w_key,
    w_value,
    w_out,
    w_gate,
    w_up,
    w_down,
    cotangent,
    item_slots,
    valid_counts,
):
    full_query, full_key, full_value, full_out, full_gate, full_up, full_down = (
        lax.all_gather(w_query, "wide", axis=0, tiled=True),
        lax.all_gather(w_key, "wide", axis=0, tiled=True),
        lax.all_gather(w_value, "wide", axis=0, tiled=True),
        lax.all_gather(w_out, "wide", axis=1, tiled=True),
        lax.all_gather(w_gate, "wide", axis=0, tiled=True),
        lax.all_gather(w_up, "wide", axis=0, tiled=True),
        lax.all_gather(w_down, "wide", axis=1, tiled=True),
    )
    row_count = patches.shape[0]
    model_width = patches.shape[1]
    share_width = w_query.shape[1]
    heads_here = share_width // HEAD_DIM
    share_start = lax.axis_index("narrow") * share_width
    block_count = row_count // UNIT
    item_start, live_mask = token_layout(item_slots, valid_counts, row_count)
    keep_mask = live_mask.astype(jnp.float32)[:, None]
    inputs = patches.astype(jnp.float32)
    scale_in = lax.rsqrt(jnp.mean(inputs * inputs, axis=1, keepdims=True) + epsilon)
    normed = (inputs * scale_in * norm_gain_attn).astype(jnp.bfloat16)
    queries = plain_dot(normed, full_query).astype(jnp.bfloat16)
    key_rows = plain_dot(normed, full_key).astype(jnp.bfloat16)
    value_rows = plain_dot(normed, full_value).astype(jnp.bfloat16)

    def block_inputs(block_index):
        block_start = block_index * UNIT
        window_start = block_start // WINDOW * WINDOW
        query_heads = lax.dynamic_slice_in_dim(queries, block_start, UNIT, 0).reshape(
            UNIT, heads_here, HEAD_DIM
        )
        key_heads = key_rows.reshape(WINDOW, heads_here, HEAD_DIM)
        value_heads = value_rows.reshape(WINDOW, heads_here, HEAD_DIM)
        item_query = lax.dynamic_slice_in_dim(item_start, block_start, UNIT)
        scores = block_scores(query_heads, key_heads, item_query, item_start, live_mask)
        return (block_start, window_start, query_heads, key_heads, value_heads, scores)

    def attend_forward(block_index):
        block_start, window_start, query_heads, key_heads, value_heads, scores = block_inputs(
            block_index
        )
        row_max = jnp.max(scores, axis=-1, keepdims=True)
        exponent = jnp.exp(scores - row_max)
        exp_total = jnp.sum(exponent, axis=-1, keepdims=True)
        probabilities = (exponent / exp_total).astype(jnp.bfloat16)
        mixed_heads = jnp.einsum(
            "hqk,khe->qhe", probabilities, value_heads, preferred_element_type=jnp.float32
        )
        return (
            mixed_heads.reshape(UNIT, share_width).astype(jnp.bfloat16),
            (row_max + jnp.log(exp_total))[:, :, 0],
        )

    block_ids = jnp.arange(block_count, dtype=jnp.int32)
    heads_out, log_total = lax.map(attend_forward, block_ids)
    heads_out = heads_out.reshape(row_count, share_width)
    attn_share = lax.psum_scatter(
        plain_dot(heads_out, full_out), "narrow", scatter_dimension=1, tiled=True
    )
    own_inputs = lax.dynamic_slice_in_dim(inputs, share_start, share_width, 1)
    middle = own_inputs + attn_share
    gain_mid = lax.dynamic_slice_in_dim(norm_gain_mlp, share_start, share_width)
    scale_mid = lax.rsqrt(row_total(jnp.sum(middle * middle, axis=1)) / model_width + epsilon)[
        :, None
    ]
    mid_hat = middle * scale_mid
    normed_mid = lax.all_gather(
        (mid_hat * gain_mid).astype(jnp.bfloat16), "narrow", axis=1, tiled=True
    )
    gate_rows = plain_dot(normed_mid, full_gate)
    up_rows = plain_dot(normed_mid, full_up)
    hidden = (jax.nn.gelu(gate_rows, approximate=True) * up_rows).astype(jnp.bfloat16)
    mlp_share = lax.psum_scatter(
        plain_dot(hidden, full_down).astype(jnp.bfloat16), "narrow", scatter_dimension=1, tiled=True
    ).astype(jnp.float32)
    layer_out = keep_mask * (middle + mlp_share)
    output = layer_out.astype(jnp.bfloat16)
    stat_terms = jnp.stack(
        [
            jnp.sum(keep_mask * attn_share * attn_share),
            jnp.sum(keep_mask * mlp_share * mlp_share),
            jnp.sum(layer_out * layer_out),
            jnp.sum(keep_mask),
        ]
    )
    grad_mlp = jnp.where(live_mask[:, None], cotangent, jnp.zeros((), jnp.bfloat16))
    grad_w_down = contract_rows(hidden, grad_mlp)
    grad_hidden = contract_cols(grad_mlp, full_down)

    def gated_unit(gate_in, up_in):
        return jax.nn.gelu(gate_in, approximate=True) * up_in

    unused, gated_back = jax.vjp(gated_unit, gate_rows, up_rows)
    grad_gate, grad_up = gated_back(grad_hidden)
    grad_gate = grad_gate.astype(jnp.bfloat16)
    grad_up = grad_up.astype(jnp.bfloat16)
    grad_w_gate = contract_rows(normed_mid, grad_gate)
    grad_w_up = contract_rows(normed_mid, grad_up)
    grad_normed_mid = lax.psum_scatter(
        contract_cols(grad_gate, full_gate) + contract_cols(grad_up, full_up),
        "narrow",
        scatter_dimension=1,
        tiled=True,
    )
    scaled_mid = grad_normed_mid * gain_mid
    mean_mid = row_total(jnp.sum(scaled_mid * mid_hat, axis=1))[:, None] / model_width
    grad_middle = lax.dynamic_slice_in_dim(grad_mlp, share_start, share_width, 1).astype(
        jnp.float32
    )
    grad_middle = grad_middle + scale_mid * (scaled_mid - mid_hat * mean_mid)
    grad_gain_mid = jnp.sum(grad_normed_mid * mid_hat, axis=0)
    grad_attn = lax.all_gather(grad_middle.astype(jnp.bfloat16), "narrow", axis=1, tiled=True)
    grad_w_out = contract_rows(heads_out, grad_attn)
    grad_heads = contract_cols(grad_attn, full_out).astype(jnp.bfloat16)

    def attend_backward(running, pieces):
        grad_key_acc, grad_value_acc = running
        block_index, lse_block = pieces
        block_start, window_start, query_heads, key_heads, value_heads, scores = block_inputs(
            block_index
        )
        probabilities = jnp.exp(scores - lse_block[:, :, None])
        grad_out_heads = lax.dynamic_slice_in_dim(grad_heads, block_start, UNIT, 0).reshape(
            UNIT, heads_here, HEAD_DIM
        )
        grad_probs = jnp.einsum(
            "qhe,khe->hqk", grad_out_heads, value_heads, preferred_element_type=jnp.float32
        )
        weighted = jnp.sum(probabilities * grad_probs, axis=-1, keepdims=True)
        grad_scores = (probabilities * (grad_probs - weighted)).astype(jnp.bfloat16)
        grad_query_block = jnp.einsum(
            "hqk,khe->qhe", grad_scores, key_heads, preferred_element_type=jnp.float32
        )
        key_part = jnp.einsum(
            "hqk,qhe->khe", grad_scores, query_heads, preferred_element_type=jnp.float32
        )
        value_part = jnp.einsum(
            "hqk,qhe->khe",
            probabilities.astype(jnp.bfloat16),
            grad_out_heads,
            preferred_element_type=jnp.float32,
        )
        key_now = grad_key_acc + key_part.reshape(WINDOW, share_width)
        value_now = grad_value_acc + value_part.reshape(WINDOW, share_width)
        grad_key_acc = key_now
        grad_value_acc = value_now
        return (
            (grad_key_acc, grad_value_acc),
            grad_query_block.reshape(UNIT, share_width).astype(jnp.bfloat16),
        )

    zero_grads = jnp.zeros((row_count, share_width), jnp.float32)
    (grad_keys, grad_values), grad_queries = lax.scan(
        attend_backward, (zero_grads, zero_grads), (block_ids, log_total)
    )
    grad_queries = grad_queries.reshape(row_count, share_width)
    grad_keys = grad_keys.astype(jnp.bfloat16)
    grad_values = grad_values.astype(jnp.bfloat16)
    grad_w_query = contract_rows(normed, grad_queries)
    grad_w_key = contract_rows(normed, grad_keys)
    grad_w_value = contract_rows(normed, grad_values)
    grad_normed = lax.psum_scatter(
        contract_cols(grad_queries, full_query)
        + contract_cols(grad_keys, full_key)
        + contract_cols(grad_values, full_value),
        "narrow",
        scatter_dimension=1,
        tiled=True,
    )
    gain_in = lax.dynamic_slice_in_dim(norm_gain_attn, share_start, share_width)
    in_hat = own_inputs * scale_in
    scaled_in = grad_normed * gain_in
    mean_in = row_total(jnp.sum(scaled_in * in_hat, axis=1))[:, None] / model_width
    grad_patches = grad_middle + scale_in * (scaled_in - in_hat * mean_in)
    grad_gain_in = jnp.sum(grad_normed * in_hat, axis=0)
    grad_w_query, grad_w_key, grad_w_value, grad_w_out, grad_w_gate, grad_w_up, grad_w_down = (
        lax.psum_scatter(grad_w_query, "wide", scatter_dimension=0, tiled=True),
        lax.psum_scatter(grad_w_key, "wide", scatter_dimension=0, tiled=True),
        lax.psum_scatter(grad_w_value, "wide", scatter_dimension=0, tiled=True),
        lax.psum_scatter(grad_w_out, "wide", scatter_dimension=1, tiled=True),
        lax.psum_scatter(grad_w_gate, "wide", scatter_dimension=0, tiled=True),
        lax.psum_scatter(grad_w_up, "wide", scatter_dimension=0, tiled=True),
        lax.psum_scatter(grad_w_down, "wide", scatter_dimension=1, tiled=True),
    )
    zero_gain = jnp.zeros((model_width,), jnp.float32)
    placed_in = lax.dynamic_update_slice_in_dim(zero_gain, grad_gain_in, share_start, 0)
    placed_mid = lax.dynamic_update_slice_in_dim(zero_gain, grad_gain_mid, share_start, 0)
    total_in, total_mid, totals = lax.psum((placed_in, placed_mid, stat_terms), ("wide", "narrow"))
    rms_values = jnp.sqrt(totals[:3] * lax.axis_size("narrow") / (totals[3] * model_width))
    return (
        output,
        grad_patches,
        total_in,
        total_mid,
        grad_w_query,
        grad_w_key,
        grad_w_value,
        grad_w_out,
        grad_w_gate,
        grad_w_up,
        grad_w_down,
        rms_values,
    )


def solution(mesh):
    return jax.shard_map(
        body,
        mesh=mesh,
        in_specs=(
            P("wide", None),
            P(),
            P(),
            P("wide", "narrow"),
            P("wide", "narrow"),
            P("wide", "narrow"),
            P("narrow", "wide"),
            P("wide", "narrow"),
            P("wide", "narrow"),
            P("narrow", "wide"),
            P("wide", None),
            P("wide"),
            P("wide"),
        ),
        out_specs=(
            P("wide", "narrow"),
            P("wide", "narrow"),
            P(),
            P(),
            P("wide", "narrow"),
            P("wide", "narrow"),
            P("wide", "narrow"),
            P("narrow", "wide"),
            P("wide", "narrow"),
            P("wide", "narrow"),
            P("narrow", "wide"),
            P(),
        ),
        check_vma=False,
    )
```

profile of v0, /device:TPU:0, one launch (start us, length us, event | category | flops | bytes accessed | tf_op | source)
XLA Modules:
  0.0 1213.6 jit_solution(964622607015488310)
XLA Ops:
  9.6 35.1 %all_gather.30 = bf16[192,768]{0,1:T(8,128)(2,1)} all-gather(bf16[192,96]{0,1:T(8,128)(2,1)S(1)} %copy.38), channel_id=1, replica_groups=mesh['wide'=8,'narrow'=4] {'wide'}, dimensions={1}, use_global_device_ids=true | all-gather | bytes 331776 | tf_op jit(solution)/shard_map/all_gather | solution.py:74
  44.6 33.3 %all_gather.27 = bf16[768,192]{1,0:T(8,128)(2,1)} all-gather(bf16[96,192]{1,0:T(8,128)(2,1)} %param.20), channel_id=1, replica_groups=mesh['wide'=8,'narrow'=4] {'wide'}, dimensions={0}, use_global_device_ids=true | all-gather | bytes 331776 | tf_op jit(solution)/shard_map/all_gather | solution.py:71
  77.9 31.2 %all_gather.28 = bf16[768,192]{1,0:T(8,128)(2,1)S(1)} all-gather(bf16[96,192]{1,0:T(8,128)(2,1)} %param.21), channel_id=1, replica_groups=mesh['wide'=8,'narrow'=4] {'wide'}, dimensions={0}, use_global_device_ids=true | all-gather | bytes 331776 | tf_op jit(solution)/shard_map/all_gather | solution.py:72
  109.1 33.3 %all_gather.29 = bf16[768,192]{1,0:T(8,128)(2,1)} all-gather(bf16[96,192]{1,0:T(8,128)(2,1)} %param.22), channel_id=1, replica_groups=mesh['wide'=8,'narrow'=4] {'wide'}, dimensions={0}, use_global_device_ids=true | all-gather | bytes 331776 | tf_op jit(solution)/shard_map/all_gather | solution.py:73
  152.4 99.9 %while.28 = (s32[]{:T(128)}, bf16[4,512,192]{1,2,0:T(8,128)(2,1)S(1)}, f32[4,3,512]{2,1,0:T(4,128)}, s32[4]{0:T(128)S(1)}, s32[2048]{0:T(1024)S(1)}, /*index=5*/...) while((s32[]{:T(128)}, ...), condition=%wide.region_4.5_spmd.clone, body=%wide.region_1.4_spmd.clone.sunk | while | flops 835836416 | bytes 44830968 | solution.py:123
  155.8 6.7 select_reduce_fusion.2
  162.5 7.8 fusion.131
  170.2 6.6 fusion.132
  180.7 6.7 select_reduce_fusion.2
  187.4 7.8 fusion.131
  195.2 6.6 fusion.132
  205.7 6.7 select_reduce_fusion.2
  212.4 7.8 fusion.131
  220.1 6.6 fusion.132
  230.6 6.7 select_reduce_fusion.2
  237.3 7.8 fusion.131
  245.0 6.6 fusion.132
  257.1 5.4 convert_element_type.103
  263.2 53.3 %reduce-scatter.14.cloned.1.call-done = f32[2048,192]{0,1:T(8,128)} async-done(((f32[2048,768]{0,1:T(8,128)}), f32[2048,192]{0,1:T(8,128)}) %reduce-scatter.14.cloned.1.call-update) | async-done | bytes 1572880 | tf_op jit(solution)/shard_map/reduce_scatter | solution.py:125
  318.7 5.9 psum.42
  325.8 4.7 copy.39
  331.3 34.3 %all_gather.32 = bf16[768,512]{1,0:T(8,128)(2,1)} all-gather(bf16[96,512]{1,0:T(8,128)(2,1)S(1)} %copy-done.33), channel_id=1, replica_groups=mesh['wide'=8,'narrow'=4] {'wide'}, dimensions={0}, use_global_device_ids=true | all-gather | bytes 884736 | tf_op jit(solution)/shard_map/all_gather | solution.py:75
  365.6 32.5 %all_gather.33 = bf16[768,512]{1,0:T(8,128)(2,1)S(1)} all-gather(bf16[96,512]{1,0:T(8,128)(2,1)} %param.25), channel_id=1, replica_groups=mesh['wide'=8,'narrow'=4] {'wide'}, dimensions={0}, use_global_device_ids=true | all-gather | bytes 884736 | tf_op jit(solution)/shard_map/all_gather | solution.py:76
  398.1 34.6 %all_gather.34 = bf16[512,768]{0,1:T(8,128)(2,1)} all-gather(bf16[512,96]{0,1:T(8,128)(2,1)} %param.26), channel_id=1, replica_groups=mesh['wide'=8,'narrow'=4] {'wide'}, dimensions={1}, use_global_device_ids=true | all-gather | bytes 884736 | tf_op jit(solution)/shard_map/all_gather | solution.py:77
  436.4 3.9 fusion.49
  442.5 6.4 multiply_convert_fusion.2
  457.5 4.7 convolution_add_fusion
  462.3 30.8 %reduce-scatter.16.cloned.1.call-done = bf16[2048,192]{0,1:T(8,128)(2,1)} async-done(((bf16[2048,768]{0,1:T(8,128)(2,1)}), bf16[2048,192]{0,1:T(8,128)(2,1)}) %reduce-scatter.16.cloned.1.call-update) | async-done | bytes 786448 | tf_op jit(solution)/shard_map/reduce_scatter | solution.py:141
  493.0 60.8 %reduce-scatter.18.cloned.1.call-done = f32[2048,192]{0,1:T(8,128)} async-done(((f32[2048,768]{0,1:T(8,128)}), f32[2048,192]{0,1:T(8,128)}) %reduce-scatter.18.cloned.1.call-update) | async-done | bytes 1572880 | tf_op jit(solution)/shard_map/reduce_scatter | solution.py:167
  553.8 4.6 fusion.31
  558.5 6.5 psum.43
  569.4 29.8 %all-gather.5.cloned.1.call-done = bf16[2048,768]{0,1:T(8,128)(2,1)} async-done(((bf16[2048,192]{0,1:T(8,128)(2,1)}), bf16[2048,768]{0,1:T(8,128)(2,1)}) %all-gather.5.cloned.1.call-update) | async-done | bytes 3145744 | tf_op jit(solution)/shard_map/all_gather | solution.py:180
  607.6 130.3 %while.29 = (s32[]{:T(128)}, f32[2048,192]{0,1:T(8,128)}, f32[2048,192]{0,1:T(8,128)}, bf16[4,512,192]{1,2,0:T(8,128)(2,1)}, s32[4]{0:T(128)S(1)}, /*index=5*/bf...) while((s32[]{:T(128)}, f32[2048,192]{0,1:T(8,128)}, ...), condition=%wide.region_14.15_spmd.clone, body=%wide.region_12.14_spmd.clone.sunk | while | flops 2054806016 | bytes 182907440 | solution.py:221
  614.7 4.3 fusion.145
  619.0 5.4 multiply_reduce_fusion.9
  624.3 5.9 multiply_convert_fusion.6
  630.2 5.2 convolution_convert_fusion.7
  647.2 4.3 fusion.145
  651.5 5.4 multiply_reduce_fusion.9
  656.9 5.9 multiply_convert_fusion.6
  662.8 5.1 convolution_convert_fusion.7
  679.7 4.3 fusion.145
  684.0 5.4 multiply_reduce_fusion.9
  689.4 5.9 multiply_convert_fusion.6
  695.3 5.1 convolution_convert_fusion.7
  712.2 4.3 fusion.145
  716.5 5.4 multiply_reduce_fusion.9
  721.8 5.9 multiply_convert_fusion.6
  727.7 5.1 convolution_convert_fusion.7
  746.7 5.6 fusion.52
  752.3 5.9 fusion.53
  758.3 5.9 fusion.56
  764.2 4.0 fusion.51
  768.3 4.0 fusion.34
  782.6 22.6 %reduce-scatter.20.cloned.1.call-done = f32[2048,192]{0,1:T(8,128)} async-done(((f32[2048,768]{0,1:T(8,128)}), f32[2048,192]{0,1:T(8,128)}) %reduce-scatter.20.cloned.1.call-update) | async-done | bytes 1572880 | tf_op jit(solution)/shard_map/reduce_scatter | solution.py:230
  807.7 40.1 %all-reduce = (f32[768]{0:T(1024)}, f32[768]{0:T(1024)}, f32[4]{0:T(128)S(1)}) all-reduce(f32[768]{0:T(1024)S(1)} %dynamic_update_slice.17, f32[768]{0:T(1024)S(1)} %dynamic_update_slice.18, f32[4]{0:T(128)S(1)} %pad_maximum_fusion), channel_id=1, replica_groups=mesh['wide'=8,'narrow'=4] {'wide','narrow'}, use_global_device_ids=true, to_apply=%region_19.20 | all-reduce | flops 1540 | bytes 12320 | tf_op jit(solution)/shard_map/psum | solution.py:256
  849.1 6.9 psum.44
  856.5 4.1 multiply_add_fusion
  860.6 14.3 %reduce-scatter.28.cloned.1.call-done = f32[96,512]{1,0:T(8,128)} async-done(((f32[768,512]{1,0:T(8,128)}), f32[96,512]{1,0:T(8,128)}) %reduce-scatter.28.cloned.1.call-update) | async-done | bytes 196624 | tf_op jit(solution)/shard_map/reduce_scatter | solution.py:249
  874.9 67.8 %reduce-scatter.30.cloned.1.call-done = f32[96,512]{1,0:T(8,128)} async-done(((f32[768,512]{1,0:T(8,128)}), f32[96,512]{1,0:T(8,128)}) %reduce-scatter.30.cloned.1.call-update) | async-done | bytes 196624 | tf_op jit(solution)/shard_map/reduce_scatter | solution.py:250
  942.7 68.0 %reduce-scatter.32.cloned.1.call-done = f32[512,96]{0,1:T(8,128)} async-done(((f32[512,768]{0,1:T(8,128)}), f32[512,96]{0,1:T(8,128)}) %reduce-scatter.32.cloned.1.call-update) | async-done | bytes 196624 | tf_op jit(solution)/shard_map/reduce_scatter | solution.py:251
  1010.7 65.3 %reduce-scatter.22.cloned.1.call-done = f32[96,192]{1,0:T(8,128)} async-done(((f32[768,192]{1,0:T(8,128)}), f32[96,192]{1,0:T(8,128)}) %reduce-scatter.22.cloned.1.call-update) | async-done | bytes 73744 | tf_op jit(solution)/shard_map/reduce_scatter | solution.py:245
  1076.0 65.6 %reduce-scatter.26.cloned.1.call-done = f32[96,192]{1,0:T(8,128)} async-done(((f32[768,192]{1,0:T(8,128)}), f32[96,192]{1,0:T(8,128)}) %reduce-scatter.26.cloned.1.call-update) | async-done | bytes 73744 | tf_op jit(solution)/shard_map/reduce_scatter | solution.py:247
  1141.5 65.3 %reduce-scatter.24.cloned.1.call-done = f32[96,192]{1,0:T(8,128)} async-done(((f32[768,192]{1,0:T(8,128)}), f32[96,192]{1,0:T(8,128)}) %reduce-scatter.24.cloned.1.call-update) | async-done | bytes 73744 | tf_op jit(solution)/shard_map/reduce_scatter | solution.py:246
  (335 shorter events, 128.9 us)
Async XLA Ops:
  7.2 309.3 %reduce-scatter.14.cloned.1.call-start = ((), (), s32[]{:S(2)}) async-start(), calls=%async_computation.11 | async-start | bytes 7864320 | tf_op jit(solution)/shard_map/reduce_scatter | solution.py:125
  109.1 40.5 %copy-start.22 = (bf16[768,192]{1,0:T(8,128)(2,1)}, bf16[768,192]{1,0:T(8,128)(2,1)S(1)}, u32[]{:S(2)}) copy-start(bf16[768,192]{1,0:T(8,128)(2,1)S(1)} %all_gather.28) | copy-start | bytes 884740
  147.6 2.8 copy-start.21
  152.4 100.9 %copy-start.25 = (bf16[192,768]{0,1:T(8,128)(2,1)S(1)}, bf16[192,768]{0,1:T(8,128)(2,1)}, u32[]{:S(2)}) copy-start(bf16[192,768]{0,1:T(8,128)(2,1)} %all_gather.30) | copy-start | bytes 884740
  257.0 179.4 %all-gather.3.cloned.1.call-start = ((), (), s32[]{:S(2)}) async-start(), calls=%async_computation.12 | async-start | bytes 3932160 | tf_op jit(solution)/shard_map/all_gather | solution.py:135
  263.2 62.4 %copy-start.43 = (f32[192]{0:T(256)}, f32[192]{0:T(256)S(1)}, u32[]{:S(2)}) copy-start(f32[192]{0:T(256)S(1)} %dynamic_slice.39) | copy-start | bytes 2308
  318.7 247.1 %copy-start.12 = (f32[2048,192]{0,1:T(8,128)}, f32[2048,192]{0,1:T(8,128)S(1)}, u32[]{:S(2)}) copy-start(f32[2048,192]{0,1:T(8,128)S(1)} %get-tuple-element.258) | copy-start | bytes 4718596
  324.5 241.2 %copy-start.29 = (f32[2048]{0:T(1024)}, f32[2048]{0:T(1024)S(1)}, u32[]{:S(2)}) copy-start(f32[2048]{0:T(1024)S(1)} %add_rsqrt_fusion) | copy-start | bytes 24580
  325.7 167.4 %reduce-scatter.16.cloned.1.call-start = ((), (), s32[]{:S(2)}) async-start(), calls=%async_computation.13 | async-start | bytes 3932160 | tf_op jit(solution)/shard_map/reduce_scatter | solution.py:141
  325.8 4.7 copy-start.41
  325.8 5.5 copy-start.33
  436.4 3.9 copy-start.20
  436.4 3.9 copy-start.48
  440.4 1.9 copy-start.15
  440.4 2.1 copy-start.28
  453.7 100.1 %reduce-scatter.18.cloned.1.call-start = ((), (), s32[]{:S(2)}) async-start(), calls=%async_computation.14 | async-start | bytes 7864320 | tf_op jit(solution)/shard_map/reduce_scatter | solution.py:167
  453.8 3.8 copy-start.16
  462.2 91.6 %copy-start.42 = (f32[2048]{0:T(1024)S(1)}, f32[2048]{0:T(1024)}, u32[]{:S(2)}) copy-start(f32[2048]{0:T(1024)} %get-tuple-element.255) | copy-start | bytes 24580
  462.2 91.6 %copy-start.44 = (f32[192]{0:T(256)S(1)}, f32[192]{0:T(256)}, u32[]{:S(2)}) copy-start(f32[192]{0:T(256)} %copy-done.43) | copy-start | bytes 2308
  462.2 137.0 %all-gather.5.cloned.1.call-start = ((), (), s32[]{:S(2)}) async-start(), calls=%async_computation.15 | async-start | bytes 3932160 | tf_op jit(solution)/shard_map/all_gather | solution.py:180
  558.5 40.7 %copy-start.18 = (bf16[4,24,8,512]{3,2,0,1:T(8,128)(2,1)S(1)}, bf16[4,24,8,512]{3,2,0,1:T(8,128)(2,1)}, u32[]{:S(2)}) copy-start(bf16[4,24,8,512]{3,2,0,1:T(8,128)(2,1)} %copy-done.17) | copy-start | bytes 2359300
  569.3 211.5 %reduce-scatter.34.cloned.1.call-start = ((), (), s32[]{:S(2)}) async-start(), calls=%async_computation.23 | async-start | bytes 884736
  603.0 4.6 copy-start.37
  603.0 4.6 copy-start.39
  603.0 202.2 %reduce-scatter.20.cloned.1.call-start = ((), (), s32[]{:S(2)}) async-start(), calls=%async_computation.16 | async-start | bytes 7864320 | tf_op jit(solution)/shard_map/reduce_scatter | solution.py:230
  607.8 6.9 copy-start.2
  612.8 1.9 copy-start.1
  630.2 5.2 copy-start
  635.4 1.9 copy-start.5
  635.4 2.3 copy-start.8
  637.8 2.5 copy-start.3
  640.3 6.9 copy-start.2
  645.4 1.9 copy-start.1
  662.8 5.1 copy-start
  667.9 1.9 copy-start.5
  667.9 2.3 copy-start.8
  670.3 2.5 copy-start.3
  672.8 6.9 copy-start.2
  677.9 1.9 copy-start.1
  695.3 5.1 copy-start
  700.4 1.9 copy-start.5
  700.4 2.3 copy-start.8
  702.8 2.5 copy-start.3
  705.3 6.9 copy-start.2
  727.7 5.1 copy-start
  732.9 1.9 copy-start.5
  732.9 2.3 copy-start.8
  735.2 2.5 copy-start.3
  739.2 2.3 copy-start.19
  739.2 2.3 copy-start.10
  739.2 2.3 copy-start.23
  746.6 128.3 %reduce-scatter.28.cloned.1.call-start = ((), (), s32[]{:S(2)}) async-start(), calls=%async_computation.20 | async-start | bytes 1769472 | tf_op jit(solution)/shard_map/reduce_scatter | solution.py:249
  752.3 190.4 %reduce-scatter.30.cloned.1.call-start = ((), (), s32[]{:S(2)}) async-start(), calls=%async_computation.21 | async-start | bytes 1769472 | tf_op jit(solution)/shard_map/reduce_scatter | solution.py:250
  758.2 252.4 %reduce-scatter.32.cloned.1.call-start = ((), (), s32[]{:S(2)}) async-start(), calls=%async_computation.22 | async-start | bytes 1769472 | tf_op jit(solution)/shard_map/reduce_scatter | solution.py:251
  764.2 311.8 %reduce-scatter.22.cloned.1.call-start = ((), (), s32[]{:S(2)}) async-start(), calls=%async_computation.17 | async-start | bytes 884736 | tf_op jit(solution)/shard_map/reduce_scatter | solution.py:245
  768.3 5.8 copy-start.47
  768.3 373.3 %reduce-scatter.26.cloned.1.call-start = ((), (), s32[]{:S(2)}) async-start(), calls=%async_computation.19 | async-start | bytes 884736 | tf_op jit(solution)/shard_map/reduce_scatter | solution.py:247
  772.4 434.5 %reduce-scatter.24.cloned.1.call-start = ((), (), s32[]{:S(2)}) async-start(), calls=%async_computation.18 | async-start | bytes 884736 | tf_op jit(solution)/shard_map/reduce_scatter | solution.py:246
  776.9 28.3 %copy-start.32 = (f32[2048]{0:T(1024)S(1)}, f32[2048]{0:T(1024)}, u32[]{:S(2)}) copy-start(f32[2048]{0:T(1024)} %copy-done.31) | copy-start | bytes 24580
  780.7 75.7 %copy-start.13 = (f32[2048,192]{0,1:T(8,128)S(1)}, f32[2048,192]{0,1:T(8,128)}, u32[]{:S(2)}) copy-start(f32[2048,192]{0,1:T(8,128)} %copy-done.12) | copy-start | bytes 4718596
  780.7 75.7 %copy-start.14 = (f32[2048,192]{0,1:T(8,128)S(1)}, f32[2048,192]{0,1:T(8,128)}, u32[]{:S(2)}) copy-start(f32[2048,192]{0,1:T(8,128)} %reduce-scatter.18.cloned.1.call-done) | copy-start | bytes 4718596
  780.7 75.7 %copy-start.30 = (f32[2048]{0:T(1024)S(1)}, f32[2048]{0:T(1024)}, u32[]{:S(2)}) copy-start(f32[2048]{0:T(1024)} %copy-done.29) | copy-start | bytes 24580
  780.7 75.7 %copy-start.35 = (f32[2048]{0:T(1024)S(1)}, f32[2048]{0:T(1024)}, u32[]{:S(2)}) copy-start(f32[2048]{0:T(1024)} %copy-done.34) | copy-start | bytes 24580
  780.8 75.7 %copy-start.45 = (f32[192]{0:T(256)S(1)}, f32[192]{0:T(256)}, u32[]{:S(2)}) copy-start(f32[192]{0:T(256)} %copy-done.43) | copy-start | bytes 2308
  (26 other events, 35.0 us)
Sparse Core Ops, SparseCore 0:
  257.1 59.3 reduce-scatter.13
  325.8 29.6 all-gather.2
  453.8 39.1 reduce-scatter.15
  495.4 58.3 reduce-scatter.17
  569.5 29.6 all-gather.4
  603.1 62.5 reduce-scatter.33
  746.8 58.4 reduce-scatter.19
  809.6 65.2 reduce-scatter.27
  878.9 63.7 reduce-scatter.29
  946.9 63.6 reduce-scatter.31
  1014.5 61.3 reduce-scatter.21
  1080.1 61.4 reduce-scatter.25
  1145.4 61.4 reduce-scatter.23
where the time goes:
time: 1220 us; the launch traced here: 1210 us
  waiting for transfers between devices  544 us (45%)
  blocking collectives  294 us (24%)
  matrix products  200 us (16%)
  other arithmetic  101 us (8%)
  local copies, waits for them, and re-layouts  53.2 us (4%)
  between operations  15.2 us (1%)
    reduce_scatter x1, waiting for transfers between devices, body(): lax.psum_scatter(grad_w_down, 'wide', scatter_dimension=1, tiled=True)  68 us
    reduce_scatter x1, waiting for transfers between devices, body(): lax.psum_scatter(grad_w_up, 'wide', scatter_dimension=0, tiled=True)  67.8 us
    reduce_scatter x1, waiting for transfers between devices, body(): lax.psum_scatter(grad_w_value, 'wide', scatter_dimension=0, tiled=True)  65.6 us
    reduce_scatter x1, waiting for transfers between devices, body(): lax.psum_scatter(grad_w_key, 'wide', scatter_dimension=0, tiled=True)  65.3 us
    reduce_scatter x1, waiting for transfers between devices, body(): lax.psum_scatter(grad_w_query, 'wide', scatter_dimension=0, tiled=True)  65.3 us
    reduce_scatter x1, waiting for transfers between devices, body(): lax.psum_scatter(contract_cols(grad_gate, full_gate) + contract_cols(grad...  60.8 us
    reduce_scatter x1, waiting for transfers between devices, body(): lax.psum_scatter(plain_dot(heads_out, full_out), 'narrow', scatter_dimens...  53.3 us
    psum x1, blocking collectives, body(): lax.psum((placed_in, placed_mid, stat_terms), ('wide', 'narrow'))  40.1 us
  transfers between devices with their start and end apart: 13, of which 11 were waited for; matrix products, arithmetic and copies ran while one was open for 16% of the time, Pallas kernels for 0%

commit v1 on v0

v1 whole, which is shorter than its diff:
```python
import functools

import jax
import jax.numpy as jnp
from jax import lax
from jax.experimental import pallas as pl
from jax.experimental.pallas import tpu as pltpu
from jax.sharding import PartitionSpec as P

f32 = jnp.float32
bf16 = jnp.bfloat16
HEAD_DIM = 64
UNIT = 512
WINDOW = 2048
LANES = 128
epsilon = 1e-06
BIG = 1e30
GELU_C = 0.7978845608028654
GELU_A = 0.044715
VMEM_LIMIT = 56 << 20

NT = (((1,), (1,)), ((), ()))
NN = (((1,), (0,)), ((), ()))


def mm(a, b, dims=NN):
    return lax.dot_general(a, b, dims, preferred_element_type=f32)


def split3(v):
    high = v.astype(bf16)
    rest = v - high.astype(f32)
    middle = rest.astype(bf16)
    low = (rest - middle.astype(f32)).astype(bf16)
    return high.astype(f32), middle.astype(f32), low.astype(f32)


def lane_halves():
    lane = lax.broadcasted_iota(jnp.int32, (1, LANES), 1)
    first = (lane < HEAD_DIM).astype(f32)
    return lane, first.astype(bf16), (1.0 - first).astype(bf16)


def load_blocks(table, sources, target, wide_index, rows, sem):
    copies = []
    for k, (src, lead, half, offset) in enumerate(table):
        start = pl.multiple_of((wide_index ^ offset) * rows, 8 if rows % 16 else 16)
        copies.append(
            pltpu.make_async_copy(
                sources[src].at[lead], target.at[half, pl.ds(start, rows), :], sem.at[k]
            )
        )
    for copy in copies:
        copy.start()
    for copy in copies:
        copy.wait()


def store_blocks(table, acc, targets, wide_index, rows):
    for src, lead, half, offset in table:
        start = pl.multiple_of((wide_index ^ offset) * rows, 8)
        targets[src][lead] = acc[half, pl.ds(start, rows), :].astype(bf16)


def lane_join(buf, first, width):
    return jnp.concatenate(
        [buf[0, :, first : first + width], buf[1, :, first : first + width]], axis=1
    )


def proj_kernel(table, n_src, rows, share, s_ref, x_ref, gain_ref, *refs):
    sources = refs[:n_src]
    q_ref, k_ref, v_ref, buf, wq, wk, wv, sem = refs[n_src:]
    i = pl.program_id(0)

    @pl.when(i == 0)
    def _():
        load_blocks(table, sources, buf, s_ref[1], rows, sem)
        wq[...] = lane_join(buf, 0, share)
        wk[...] = lane_join(buf, share, share)
        wv[...] = lane_join(buf, 2 * share, share)

    x = x_ref[...].astype(f32)
    scale = lax.rsqrt(jnp.mean(x * x, axis=1, keepdims=True) + epsilon)
    normed = (x * scale * gain_ref[...]).astype(bf16)
    k_ref[...] = mm(normed, wk[...]).astype(bf16)
    v_ref[...] = mm(normed, wv[...]).astype(bf16)
    half = pl.num_programs(0) // 2

    @pl.when(i // half == s_ref[0])
    def _():
        q_ref[...] = mm(normed, wq[...]).astype(bf16)


def own_tile(i, s, half):
    return jnp.clip(i - s[0] * half, 0, half - 1)


def project(scalars, patches, gain, table, sources, rows, share, tile=512):
    n, d = patches.shape
    width = sources[0].shape[-1]
    steps = n // tile
    half = steps // 2
    any_spec = pl.BlockSpec(memory_space=pl.ANY)
    return pl.pallas_call(
        functools.partial(proj_kernel, table, len(sources), rows, share),
        out_shape=(
            jax.ShapeDtypeStruct((n // 2, 2 * share), bf16),
            jax.ShapeDtypeStruct((n, 2 * share), bf16),
            jax.ShapeDtypeStruct((n, 2 * share), bf16),
        ),
        grid_spec=pltpu.PrefetchScalarGridSpec(
            num_scalar_prefetch=1,
            grid=(steps,),
            in_specs=[
                pl.BlockSpec((tile, d), lambda i, s: (i, 0)),
                pl.BlockSpec((1, d), lambda i, s: (0, 0)),
            ]
            + [any_spec] * len(sources),
            out_specs=[
                pl.BlockSpec((tile, 2 * share), lambda i, s: (own_tile(i, s, half), 0)),
                pl.BlockSpec((tile, 2 * share), lambda i, s: (i, 0)),
                pl.BlockSpec((tile, 2 * share), lambda i, s: (i, 0)),
            ],
            scratch_shapes=[pltpu.VMEM((2, d, width), bf16)]
            + [pltpu.VMEM((d, 2 * share), bf16)] * 3
            + [pltpu.SemaphoreType.DMA((len(table),))],
        ),
        compiler_params=pltpu.CompilerParams(vmem_limit_bytes=VMEM_LIMIT),
        cost_estimate=pl.CostEstimate(
            flops=2 * n * d * 5 * share, bytes_accessed=4 * n * d, transcendentals=0
        ),
        name="project",
    )(scalars, patches, gain, *sources)


def attend_kernel(table, n_src, rows, share, chunk, s_ref, q_ref, k_ref, v_ref, qf_ref, kf_ref, *refs):
    sources = refs[:n_src]
    o_ref, qfo_ref, part_ref, k_a, k_b, v_a, v_b, buf, wo, acc, sem = refs[n_src:]
    lane, first, second = lane_halves()
    pair, i = pl.program_id(0), pl.program_id(1)

    @pl.when((pair == 0) & (i == 0))
    def _():
        load_blocks(table, sources, buf, s_ref[1], rows, sem)
        joined = lane_join(buf, 3 * share, share)
        for p in range(wo.shape[0]):
            wo[p] = joined[:, p * LANES : (p + 1) * LANES]

    @pl.when(i == 0)
    def _():
        k, v, kf = k_ref[...], v_ref[...], kf_ref[...]
        k_a[...] = k * first + kf * second
        k_b[...] = k * second + kf * first
        v_a[...] = v * first + (lane == HEAD_DIM).astype(f32).astype(bf16)
        v_b[...] = v * second + (lane == 0).astype(f32).astype(bf16)

    q, qf = q_ref[...], qf_ref[...]
    keys = k_a.shape[0]
    results = []
    for kk, vv, own, other, column in ((k_a, v_a, first, second, HEAD_DIM), (k_b, v_b, second, first, 0)):
        query = q * own + qf * other
        scores = [mm(query, kk[c : c + chunk, :], NT) for c in range(0, keys, chunk)]
        top = functools.reduce(jnp.maximum, [jnp.max(s, axis=1, keepdims=True) for s in scores])
        mixed = None
        for at, s in enumerate(scores):
            part = mm(jnp.exp(s - top).astype(bf16), vv[at * chunk : (at + 1) * chunk, :])
            mixed = part if mixed is None else mixed + part
        total = mixed[:, column : column + 1]
        results.append((mixed / total, top + jnp.log(total)))
    (out_a, lse_a), (out_b, lse_b) = results
    out = jnp.where(lane < HEAD_DIM, out_a, out_b).astype(bf16)
    o_ref[...] = out
    features = qf.astype(f32)
    for at, value in zip((69, 70, 71, 5, 6, 7), split3(lse_a) + split3(lse_b)):
        features = jnp.where(lane == at, value, features)
    qfo_ref[...] = features.astype(bf16)
    part = mm(out, wo[pair], NT)
    tile = q.shape[0]
    here = pl.ds(pl.multiple_of(i * tile, tile), tile)

    @pl.when(pair == 0)
    def _():
        acc[here, :] = part

    @pl.when(pair > 0)
    def _():
        acc[here, :] += part

    part_ref[...] = acc[here, :].astype(bf16)


def attend(scalars, q, k, v, qf, kf, table, sources, rows, share, tile=256, chunk=512):
    n, width = q.shape
    keys = k.shape[0]
    pairs = width // LANES
    steps = n // tile
    d = rows * (len(table) // 2)
    any_spec = pl.BlockSpec(memory_space=pl.ANY)
    row_spec = pl.BlockSpec((tile, LANES), lambda p, i, s: (i, p))
    key_spec = pl.BlockSpec((keys, LANES), lambda p, i, s: (0, p))
    return pl.pallas_call(
        functools.partial(attend_kernel, table, len(sources), rows, share, chunk),
        out_shape=(
            jax.ShapeDtypeStruct((n, width), bf16),
            jax.ShapeDtypeStruct((n, width), bf16),
            jax.ShapeDtypeStruct((n, d), bf16),
        ),
        grid_spec=pltpu.PrefetchScalarGridSpec(
            num_scalar_prefetch=1,
            grid=(pairs, steps),
            in_specs=[
                row_spec,
                key_spec,
                key_spec,
                pl.BlockSpec((tile, LANES), lambda p, i, s: (s[0] * steps + i, 0)),
                pl.BlockSpec((keys, LANES), lambda p, i, s: (0, 0)),
            ]
            + [any_spec] * len(sources),
            out_specs=[
                row_spec,
                row_spec,
                pl.BlockSpec((tile, d), lambda p, i, s: (jnp.where(p == pairs - 1, i, 0), 0)),
            ],
            scratch_shapes=[pltpu.VMEM((keys, LANES), bf16)] * 4
            + [
                pltpu.VMEM((2, d, sources[0].shape[-1]), bf16),
                pltpu.VMEM((pairs, d, LANES), bf16),
                pltpu.VMEM((n, d), f32),
                pltpu.SemaphoreType.DMA((len(table),)),
            ],
        ),
        compiler_params=pltpu.CompilerParams(vmem_limit_bytes=VMEM_LIMIT),
        cost_estimate=pl.CostEstimate(
            flops=4 * n * keys * width * 4, bytes_accessed=8 * n * d, transcendentals=n * keys
        ),
        name="attend",
    )(scalars, q, k, v, qf, kf, *sources)


def mid_norm(x_ref, a_ref, b_ref):
    attn = a_ref[...].astype(f32) + b_ref[...].astype(f32)
    middle = x_ref[...].astype(f32) + attn
    scale = lax.rsqrt(jnp.mean(middle * middle, axis=1, keepdims=True) + epsilon)
    return attn, middle, scale


def feed_kernel(
    table, n_src, rows, out_table, n_out, ff, s_ref, x_ref, a_ref, b_ref, cot_ref, kf_ref, gain_ref, *refs
):
    sources = refs[:n_src]
    mlp_ref, mid_ref, gnm_ref, stat_ref = refs[n_src : n_src + 4]
    targets = refs[n_src + 4 : n_src + 4 + n_out]
    buf, acc, stat, sem = refs[n_src + 4 + n_out :]
    i = pl.program_id(0)
    d = x_ref.shape[1]
    quarter = d // 4

    @pl.when(i == 0)
    def _():
        load_blocks(table, sources, buf, s_ref[1], rows, sem)
        acc[...] = jnp.zeros_like(acc)
        stat[...] = jnp.zeros_like(stat)

    attn, middle, scale = mid_norm(x_ref, a_ref, b_ref)
    live = kf_ref[:, 4:5].astype(f32) >= 0.0
    stat[...] += jnp.sum(jnp.where(live, attn * attn, 0.0), axis=0, keepdims=True)
    normed = (middle * scale * gain_ref[...]).astype(bf16)
    grad = jnp.where(live, cot_ref[...].astype(f32), 0.0).astype(bf16)
    normed_t = normed.T
    grad_t = grad.T
    mid_t = middle.T
    back = None
    hiddens = []
    for half in range(2):
        w_gate = buf[half, :, 0:ff]
        w_up = buf[half, :, ff : 2 * ff]
        w_down = buf[half, :, 2 * ff : 3 * ff]
        gate = mm(normed, w_gate)
        up = mm(normed, w_up)
        back_hidden = mm(grad, w_down)
        square = gate * gate
        angle = jnp.tanh(GELU_C * gate * (1.0 + GELU_A * square))
        cdf = 0.5 * (1.0 + angle)
        act = gate * cdf
        slope = cdf + 0.5 * gate * (1.0 - angle * angle) * (GELU_C * (1.0 + 3.0 * GELU_A * square))
        hidden = (act * up).astype(bf16)
        grad_gate = (back_hidden * up * slope).astype(bf16)
        grad_up = (back_hidden * act).astype(bf16)
        acc[half, :, 0:ff] += mm(normed_t, grad_gate)
        acc[half, :, ff : 2 * ff] += mm(normed_t, grad_up)
        acc[half, :, 2 * ff : 3 * ff] += mm(grad_t, hidden)
        part = mm(grad_gate, w_gate, NT) + mm(grad_up, w_up, NT)
        back = part if back is None else back + part
        hiddens.append(hidden)
    gnm_ref[...] = back.astype(bf16)
    here = s_ref[2]
    for at, offset in enumerate((0, 2, 1, 3)):
        start = pl.ds(pl.multiple_of((here ^ offset) * quarter, 16), quarter)
        out = mm(buf[0, start, 2 * ff : 3 * ff], hiddens[0], NT) + mm(
            buf[1, start, 2 * ff : 3 * ff], hiddens[1], NT
        )
        mlp_ref[at * quarter : (at + 1) * quarter, :] = out.astype(bf16)
    mid_ref[...] = mid_t

    @pl.when(i == pl.num_programs(0) - 1)
    def _():
        stat_ref[...] = stat[...]
        store_blocks(out_table, acc, targets, s_ref[1], rows)


def feed_forward(scalars, patches, a, b, cot, kf, gain, table, sources, rows, out_table, out_leads, tile=256):
    n, d = a.shape
    width = sources[0].shape[-1]
    ff = width // 3
    steps = n // tile
    any_spec = pl.BlockSpec(memory_space=pl.ANY)
    own_spec = pl.BlockSpec((tile, d), lambda i, s: (s[0] * steps + i, 0))
    row_spec = pl.BlockSpec((tile, d), lambda i, s: (i, 0))
    return pl.pallas_call(
        functools.partial(feed_kernel, table, len(sources), rows, out_table, len(out_leads), ff),
        out_shape=(
            jax.ShapeDtypeStruct((d, n), bf16),
            jax.ShapeDtypeStruct((d, n), f32),
            jax.ShapeDtypeStruct((n, d), bf16),
            jax.ShapeDtypeStruct((1, d), f32),
        )
        + tuple(jax.ShapeDtypeStruct((lead, rows, width), bf16) for lead in out_leads),
        grid_spec=pltpu.PrefetchScalarGridSpec(
            num_scalar_prefetch=1,
            grid=(steps,),
            in_specs=[
                own_spec,
                row_spec,
                row_spec,
                own_spec,
                pl.BlockSpec((tile, LANES), lambda i, s: (s[0] * steps + i, 0)),
                pl.BlockSpec((1, d), lambda i, s: (0, 0)),
            ]
            + [any_spec] * len(sources),
            out_specs=[
                pl.BlockSpec((d, tile), lambda i, s: (0, i)),
                pl.BlockSpec((d, tile), lambda i, s: (0, i)),
                row_spec,
                pl.BlockSpec((1, d), lambda i, s: (0, 0)),
            ]
            + [
                pl.BlockSpec((lead, rows, width), lambda i, s: (0, 0, 0), pipeline_mode=pl.Buffered(1))
                for lead in out_leads
            ],
            scratch_shapes=[
                pltpu.VMEM((2, d, width), bf16),
                pltpu.VMEM((2, d, width), f32),
                pltpu.VMEM((1, d), f32),
                pltpu.SemaphoreType.DMA((len(table),)),
            ],
        ),
        compiler_params=pltpu.CompilerParams(vmem_limit_bytes=VMEM_LIMIT),
        cost_estimate=pl.CostEstimate(
            flops=2 * n * d * width * 6, bytes_accessed=10 * n * d, transcendentals=n * ff
        ),
        name="feed_forward",
    )(scalars, patches, a, b, cot, kf, gain, *sources)


def mid_kernel(
    table, n_src, rows, share, s_ref, x_ref, a_ref, b_ref, g_ref, h_ref, cot_ref, kf_ref, gain_ref, o_ref, *refs
):
    sources = refs[:n_src]
    gm_ref, do_ref, dwo_ref, gain_out, buf, wo, acc, total, sem = refs[n_src:]
    i = pl.program_id(0)

    @pl.when(i == 0)
    def _():
        load_blocks(table, sources, buf, s_ref[1], rows, sem)
        wo[...] = lane_join(buf, 3 * share, share)
        acc[...] = jnp.zeros_like(acc)
        total[...] = jnp.zeros_like(total)

    _, middle, scale = mid_norm(x_ref, a_ref, b_ref)
    hat = middle * scale
    back = g_ref[...].astype(f32) + h_ref[...].astype(f32)
    live = kf_ref[:, 4:5].astype(f32) >= 0.0
    cot = jnp.where(live, cot_ref[...].astype(f32), 0.0)
    total[...] += jnp.sum(back * hat, axis=0, keepdims=True)
    scaled = back * gain_ref[...]
    mean = jnp.mean(scaled * hat, axis=1, keepdims=True)
    grad_mid = cot + scale * (scaled - hat * mean)
    gm_ref[...] = grad_mid
    grad = grad_mid.astype(bf16)
    do_ref[...] = mm(grad, wo[...]).astype(bf16)
    acc[...] += mm(grad.T, o_ref[...])

    @pl.when(i == pl.num_programs(0) - 1)
    def _():
        gain_out[...] = total[...]
        dwo_ref[...] = acc[...]


def mid_backward(scalars, patches, a, b, g, h, cot, kf, gain, o, table, sources, rows, share, tile=256):
    n, d = a.shape
    steps = n // tile
    any_spec = pl.BlockSpec(memory_space=pl.ANY)
    own_spec = pl.BlockSpec((tile, d), lambda i, s: (s[0] * steps + i, 0))
    row_spec = pl.BlockSpec((tile, d), lambda i, s: (i, 0))
    head_spec = pl.BlockSpec((tile, 2 * share), lambda i, s: (i, 0))
    one_spec = pl.BlockSpec((1, d), lambda i, s: (0, 0))
    return pl.pallas_call(
        functools.partial(mid_kernel, table, len(sources), rows, share),
        out_shape=(
            jax.ShapeDtypeStruct((n, d), f32),
            jax.ShapeDtypeStruct((n, 2 * share), bf16),
            jax.ShapeDtypeStruct((d, 2 * share), f32),
            jax.ShapeDtypeStruct((1, d), f32),
        ),
        grid_spec=pltpu.PrefetchScalarGridSpec(
            num_scalar_prefetch=1,
            grid=(steps,),
            in_specs=[own_spec, row_spec, row_spec, row_spec, row_spec, own_spec]
            + [pl.BlockSpec((tile, LANES), lambda i, s: (s[0] * steps + i, 0)), one_spec, head_spec]
            + [any_spec] * len(sources),
            out_specs=[
                row_spec,
                head_spec,
                pl.BlockSpec((d, 2 * share), lambda i, s: (0, 0)),
                one_spec,
            ],
            scratch_shapes=[
                pltpu.VMEM((2, d, sources[0].shape[-1]), bf16),
                pltpu.VMEM((d, 2 * share), bf16),
                pltpu.VMEM((d, 2 * share), f32),
                pltpu.VMEM((1, d), f32),
                pltpu.SemaphoreType.DMA((len(table),)),
            ],
        ),
        compiler_params=pltpu.CompilerParams(vmem_limit_bytes=VMEM_LIMIT),
        cost_estimate=pl.CostEstimate(
            flops=8 * n * d * share, bytes_accessed=16 * n * d, transcendentals=0
        ),
        name="mid_backward",
    )(scalars, patches, a, b, g, h, cot, kf, gain, o, *sources)


def attend_back_kernel(
    chunk, q_ref, k_ref, v_ref, qf_ref, kf_ref, o_ref, do_ref, dq_ref, dk_ref, dv_ref, k_a, k_b, v_a, v_b, k_t, dk_acc, dv_acc
):
    lane, first, second = lane_halves()
    i = pl.program_id(1)

    @pl.when(i == 0)
    def _():
        k, v, kf = k_ref[...], v_ref[...], kf_ref[...]
        k_a[...] = k * first + kf * second
        k_b[...] = k * second + kf * first
        v_a[...] = v * first - ((lane >= 64) & (lane < 67)).astype(f32).astype(bf16)
        v_b[...] = v * second - (lane < 3).astype(f32).astype(bf16)
        k_t[...] = k.T
        dk_acc[...] = jnp.zeros_like(dk_acc)
        dv_acc[...] = jnp.zeros_like(dv_acc)

    q, qf, do = q_ref[...], qf_ref[...], do_ref[...]
    product = do.astype(f32) * o_ref[...].astype(f32)
    in_first = lane < HEAD_DIM
    sum_a = jnp.sum(jnp.where(in_first, product, 0.0), axis=1, keepdims=True)
    sum_b = jnp.sum(jnp.where(in_first, 0.0, product), axis=1, keepdims=True)
    features = jnp.zeros(q.shape, f32)
    for at, value in zip((64, 65, 66, 0, 1, 2), split3(sum_a) + split3(sum_b)):
        features = jnp.where(lane == at, value, features)
    features = features.astype(bf16)
    q_first, q_second, do_first, do_second = q * first, q * second, do * first, do * second
    queries = (q_first + qf * second, q_second + qf * first)
    grads = (do_first + features * second, do_second + features * first)
    q_both = jnp.concatenate([q_first, q_second], axis=0)
    do_both = jnp.concatenate([do_first, do_second], axis=0)
    keys = k_a.shape[0]
    dq = [None, None]
    for c in range(0, keys, chunk):
        probs, backs = [], []
        for head, (kk, vv) in enumerate(((k_a, v_a), (k_b, v_b))):
            p = jnp.exp(mm(kk[c : c + chunk, :], queries[head], NT))
            back = (p * mm(vv[c : c + chunk, :], grads[head], NT)).astype(bf16)
            probs.append(p.astype(bf16))
            backs.append(back)
            part = mm(k_t[head * HEAD_DIM : (head + 1) * HEAD_DIM, c : c + chunk], back)
            dq[head] = part if dq[head] is None else dq[head] + part
        dv_acc[c : c + chunk, :] += mm(jnp.concatenate(probs, axis=1), do_both)
        dk_acc[c : c + chunk, :] += mm(jnp.concatenate(backs, axis=1), q_both)
    dq_ref[...] = jnp.concatenate(dq, axis=0).T.astype(bf16)

    @pl.when(i == pl.num_programs(1) - 1)
    def _():
        dk_ref[...] = dk_acc[...].astype(bf16)
        dv_ref[...] = dv_acc[...].astype(bf16)


def attend_back(q, k, v, qf, kf, o, do, tile=512, chunk=512):
    n, width = q.shape
    keys = k.shape[0]
    row_spec = pl.BlockSpec((tile, LANES), lambda p, i: (i, p))
    key_spec = pl.BlockSpec((keys, LANES), lambda p, i: (0, p))
    return pl.pallas_call(
        functools.partial(attend_back_kernel, chunk),
        out_shape=(
            jax.ShapeDtypeStruct((n, width), bf16),
            jax.ShapeDtypeStruct((keys, width), bf16),
            jax.ShapeDtypeStruct((keys, width), bf16),
        ),
        grid=(width // LANES, n // tile),
        in_specs=[
            row_spec,
            key_spec,
            key_spec,
            row_spec,
            pl.BlockSpec((keys, LANES), lambda p, i: (0, 0)),
            row_spec,
            row_spec,
        ],
        out_specs=[row_spec, key_spec, key_spec],
        scratch_shapes=[pltpu.VMEM((keys, LANES), bf16)] * 4
        + [pltpu.VMEM((LANES, keys), bf16)]
        + [pltpu.VMEM((keys, LANES), f32)] * 2,
        compiler_params=pltpu.CompilerParams(vmem_limit_bytes=VMEM_LIMIT),
        cost_estimate=pl.CostEstimate(
            flops=10 * n * keys * width * 4, bytes_accessed=8 * keys * width, transcendentals=n * keys
        ),
        name="attend_back",
    )(q, k, v, qf, kf, o, do)


def last_kernel(
    table, n_src, rows, out_table, n_out, share, s_ref, x_ref, gain_ref, dq_ref, dk_ref, dv_ref, gm_ref, dwo_ref, *refs
):
    sources = refs[:n_src]
    gp_ref, gain_out = refs[n_src : n_src + 2]
    targets = refs[n_src + 2 : n_src + 2 + n_out]
    buf, wq, wk, wv, dwq, dwk, dwv, pack, total, sem = refs[n_src + 2 + n_out :]
    i = pl.program_id(0)
    half = pl.num_programs(0) // 2
    d = x_ref.shape[1]
    quarter = d // 4

    @pl.when(i == 0)
    def _():
        load_blocks(table, sources, buf, s_ref[1], rows, sem)
        wq[...] = lane_join(buf, 0, share)
        wk[...] = lane_join(buf, share, share)
        wv[...] = lane_join(buf, 2 * share, share)
        for ref in (dwq, dwk, dwv, total):
            ref[...] = jnp.zeros_like(ref)

    mine = i // half == s_ref[0]
    x = x_ref[...].astype(f32)
    scale = lax.rsqrt(jnp.mean(x * x, axis=1, keepdims=True) + epsilon)
    hat = x * scale
    normed_t = (hat * gain_ref[...]).astype(bf16).T
    dk, dv = dk_ref[...], dv_ref[...]
    dq = jnp.where(mine, dq_ref[...].astype(f32), 0.0).astype(bf16)
    dwk[...] += mm(normed_t, dk)
    dwv[...] += mm(normed_t, dv)
    dwq[...] += mm(normed_t, dq)
    back = mm(dk, wk[...], NT) + mm(dv, wv[...], NT) + mm(dq, wq[...], NT)
    total[...] += jnp.sum(back * hat, axis=0, keepdims=True)
    scaled = back * gain_ref[...]
    mean = jnp.mean(scaled * hat, axis=1, keepdims=True)
    grad = scale * (scaled - hat * mean) + jnp.where(mine, 0.5, 0.0) * gm_ref[...]
    grad_t = grad.T
    here = s_ref[2]
    buf_t = grad_t.astype(bf16)
    for block in range(4):
        at = here ^ block
        slot = jnp.where(at == 0, 0, jnp.where(at == 2, 1, jnp.where(at == 1, 2, 3)))
        gp_ref[pl.ds(pl.multiple_of(slot * quarter, 16), quarter), :] = buf_t[
            block * quarter : (block + 1) * quarter, :
        ]

    @pl.when(i == pl.num_programs(0) - 1)
    def _():
        gain_out[...] = total[...]
        for h in range(2):
            lanes = slice(h * share, (h + 1) * share)
            for at, ref in enumerate((dwq, dwk, dwv, dwo_ref)):
                pack[h, :, at * share : (at + 1) * share] = ref[:, lanes]
        store_blocks(out_table, pack, targets, s_ref[1], rows)


def last_backward(
    scalars, patches, gain, dq, dk, dv, gm, dwo, table, sources, rows, out_table, out_leads, share, tile=512
):
    n, d = patches.shape
    width = sources[0].shape[-1]
    steps = n // tile
    half = steps // 2
    any_spec = pl.BlockSpec(memory_space=pl.ANY)
    key_spec = pl.BlockSpec((tile, 2 * share), lambda i, s: (i, 0))
    one_spec = pl.BlockSpec((1, d), lambda i, s: (0, 0))
    return pl.pallas_call(
        functools.partial(last_kernel, table, len(sources), rows, out_table, len(out_leads), share),
        out_shape=(
            jax.ShapeDtypeStruct((d, n), bf16),
            jax.ShapeDtypeStruct((1, d), f32),
        )
        + tuple(jax.ShapeDtypeStruct((lead, rows, width), bf16) for lead in out_leads),
        grid_spec=pltpu.PrefetchScalarGridSpec(
            num_scalar_prefetch=1,
            grid=(steps,),
            in_specs=[
                pl.BlockSpec((tile, d), lambda i, s: (i, 0)),
                one_spec,
                pl.BlockSpec((tile, 2 * share), lambda i, s: (own_tile(i, s, half), 0)),
                key_spec,
                key_spec,
                pl.BlockSpec((tile, d), lambda i, s: (own_tile(i, s, half), 0)),
                pl.BlockSpec((d, 2 * share), lambda i, s: (0, 0)),
            ]
            + [any_spec] * len(sources),
            out_specs=[pl.BlockSpec((d, tile), lambda i, s: (0, i)), one_spec]
            + [
                pl.BlockSpec((lead, rows, width), lambda i, s: (0, 0, 0), pipeline_mode=pl.Buffered(1))
                for lead in out_leads
            ],
            scratch_shapes=[pltpu.VMEM((2, d, width), bf16)]
            + [pltpu.VMEM((d, 2 * share), bf16)] * 3
            + [pltpu.VMEM((d, 2 * share), f32)] * 3
            + [
                pltpu.VMEM((2, d, width), f32),
                pltpu.VMEM((1, d), f32),
                pltpu.SemaphoreType.DMA((len(table),)),
            ],
        ),
        compiler_params=pltpu.CompilerParams(vmem_limit_bytes=VMEM_LIMIT),
        cost_estimate=pl.CostEstimate(
            flops=2 * n * d * share * 10, bytes_accessed=10 * n * d, transcendentals=0
        ),
        name="last_backward",
    )(scalars, patches, gain, dq, dk, dv, gm, dwo, *sources)


def swap_core(value):
    return lax.ppermute(value, "narrow", [(i, i ^ 1) for i in range(4)])


def swap_x(value):
    return lax.ppermute(value, "narrow", [(i, i ^ 2) for i in range(4)])


def swap_wide(value, offset):
    n = lax.axis_size("wide")
    return lax.ppermute(value, "wide", [(i, i ^ offset) for i in range(n)])


GATHER_TABLE = (
    [(0, z, 0, 2 * z) for z in range(4)]
    + [(1, z, 0, 2 * z + 1) for z in range(4)]
    + [(2, z, 1, 2 * z) for z in range(4)]
    + [(3, z, 1, 2 * z + 1) for z in range(2)]
    + [(4, z, 1, 2 * z + 5) for z in range(2)]
)
REDUCE_TABLE = GATHER_TABLE
REDUCE_LEADS = (4, 4, 4, 2, 2)
WHOLE_TABLE = [(0, 0, 0, 0), (0, 1, 1, 0)]


def gather_shards(shard):
    if lax.axis_size("wide") != 8:
        full = lax.all_gather(shard, "wide", axis=0, tiled=True)
        return WHOLE_TABLE, [jnp.stack([full, swap_x(full)])], full.shape[0]
    column = jnp.stack([shard] + [swap_wide(shard, 2 * z) for z in (1, 2, 3)])
    from_y = swap_wide(column, 1)
    from_x = swap_x(column)
    corner_x = swap_x(from_y[:2])
    corner_y = swap_wide(from_x[2:], 1)
    return GATHER_TABLE, [column, from_y, from_x, corner_x, corner_y], shard.shape[0]


def reduce_tables():
    if lax.axis_size("wide") != 8:
        return WHOLE_TABLE, (2,)
    return REDUCE_TABLE, REDUCE_LEADS


def total(*terms):
    return functools.reduce(jnp.add, [t.astype(f32) for t in terms])


def reduce_shards(parts):
    if lax.axis_size("wide") != 8:
        both = total(parts[0][0], swap_x(parts[0][1])).astype(bf16)
        return lax.psum_scatter(both, "wide", scatter_dimension=0, tiled=True).astype(f32)
    column, to_y, to_x, corner_x, corner_y = parts
    got_x = swap_x(corner_x)
    got_y = swap_wide(corner_y, 1)
    to_y = jnp.concatenate([total(to_y[:2], got_x).astype(bf16), to_y[2:]])
    to_x = jnp.concatenate([to_x[:2], total(to_x[2:], got_y).astype(bf16)])
    column = total(column, swap_wide(to_y, 1), swap_x(to_x))
    sent = column[1:].astype(bf16)
    return total(column[0], *[swap_wide(sent[z - 1], 2 * z) for z in (1, 2, 3)])


def sum_all(value):
    if lax.axis_size("wide") != 8:
        return lax.psum(value, ("wide", "narrow"))
    value = value + swap_core(value)
    value = value + swap_x(value)
    for offset in (1, 2, 4):
        value = value + swap_wide(value, offset)
    return value


def mask_features(item_slots, valid_counts, rows):
    def spread(values):
        return jnp.repeat(values, rows // values.shape[0], total_repeat_length=rows)

    position = jnp.arange(rows, dtype=jnp.int32)
    start = position // spread(item_slots) * spread(item_slots)
    live = position - start < spread(valid_counts)
    unit = start // UNIT
    lane = jnp.arange(LANES, dtype=jnp.int32)[None, :] % HEAD_DIM
    same = unit[:, None] == lane
    query = jnp.where(lane < 4, jnp.where(same, 0.0, 1.0), jnp.where(lane == 4, 1.0, 0.0))
    key = jnp.where(lane < 4, jnp.where(same, -BIG, 0.0), 0.0)
    key = jnp.where(lane == 4, jnp.where(live[:, None], 0.0, -BIG), key)
    key = jnp.where((lane >= 5) & (lane < 8), -1.0, key)
    return query.astype(bf16), key.astype(bf16), live


def body(
    patches,
    norm_gain_attn,
    norm_gain_mlp,
    w_query,
    w_key,
    w_value,
    w_out,
    w_gate,
    w_up,
    w_down,
    cotangent,
    item_slots,
    valid_counts,
):
    rows, d = patches.shape
    share = w_query.shape[1]
    ff = w_gate.shape[1]
    half_rows = rows // 2
    quarter = d // 4
    narrow = lax.axis_index("narrow")
    wide = lax.axis_index("wide")
    x_half = narrow // 2
    exact_blocks = lax.axis_size("wide") == 8
    scalars = jnp.stack([x_half, wide if exact_blocks else 0 * wide, narrow]).astype(jnp.int32)

    head_table, head_parts, block_rows = gather_shards(
        jnp.concatenate([w_query, w_key, w_value, w_out.T], axis=1)
    )
    ff_table, ff_parts, _ = gather_shards(jnp.concatenate([w_gate, w_up, w_down.T], axis=1))
    out_table, out_leads = reduce_tables()

    gain_in = norm_gain_attn[None, :]
    gain_mid = norm_gain_mlp[None, :]
    query_mask, key_mask, live = mask_features(item_slots, valid_counts, rows)

    q, k, v = project(scalars, patches, gain_in, head_table, head_parts, block_rows, share)
    heads, query_aux, attn_part = attend(
        scalars, q, k, v, query_mask, key_mask, head_table, head_parts, block_rows, share
    )
    attn_other = swap_core(attn_part)
    mlp_part, mid_t, back_part, attn_square, *ff_grads = feed_forward(
        scalars, patches, attn_part, attn_other, cotangent, key_mask, gain_mid,
        ff_table, ff_parts, block_rows, out_table, out_leads,
    )
    back_other = swap_core(back_part)
    grad_mid, grad_heads, dwo, gain_mid_sum = mid_backward(
        scalars, patches, attn_part, attn_other, back_part, back_other, cotangent, key_mask,
        gain_mid, heads, head_table, head_parts, block_rows, share,
    )
    dq, dk, dv = attend_back(q, k, v, query_aux, key_mask, heads, grad_heads)
    grad_t, gain_in_sum, *head_grads = last_backward(
        scalars, patches, gain_in, dq, dk, dv, grad_mid, dwo,
        head_table, head_parts, block_rows, out_table, out_leads, share,
    )

    mlp_keep = total(mlp_part[: 2 * quarter], swap_core(mlp_part[2 * quarter :]))
    mid_keep = jnp.concatenate(
        [
            lax.dynamic_slice_in_dim(mid_t, narrow * quarter, quarter, 0),
            lax.dynamic_slice_in_dim(mid_t, (narrow ^ 2) * quarter, quarter, 0),
        ]
    )
    live_own = lax.dynamic_slice_in_dim(live, x_half * half_rows, half_rows)
    layer = jnp.where(live_own[None, :], mid_keep + mlp_keep, 0.0)
    layer16 = layer.astype(bf16)
    mlp_square = jnp.sum(jnp.where(live_own[None, :], mlp_keep * mlp_keep, 0.0))
    layer_square = jnp.sum(layer * layer)
    mine, theirs = layer16[:quarter], swap_x(layer16[quarter:])
    output = jnp.where(
        x_half == 0,
        jnp.concatenate([mine, theirs], axis=1),
        jnp.concatenate([theirs, mine], axis=1),
    ).T

    grad_keep = total(grad_t[: 2 * quarter], swap_core(grad_t[2 * quarter :]))
    grad_patches = total(grad_keep[:quarter], swap_x(grad_keep[quarter:].astype(bf16))).T

    head_own = reduce_shards(head_grads)
    ff_own = reduce_shards(ff_grads)

    stats = jnp.stack(
        [
            0.5 * jnp.sum(attn_square),
            mlp_square,
            layer_square,
            0.5 * jnp.sum(live_own.astype(f32)),
        ]
    )
    sums = sum_all(
        jnp.concatenate([gain_in_sum[0], 0.5 * gain_mid_sum[0], jnp.pad(stats, (0, LANES - 4))])
    )
    total_in, total_mid, totals = sums[:d], sums[d : 2 * d], sums[2 * d : 2 * d + 4]
    rms_values = jnp.sqrt(totals[:3] / (totals[3] * d))
    return (
        output,
        grad_patches,
        total_in,
        total_mid,
        head_own[:, :share],
        head_own[:, share : 2 * share],
        head_own[:, 2 * share : 3 * share],
        head_own[:, 3 * share :].T,
        ff_own[:, :ff],
        ff_own[:, ff : 2 * ff],
        ff_own[:, 2 * ff :].T,
        rms_values,
    )


def solution(mesh):
    return jax.shard_map(
        body,
        mesh=mesh,
        in_specs=(
            P("wide", None),
            P(),
            P(),
            P("wide", "narrow"),
            P("wide", "narrow"),
            P("wide", "narrow"),
            P("narrow", "wide"),
            P("wide", "narrow"),
            P("wide", "narrow"),
            P("narrow", "wide"),
            P("wide", None),
            P("wide"),
            P("wide"),
        ),
        out_specs=(
            P("wide", "narrow"),
            P("wide", "narrow"),
            P(),
            P(),
            P("wide", "narrow"),
            P("wide", "narrow"),
            P("wide", "narrow"),
            P("narrow", "wide"),
            P("wide", "narrow"),
            P("wide", "narrow"),
            P("narrow", "wide"),
            P(),
        ),
        check_vma=False,
    )
```

time: 1220 us -> 331 us (0.27)
  waiting for transfers between devices: 544 us -> 84.6 us
  blocking collectives: 294 us -> 0 us
  matrix products: 200 us -> 0 us
  Pallas kernels: 0 us -> 147 us
  other arithmetic: 101 us -> 29.8 us
  starting transfers between devices: 0.54 us -> 43.5 us
  local copies, waits for them, and re-layouts: 53.2 us -> 21 us
    reduce_scatter x10 -> x0, waiting for transfers between devices: 514 us -> none  [the longest x1 68 us: body(): lax.psum_scatter(grad_w_down, 'wide', scatter_dimension=1, tiled=True)]
    all_gather x7 -> x0, blocking collectives: 234 us -> none  [the longest x1 35.1 us: body(): lax.all_gather(w_out, 'wide', axis=1, tiled=True)]
    dot_general x48 -> x0, matrix products: 196 us -> none  [the longest x8 34 us: block_scores(): jnp.einsum('qhe,khe->hqk', query_heads, key_heads, preferred_element_type...]
    pallas_call x0 -> x6, Pallas kernels: none -> 147 us  [the longest x1 42.2 us: attend_back(): pl.pallas_call(functools.partial(attend_back_kernel, chunk), out_shape=(j...]
    ppermute x0 -> x39, waiting for transfers between devices: none -> 84.6 us  [the longest x23 62.9 us: swap_wide(): return lax.ppermute(value, 'wide', [(i, i ^ offset) for i in range(n)])]
    psum x4 -> x0, blocking collectives: 59.4 us -> none  [the longest x1 40.1 us: body(): lax.psum((placed_in, placed_mid, stat_terms), ('wide', 'narrow'))]
    ppermute x0 -> x39, starting transfers between devices: none -> 43.5 us  [the longest x23 30.6 us: swap_wide(): return lax.ppermute(value, 'wide', [(i, i ^ offset) for i in range(n)])]
    reduce_sum x9 -> x3, other arithmetic: 41.6 us -> 3.24 us  [the longest x1 1.35 us: body(): mlp_square = jnp.sum(jnp.where(live_own[None, :], mlp_keep * mlp_keep, 0.0))]
  transfers between devices with their start and end apart: 13 -> 39, of which waited for: 11 -> 18; matrix products, arithmetic and copies ran while one was open for 16% -> 12% of each run, Pallas kernels for 0% -> 36%
where the time goes in v1:
time: 331 us; the launch traced here: 329 us
  Pallas kernels  147 us (44%)
  waiting for transfers between devices  84.6 us (26%)
  starting transfers between devices  43.5 us (13%)
  other arithmetic  29.8 us (9%)
  local copies, waits for them, and re-layouts  21 us (6%)
  between operations  3.31 us (1%)
    ppermute x23, waiting for transfers between devices, swap_wide(): return lax.ppermute(value, 'wide', [(i, i ^ offset) for i in range(n)])  62.9 us
    pallas_call x1, Pallas kernels, attend_back(): pl.pallas_call(functools.partial(attend_back_kernel, chunk), out_shape=(j...  42.2 us
    pallas_call x1, Pallas kernels, attend(): pl.pallas_call(functools.partial(attend_kernel, table, len(sources), rows...  31.9 us
    ppermute x23, starting transfers between devices, swap_wide(): return lax.ppermute(value, 'wide', [(i, i ^ offset) for i in range(n)])  30.6 us
    pallas_call x1, Pallas kernels, feed_forward(): pl.pallas_call(functools.partial(feed_kernel, table, len(sources), rows,...  27.5 us
    pallas_call x1, Pallas kernels, last_backward(): pl.pallas_call(functools.partial(last_kernel, table, len(sources), rows,...  22.8 us
    ppermute x11, waiting for transfers between devices, swap_x(): return lax.ppermute(value, 'narrow', [(i, i ^ 2) for i in range(4)])  20.6 us
    ppermute x11, starting transfers between devices, swap_x(): return lax.ppermute(value, 'narrow', [(i, i ^ 2) for i in range(4)])  12.1 us
  transfers between devices with their start and end apart: 39, of which 18 were waited for; matrix products, arithmetic and copies ran while one was open for 12% of the time, Pallas kernels for 36%

profile of v1, /device:TPU:0, one launch (start us, length us, event | category | flops | bytes accessed | tf_op | source)
XLA Modules:
  0.0 329.4 jit_solution(1201775598926313403)
XLA Ops:
  2.5 4.1 %collective-permute-start.1 = (bf16[96,768]{1,0:T(8,128)(2,1)S(1)}, bf16[96,768]{1,0:T(8,128)(2,1)S(1)}, u32[]{:S(2)}, u32[]{:S(2)}) collective-permute-start(bf16[96,768]{1,0:T(8,128)(2,1)S(1)} %pad_maximum_fusion.7), channel_id=1, source_target_pairs={{0,16},{4,20},{8,24},{12,28},{16,0},{20,4},{24,8},{28,12},{1,17},{... | collective-permute-start | bytes 442376 | tf_op jit(solution)/shard_map/ppermute | solution.py:648
  6.6 1.6 collective-permute-start
  8.2 1.0 fusion.26
  9.2 2.0 collective-permute-start.9
  11.2 2.5 collective-permute-start.8
  13.7 1.4 fusion.32
  15.1 1.4 fusion.31
  16.5 3.4 %add_select_fusion = s32[2048]{0:T(1024)S(1)} fusion(pred[2048]{0:T(1024)(128)(4,1)} %constant.217, pred[2048]{0:T(1024)(128)(4,1)} %constant.218, pred[2048]{0:T(1024)(128)(4,1)} %constant.219, s32[]{:T(128)} %bitcast.3, s32[]{:T(128)} %bitcast.2, s32[]{:T(128)} %bitcast.1, s32[]{:T(128)} %bitcast), kind=kLoop, calls=%fused_computation.50 | loop fusion | flops 57344 | bytes 14352 | tf_op jit(solution)/shard_map/jit(floor_divide)/jit(_where)/select_n | solution.py:716
  19.9 6.0 %broadcast_select_fusion = (bf16[2048]{0:T(1024)(128)(2,1)S(1)}, pred[2048]{0:T(1024)(128)(4,1)S(1)}) fusion(pred[2048]{0:T(1024)(128)(4,1)} %constant.217, pred[2048]{0:T(1024)(128)(4,1)} %constant.218, pred[2048]{0:T(1024)(128)(4,1)} %constant.219, s32[]{:T(128)} %bitcast.7, s32[]{:T(128)} %bitcast.6, s32[]{:T(128)} %bitcast.5, s32[]{:T(128)} %bitcast.4, ...), kind=kLoop, calls=%fused_computation.69 | loop fusion | flops 38912 | bytes 12320 | tf_op jit(solution)/shard_map/jit(_where)/select_n | solution.py:721
  27.1 1.7 collective-permute-start.4
  28.8 1.5 collective-permute-start.3
  30.4 1.5 fusion.7
  31.9 8.9 %collective-permute-done.4.refs_2_ = bf16[4,96,768]{2,1,0:T(8,128)(2,1)S(1)} collective-permute-done((bf16[4,96,768]{2,1,0:T(8,128)(2,1)S(1)}, bf16[4,96,768]{2,1,0:T(8,128)(2,1)S(1)}, u32[]{:S(2)}, u32[]{:S(2)}) %collective-permute-start.4) | collective-permute-done | bytes 589856 | tf_op jit(solution)/shard_map/ppermute | solution.py:643
  40.9 1.6 collective-permute-start.6
  43.0 1.0 collective-permute-start.5
  45.4 1.1 collective-permute-start.12
  46.6 1.7 collective-permute-start.11
  48.3 2.6 collective-permute-done.6.refs_4_
  50.9 2.2 collective-permute-done.5.refs_3_
  53.8 10.8 %project.1 = (bf16[1024,384]{1,0:T(8,128)(2,1)}, bf16[2048,384]{1,0:T(8,128)(2,1)}, bf16[2048,384]{1,0:T(8,128)(2,1)}) custom-call(s32[3]{0:T(128)} %pad_add_fusion.s_ref, bf16[2048,768]{1,0:T(8,128)(2,1)} %x_ref.7, f32[1,768]{1,0:T(1,128)} %broadcast_in_dim.115.gain_ref, bf16[4,96,768]{2,1,0:T(8,128)(2,1)} %copy-done.1, bf16[4,96,768]{2,1,0:T(8,128)(2,1)} %copy-done.7, ...), custom_call_target="tpu_custom_call" | custom-call | flops 3019898880 | bytes 6291456 | tf_op jit(solution)/shard_map/project/pallas_call | solution.py:105
  64.6 31.9 %attend.1 = (bf16[1024,384]{1,0:T(8,128)(2,1)}, bf16[1024,384]{1,0:T(8,128)(2,1)}, bf16[1024,768]{1,0:T(8,128)(2,1)}) custom-call(s32[3]{0:T(128)} %pad_add_fusion.s_ref, bf16[1024,384]{1,0:T(8,128)(2,1)} %get-tuple-element.70.q_ref, bf16[2048,384]{1,0:T(8,128)(2,1)} %get-tuple-element.71.k_ref, bf16[2048,384]{1,0:T(8,128)(2,1)} %get-tuple-element.72.v_ref, ...), custom_call_target="tpu_custom_call" | custom-call | flops 12884901888 | bytes 6291456 | tf_op jit(solution)/shard_map/attend/pallas_call | solution.py:202
  96.7 1.8 collective-permute-start.14
  99.3 13.2 %collective-permute-done.14.refs_4_ = bf16[2,96,1536]{2,1,0:T(8,128)(2,1)S(1)} collective-permute-done((bf16[2,96,1536]{2,1,0:T(8,128)(2,1)S(1)}, bf16[2,96,1536]{2,1,0:T(8,128)(2,1)S(1)}, u32[]{:S(2)}, u32[]{:S(2)}) %collective-permute-start.14) | collective-permute-done | bytes 589856 | tf_op jit(solution)/shard_map/ppermute | solution.py:648
  112.5 1.5 collective-permute-done.13.refs_3_
  114.8 1.2 copy-done.3
  116.1 27.5 %feed_forward.1 = (bf16[768,1024]{1,0:T(8,128)(2,1)}, f32[768,1024]{1,0:T(8,128)}, bf16[1024,768]{1,0:T(8,128)(2,1)}, f32[1,768]{1,0:T(1,128)}, bf16[4,96,1536]{...) custom-call(s32[3]{0:T(128)} %pad_add_fusion.s_ref, ...), custom_call_target="tpu_custom_call" | custom-call | flops 14495514624 | bytes 7864320 | tf_op jit(solution)/shard_map/feed_forward/pallas_call | solution.py:320
  145.3 1.3 reduce_sum.36
  147.2 1.1 slice.188
  148.4 1.2 slice.189
  151.2 1.6 constant_dynamic-slice_fusion.1
  152.9 5.6 %collective-permute-done.34 = bf16[2,96,1536]{2,1,0:T(8,128)(2,1)S(1)} collective-permute-done((bf16[2,96,1536]{2,1,0:T(8,128)(2,1)}, bf16[2,96,1536]{2,1,0:T(8,128)(2,1)S(1)}, u32[]{:S(2)}, u32[]{:S(2)}) %collective-permute-start.34) | collective-permute-done | bytes 589856 | tf_op jit(solution)/shard_map/ppermute | solution.py:648
  158.6 1.1 pad_maximum_fusion.2
  160.3 5.6 %collective-permute-done.32 = bf16[2,96,1536]{2,1,0:T(8,128)(2,1)S(1)} collective-permute-done((bf16[2,96,1536]{2,1,0:T(8,128)(2,1)S(1)}, bf16[2,96,1536]{2,1,0:T(8,128)(2,1)S(1)}, u32[]{:S(2)}, u32[]{:S(2)}) %collective-permute-start.32) | collective-permute-done | bytes 589856 | tf_op jit(solution)/shard_map/ppermute | solution.py:643
  166.1 1.1 pad_maximum_fusion.1
  167.2 1.7 collective-permute-start.33
  168.9 1.3 select_reduce_fusion
  170.6 1.4 select_maximum_fusion
  172.0 1.1 copy-done.5
  173.2 11.8 %mid_backward.1 = (f32[1024,768]{1,0:T(8,128)}, bf16[1024,384]{1,0:T(8,128)(2,1)}, f32[768,384]{1,0:T(8,128)}, f32[1,768]{1,0:T(1,128)}) custom-call(s32[3]{0:T(128)} %pad_add_fusion.s_ref, bf16[2048,768]{1,0:T(8,128)(2,1)} %x_ref.7, bf16[1024,768]{1,0:T(8,128)(2,1)} %get-tuple-element.73.a_ref, bf16[1024,768]{1,0:T(8,128)(2,1)} %copy-done.3, ...), custom_call_target="tpu_custom_call" | custom-call | flops 1207959552 | bytes 12582912 | tf_op jit(solution)/shard_map/mid_backward/pallas_call | solution.py:408
  185.0 42.2 %attend_back.1 = (bf16[1024,384]{1,0:T(8,128)(2,1)}, bf16[2048,384]{1,0:T(8,128)(2,1)}, bf16[2048,384]{1,0:T(8,128)(2,1)}) custom-call(bf16[1024,384]{1,0:T(8,128)(2,1)} %get-tuple-element.70.q_ref, bf16[2048,384]{1,0:T(8,128)(2,1)} %get-tuple-element.71.k_ref, bf16[2048,384]{1,0:T(8,128)(2,1)} %get-tuple-element.72.v_ref, ...), custom_call_target="tpu_custom_call" | custom-call | flops 32212254720 | bytes 6291456 | tf_op jit(solution)/shard_map/attend_back/pallas_call | solution.py:501
  227.1 22.8 %last_backward.1 = (bf16[768,2048]{1,0:T(8,128)(2,1)}, f32[1,768]{1,0:T(1,128)}, bf16[4,96,768]{2,1,0:T(8,128)(2,1)}, bf16[4,96,768]{2,1,0:T(8,128)(2,1)}, bf16[...) custom-call(s32[3]{0:T(128)} %pad_add_fusion.s_ref, bf16[2048,768]{1,0:T(8,128)(2,1)} %x_ref.7, ...), custom_call_target="tpu_custom_call" | custom-call | flops 6039797760 | bytes 15728640 | tf_op jit(solution)/shard_map/last_backward/pallas_call | solution.py:596
  250.9 1.2 collective-permute-done.20
  252.1 1.5 collective-permute-start.21
  253.6 2.1 collective-permute-done.21
  256.7 2.7 collective-permute-done.22
  259.4 3.6 %collective-permute-done.23 = f32[1664]{0:T(1024)S(1)} collective-permute-done((f32[1664]{0:T(1024)S(1)}, f32[1664]{0:T(1024)S(1)}, u32[]{:S(2)}, u32[]{:S(2)}) %collective-permute-start.23) | collective-permute-done | bytes 6688 | tf_op jit(solution)/shard_map/ppermute | solution.py:648
  263.1 2.8 collective-permute-start.24
  265.8 1.2 fusion.8
  267.1 1.2 collective-permute-start.25
  269.1 1.6 slice.170
  272.7 1.7 fusion.27
  274.5 1.5 collective-permute-start.36
  276.0 2.0 collective-permute-start.37
  278.2 1.8 collective-permute-start.28
  280.2 10.1 %collective-permute-done.36 = bf16[96,1536]{1,0:T(8,128)(2,1)S(1)} collective-permute-done((bf16[96,1536]{1,0:T(8,128)(2,1)S(1)}, bf16[96,1536]{1,0:T(8,128)(2,1)S(1)}, u32[]{:S(2)}, u32[]{:S(2)}) %collective-permute-start.36) | collective-permute-done | bytes 294944 | tf_op jit(solution)/shard_map/ppermute | solution.py:648
  290.8 13.3 %collective-permute-done.37 = bf16[96,1536]{1,0:T(8,128)(2,1)S(1)} collective-permute-done((bf16[96,1536]{1,0:T(8,128)(2,1)S(1)}, bf16[96,1536]{1,0:T(8,128)(2,1)S(1)}, u32[]{:S(2)}, u32[]{:S(2)}) %collective-permute-start.37) | collective-permute-done | bytes 294944 | tf_op jit(solution)/shard_map/ppermute | solution.py:648
  304.5 1.6 copy-done
  307.8 1.7 collective-permute-start.19
  309.6 1.2 collective-permute-start.31
  310.8 2.2 collective-permute-start.30
  313.9 3.5 %collective-permute-done.29 = bf16[96,768]{1,0:T(8,128)(2,1)S(1)} collective-permute-done((bf16[96,768]{1,0:T(8,128)(2,1)S(1)}, bf16[96,768]{1,0:T(8,128)(2,1)S(1)}, u32[]{:S(2)}, u32[]{:S(2)}) %collective-permute-start.29) | collective-permute-done | bytes 147488 | tf_op jit(solution)/shard_map/ppermute | solution.py:648
  317.4 1.1 collective-permute-done.31
  318.4 6.7 %collective-permute-done.30 = bf16[96,768]{1,0:T(8,128)(2,1)S(1)} collective-permute-done((bf16[96,768]{1,0:T(8,128)(2,1)S(1)}, bf16[96,768]{1,0:T(8,128)(2,1)S(1)}, u32[]{:S(2)}, u32[]{:S(2)}) %collective-permute-start.30) | collective-permute-done | bytes 147488 | tf_op jit(solution)/shard_map/ppermute | solution.py:648
  326.9 2.4 fusion
  (140 shorter events, 21.0 us)
Async XLA Ops:
  2.5 24.4 %collective-permute-start.1 = (bf16[96,768]{1,0:T(8,128)(2,1)S(1)}, bf16[96,768]{1,0:T(8,128)(2,1)S(1)}, u32[]{:S(2)}, u32[]{:S(2)}) collective-permute-start(bf16[96,768]{1,0:T(8,128)(2,1)S(1)} %pad_maximum_fusion.7), channel_id=1, source_target_pairs={{0,16},{4,20},{8,24},{12,28},{16,0},{20,4},{24,8},{28,12},{1,17},{... | collective-permute-start | bytes 442376 | tf_op jit(solution)/shard_map/ppermute | solution.py:648
  6.6 20.4 %collective-permute-start = (bf16[96,768]{1,0:T(8,128)(2,1)S(1)}, bf16[96,768]{1,0:T(8,128)(2,1)S(1)}, u32[]{:S(2)}, u32[]{:S(2)}) collective-permute-start(bf16[96,768]{1,0:T(8,128)(2,1)S(1)} %pad_maximum_fusion.7), channel_id=1, source_target_pairs={{0,8},{4,12},{8,0},{12,4},{16,24},{20,28},{24,16},{28,20},{1,9},{5... | collective-permute-start | bytes 442376 | tf_op jit(solution)/shard_map/ppermute | solution.py:648
  8.2 18.8 %collective-permute-start.2 = (bf16[96,768]{1,0:T(8,128)(2,1)S(1)}, bf16[96,768]{1,0:T(8,128)(2,1)S(1)}, u32[]{:S(2)}, u32[]{:S(2)}) collective-permute-start(bf16[96,768]{1,0:T(8,128)(2,1)S(1)} %pad_maximum_fusion.7), channel_id=1, source_target_pairs={{0,24},{4,28},{8,16},{12,20},{16,8},{20,12},{24,0},{28,4},{1,25},{... | collective-permute-start | bytes 442376 | tf_op jit(solution)/shard_map/ppermute | solution.py:648
  9.2 36.0 %collective-permute-start.9 = (bf16[96,1536]{1,0:T(8,128)(2,1)S(1)}, bf16[96,1536]{1,0:T(8,128)(2,1)S(1)}, u32[]{:S(2)}, u32[]{:S(2)}) collective-permute-start(bf16[96,1536]{1,0:T(8,128)(2,1)S(1)} %get-tuple-element.140), channel_id=1, source_target_pairs={{0,16},{4,20},{8,24},{12,28},{16,0},{20,4},{24,8},{28,12},{1,17},{... | collective-permute-start | bytes 884744 | tf_op jit(solution)/shard_map/ppermute | solution.py:648
  11.2 34.0 %collective-permute-start.8 = (bf16[96,1536]{1,0:T(8,128)(2,1)S(1)}, bf16[96,1536]{1,0:T(8,128)(2,1)S(1)}, u32[]{:S(2)}, u32[]{:S(2)}) collective-permute-start(bf16[96,1536]{1,0:T(8,128)(2,1)S(1)} %get-tuple-element.140), channel_id=1, source_target_pairs={{0,8},{4,12},{8,0},{12,4},{16,24},{20,28},{24,16},{28,20},{1,9},{5... | collective-permute-start | bytes 884744 | tf_op jit(solution)/shard_map/ppermute | solution.py:648
  26.9 18.3 %collective-permute-start.10 = (bf16[96,1536]{1,0:T(8,128)(2,1)S(1)}, bf16[96,1536]{1,0:T(8,128)(2,1)S(1)}, u32[]{:S(2)}, u32[]{:S(2)}) collective-permute-start(bf16[96,1536]{1,0:T(8,128)(2,1)S(1)} %get-tuple-element.140), channel_id=1, source_target_pairs={{0,24},{4,28},{8,16},{12,20},{16,8},{20,12},{24,0},{28,4},{1,25},{... | collective-permute-start | bytes 884744 | tf_op jit(solution)/shard_map/ppermute | solution.py:648
  27.0 17.6 %copy-start.19 = (f32[768]{0:T(1024)S(1)}, f32[768]{0:T(1024)}, u32[]{:S(2)}) copy-start(f32[768]{0:T(1024)} %param.22) | copy-start | bytes 9220
  27.1 18.3 %copy-start.1 = (bf16[4,96,768]{2,1,0:T(8,128)(2,1)}, bf16[4,96,768]{2,1,0:T(8,128)(2,1)S(1)}, u32[]{:S(2)}) copy-start(bf16[4,96,768]{2,1,0:T(8,128)(2,1)S(1)} %pad_maximum_fusion.3.refs_0_) | copy-start | bytes 1769476
  27.1 13.7 %collective-permute-start.4 = (bf16[4,96,768]{2,1,0:T(8,128)(2,1)S(1)}, bf16[4,96,768]{2,1,0:T(8,128)(2,1)S(1)}, u32[]{:S(2)}, u32[]{:S(2)}) collective-permute-start(bf16[4,96,768]{2,1,0:T(8,128)(2,1)S(1)} %pad_maximum_fusion.3.refs_0_), channel_id=1, source_target_pairs={{0,2},{1,3},{2,0},{3,1},{4,6},{5,7},{6,4},{7,5},{8,10},{9,11},{10,... | collective-permute-start | bytes 1769480 | tf_op jit(solution)/shard_map/ppermute | solution.py:643
  28.8 14.2 %collective-permute-start.3 = (bf16[4,96,768]{2,1,0:T(8,128)(2,1)S(1)}, bf16[4,96,768]{2,1,0:T(8,128)(2,1)S(1)}, u32[]{:S(2)}, u32[]{:S(2)}) collective-permute-start(bf16[4,96,768]{2,1,0:T(8,128)(2,1)S(1)} %pad_maximum_fusion.3.refs_0_), channel_id=1, source_target_pairs={{0,4},{4,0},{8,12},{12,8},{16,20},{20,16},{24,28},{28,24},{1,5},{5... | collective-permute-start | bytes 1769480 | tf_op jit(solution)/shard_map/ppermute | solution.py:648
  40.8 4.6 %copy-start.6 = (bf16[4,96,768]{2,1,0:T(8,128)(2,1)}, bf16[4,96,768]{2,1,0:T(8,128)(2,1)S(1)}, u32[]{:S(2)}) copy-start(bf16[4,96,768]{2,1,0:T(8,128)(2,1)S(1)} %collective-permute-done.4.refs_2_) | copy-start | bytes 1769476
  40.9 10.0 %collective-permute-start.6 = (bf16[2,96,768]{2,1,0:T(8,128)(2,1)S(1)}, bf16[2,96,768]{2,1,0:T(8,128)(2,1)S(1)}, u32[]{:S(2)}, u32[]{:S(2)}) collective-permute-start(bf16[2,96,768]{2,1,0:T(8,128)(2,1)S(1)} %slice.219), channel_id=1, source_target_pairs={{0,4},{4,0},{8,12},{12,8},{16,20},{20,16},{24,28},{28,24},{1,5},{5... | collective-permute-start | bytes 884744 | tf_op jit(solution)/shard_map/ppermute | solution.py:648
  43.0 10.0 %copy-start.7 = (bf16[4,96,768]{2,1,0:T(8,128)(2,1)}, bf16[4,96,768]{2,1,0:T(8,128)(2,1)S(1)}, u32[]{:S(2)}) copy-start(bf16[4,96,768]{2,1,0:T(8,128)(2,1)S(1)} %collective-permute-done.3.refs_1_) | copy-start | bytes 1769476
  43.0 10.0 %collective-permute-start.5 = (bf16[2,96,768]{2,1,0:T(8,128)(2,1)S(1)}, bf16[2,96,768]{2,1,0:T(8,128)(2,1)S(1)}, u32[]{:S(2)}, u32[]{:S(2)}) collective-permute-start(bf16[2,96,768]{2,1,0:T(8,128)(2,1)S(1)} %slice.218), channel_id=1, source_target_pairs={{0,2},{1,3},{2,0},{3,1},{4,6},{5,7},{6,4},{7,5},{8,10},{9,11},{10,... | collective-permute-start | bytes 884744 | tf_op jit(solution)/shard_map/ppermute | solution.py:643
  45.4 19.2 %copy-start.11 = (bf16[4,96,1536]{2,1,0:T(8,128)(2,1)}, bf16[4,96,1536]{2,1,0:T(8,128)(2,1)S(1)}, u32[]{:S(2)}) copy-start(bf16[4,96,1536]{2,1,0:T(8,128)(2,1)S(1)} %pad_maximum_fusion.refs_0_) | copy-start | bytes 3538948
  45.4 51.2 %collective-permute-start.12 = (bf16[4,96,1536]{2,1,0:T(8,128)(2,1)S(1)}, bf16[4,96,1536]{2,1,0:T(8,128)(2,1)S(1)}, u32[]{:S(2)}, u32[]{:S(2)}) collective-permute-start(bf16[4,96,1536]{2,1,0:T(8,128)(2,1)S(1)} %pad_maximum_fusion.refs_0_), channel_id=1, source_target_pairs={{0,2},{1,3},{2,0},{3,1},{4,6},{5,7},{6,4},{7,5},{8,10},{9,11},{10,... | collective-permute-start | bytes 3538952 | tf_op jit(solution)/shard_map/ppermute | solution.py:643
  46.6 51.9 %collective-permute-start.11 = (bf16[4,96,1536]{2,1,0:T(8,128)(2,1)S(1)}, bf16[4,96,1536]{2,1,0:T(8,128)(2,1)S(1)}, u32[]{:S(2)}, u32[]{:S(2)}) collective-permute-start(bf16[4,96,1536]{2,1,0:T(8,128)(2,1)S(1)} %pad_maximum_fusion.refs_0_), channel_id=1, source_target_pairs={{0,4},{4,0},{8,12},{12,8},{16,20},{20,16},{24,28},{28,24},{1,5},{5... | collective-permute-start | bytes 3538952 | tf_op jit(solution)/shard_map/ppermute | solution.py:648
  50.9 2.2 copy-start.17
  96.5 2.0 copy-start.20
  96.5 17.5 %collective-permute-start.7 = (bf16[1024,768]{1,0:T(8,128)(2,1)}, bf16[1024,768]{1,0:T(8,128)(2,1)S(1)}, u32[]{:S(2)}, u32[]{:S(2)}) collective-permute-start(bf16[1024,768]{1,0:T(8,128)(2,1)} %get-tuple-element.73.a_ref), channel_id=1, source_target_pairs={{0,1},{1,0},{2,3},{3,2},{4,5},{5,4},{6,7},{7,6},{8,9},{9,8},{10,11... | collective-permute-start | bytes 4718600 | tf_op jit(solution)/shard_map/ppermute | solution.py:639
  96.6 17.4 %copy-start.15 = (bf16[4,96,1536]{2,1,0:T(8,128)(2,1)}, bf16[4,96,1536]{2,1,0:T(8,128)(2,1)S(1)}, u32[]{:S(2)}) copy-start(bf16[4,96,1536]{2,1,0:T(8,128)(2,1)S(1)} %collective-permute-done.12.refs_2_) | copy-start | bytes 3538948
  96.7 15.8 %collective-permute-start.14 = (bf16[2,96,1536]{2,1,0:T(8,128)(2,1)S(1)}, bf16[2,96,1536]{2,1,0:T(8,128)(2,1)S(1)}, u32[]{:S(2)}, u32[]{:S(2)}) collective-permute-start(bf16[2,96,1536]{2,1,0:T(8,128)(2,1)S(1)} %slice.221), channel_id=1, source_target_pairs={{0,4},{4,0},{8,12},{12,8},{16,20},{20,16},{24,28},{28,24},{1,5},{5... | collective-permute-start | bytes 1769480 | tf_op jit(solution)/shard_map/ppermute | solution.py:648
  98.4 15.6 %copy-start.16 = (bf16[4,96,1536]{2,1,0:T(8,128)(2,1)}, bf16[4,96,1536]{2,1,0:T(8,128)(2,1)S(1)}, u32[]{:S(2)}) copy-start(bf16[4,96,1536]{2,1,0:T(8,128)(2,1)S(1)} %collective-permute-done.11.refs_1_) | copy-start | bytes 3538948
  98.5 15.5 %collective-permute-start.13 = (bf16[2,96,1536]{2,1,0:T(8,128)(2,1)S(1)}, bf16[2,96,1536]{2,1,0:T(8,128)(2,1)S(1)}, u32[]{:S(2)}, u32[]{:S(2)}) collective-permute-start(bf16[2,96,1536]{2,1,0:T(8,128)(2,1)S(1)} %slice.220), channel_id=1, source_target_pairs={{0,2},{1,3},{2,0},{3,1},{4,6},{5,7},{6,4},{7,5},{8,10},{9,11},{10,... | collective-permute-start | bytes 1769480 | tf_op jit(solution)/shard_map/ppermute | solution.py:643
  112.5 1.6 copy-start.23
  114.8 1.2 copy-start.3
  143.6 7.0 %copy-start.2 = (bf16[768,1024]{1,0:T(8,128)(2,1)S(1)}, bf16[768,1024]{1,0:T(8,128)(2,1)}, u32[]{:S(2)}) copy-start(bf16[768,1024]{1,0:T(8,128)(2,1)} %get-tuple-element.75) | copy-start | bytes 4718596
  143.6 14.9 %collective-permute-start.34 = (bf16[2,96,1536]{2,1,0:T(8,128)(2,1)}, bf16[2,96,1536]{2,1,0:T(8,128)(2,1)S(1)}, u32[]{:S(2)}, u32[]{:S(2)}) collective-permute-start(bf16[2,96,1536]{2,1,0:T(8,128)(2,1)} %get-tuple-element.98), channel_id=1, source_target_pairs={{0,4},{4,0},{8,12},{12,8},{16,20},{20,16},{24,28},{28,24},{1,5},{5... | collective-permute-start | bytes 1769480 | tf_op jit(solution)/shard_map/ppermute | solution.py:648
  144.6 5.0 %copy-start.22 = (bf16[2,96,1536]{2,1,0:T(8,128)(2,1)S(1)}, bf16[2,96,1536]{2,1,0:T(8,128)(2,1)}, u32[]{:S(2)}) copy-start(bf16[2,96,1536]{2,1,0:T(8,128)(2,1)} %get-tuple-element.96) | copy-start | bytes 1769476
  148.4 2.4 copy-start.4
  149.6 16.3 %collective-permute-start.32 = (bf16[2,96,1536]{2,1,0:T(8,128)(2,1)S(1)}, bf16[2,96,1536]{2,1,0:T(8,128)(2,1)S(1)}, u32[]{:S(2)}, u32[]{:S(2)}) collective-permute-start(bf16[2,96,1536]{2,1,0:T(8,128)(2,1)S(1)} %copy-done.22), channel_id=1, source_target_pairs={{0,2},{1,3},{2,0},{3,1},{4,6},{5,7},{6,4},{7,5},{8,10},{9,11},{10,... | collective-permute-start | bytes 1769480 | tf_op jit(solution)/shard_map/ppermute | solution.py:643
  150.6 18.2 %collective-permute-start.15 = (bf16[384,1024]{1,0:T(8,128)(2,1)S(1)}, bf16[384,1024]{1,0:T(8,128)(2,1)S(1)}, u32[]{:S(2)}, u32[]{:S(2)}) collective-permute-start(bf16[384,1024]{1,0:T(8,128)(2,1)S(1)} %slice.166), channel_id=1, source_target_pairs={{0,1},{1,0},{2,3},{3,2},{4,5},{5,4},{6,7},{7,6},{8,9},{9,8},{10,11... | collective-permute-start | bytes 2359304 | tf_op jit(solution)/shard_map/ppermute | solution.py:639
  150.7 21.3 %collective-permute-start.17 = (bf16[1024,768]{1,0:T(8,128)(2,1)S(1)}, bf16[1024,768]{1,0:T(8,128)(2,1)S(1)}, u32[]{:S(2)}, u32[]{:S(2)}) collective-permute-start(bf16[1024,768]{1,0:T(8,128)(2,1)S(1)} %copy-done.4), channel_id=1, source_target_pairs={{0,1},{1,0},{2,3},{3,2},{4,5},{5,4},{6,7},{7,6},{8,9},{9,8},{10,11... | collective-permute-start | bytes 4718600 | tf_op jit(solution)/shard_map/ppermute | solution.py:639
  151.2 7.2 %copy-start.10 = (bf16[4,96,1536]{2,1,0:T(8,128)(2,1)S(1)}, bf16[4,96,1536]{2,1,0:T(8,128)(2,1)}, u32[]{:S(2)}) copy-start(bf16[4,96,1536]{2,1,0:T(8,128)(2,1)} %get-tuple-element.97) | copy-start | bytes 3538948
  158.6 7.3 %copy-start.9 = (bf16[4,96,1536]{2,1,0:T(8,128)(2,1)S(1)}, bf16[4,96,1536]{2,1,0:T(8,128)(2,1)}, u32[]{:S(2)}) copy-start(bf16[4,96,1536]{2,1,0:T(8,128)(2,1)} %get-tuple-element.95) | copy-start | bytes 3538948
  159.7 113.0 %collective-permute-start.35 = (bf16[4,96,1536]{2,1,0:T(8,128)(2,1)}, bf16[4,96,1536]{2,1,0:T(8,128)(2,1)S(1)}, u32[]{:S(2)}, u32[]{:S(2)}) collective-permute-start(bf16[4,96,1536]{2,1,0:T(8,128)(2,1)} %pad_maximum_fusion.2), channel_id=1, source_target_pairs={{0,2},{1,3},{2,0},{3,1},{4,6},{5,7},{6,4},{7,5},{8,10},{9,11},{10,... | collective-permute-start | bytes 3538952 | tf_op jit(solution)/shard_map/ppermute | solution.py:643
  167.2 105.5 %collective-permute-start.33 = (bf16[4,96,1536]{2,1,0:T(8,128)(2,1)}, bf16[4,96,1536]{2,1,0:T(8,128)(2,1)}, u32[]{:S(2)}, u32[]{:S(2)}) collective-permute-start(bf16[4,96,1536]{2,1,0:T(8,128)(2,1)} %pad_maximum_fusion.1), channel_id=1, source_target_pairs={{0,4},{4,0},{8,12},{12,8},{16,20},{20,16},{24,28},{28,24},{1,5},{5... | collective-permute-start | bytes 3538952 | tf_op jit(solution)/shard_map/ppermute | solution.py:648
  170.3 95.6 %collective-permute-start.16 = (bf16[192,1024]{1,0:T(8,128)(2,1)S(1)}, bf16[192,1024]{1,0:T(8,128)(2,1)S(1)}, u32[]{:S(2)}, u32[]{:S(2)}) collective-permute-start(bf16[192,1024]{1,0:T(8,128)(2,1)S(1)} %get-tuple-element.128), channel_id=1, source_target_pairs={{0,2},{1,3},{2,0},{3,1},{4,6},{5,7},{6,4},{7,5},{8,10},{9,11},{10,... | collective-permute-start | bytes 1179656 | tf_op jit(solution)/shard_map/ppermute | solution.py:643
  172.0 1.1 copy-start.5
  227.1 22.9 %copy-start.21 = (f32[1,768]{1,0:T(1,128)S(1)}, f32[1,768]{1,0:T(1,128)}, u32[]{:S(2)}) copy-start(f32[1,768]{1,0:T(1,128)} %get-tuple-element.87) | copy-start | bytes 9220
  250.0 17.0 %copy-start.13 = (bf16[4,96,768]{2,1,0:T(8,128)(2,1)S(1)}, bf16[4,96,768]{2,1,0:T(8,128)(2,1)}, u32[]{:S(2)}) copy-start(bf16[4,96,768]{2,1,0:T(8,128)(2,1)} %get-tuple-element.90) | copy-start | bytes 1769476
  250.0 17.0 %copy-start.14 = (bf16[4,96,768]{2,1,0:T(8,128)(2,1)S(1)}, bf16[4,96,768]{2,1,0:T(8,128)(2,1)}, u32[]{:S(2)}) copy-start(bf16[4,96,768]{2,1,0:T(8,128)(2,1)} %get-tuple-element.92) | copy-start | bytes 1769476
  250.8 1.2 collective-permute-start.20
  252.1 3.7 %collective-permute-start.21 = (f32[1664]{0:T(1024)S(1)}, f32[1664]{0:T(1024)S(1)}, u32[]{:S(2)}, u32[]{:S(2)}) collective-permute-start(f32[1664]{0:T(1024)S(1)} %fusion.33), channel_id=1, source_target_pairs={{0,2},{1,3},{2,0},{3,1},{4,6},{5,7},{6,4},{7,5},{8,10},{9,11},{10,... | collective-permute-start | bytes 19976 | tf_op jit(solution)/shard_map/ppermute | solution.py:643
  255.7 3.7 %collective-permute-start.22 = (f32[1664]{0:T(1024)S(1)}, f32[1664]{0:T(1024)S(1)}, u32[]{:S(2)}, u32[]{:S(2)}) collective-permute-start(f32[1664]{0:T(1024)S(1)} %add.140), channel_id=1, source_target_pairs={{0,4},{4,0},{8,12},{12,8},{16,20},{20,16},{24,28},{28,24},{1,5},{5... | collective-permute-start | bytes 19976 | tf_op jit(solution)/shard_map/ppermute | solution.py:648
  259.4 3.7 %collective-permute-start.23 = (f32[1664]{0:T(1024)S(1)}, f32[1664]{0:T(1024)S(1)}, u32[]{:S(2)}, u32[]{:S(2)}) collective-permute-start(f32[1664]{0:T(1024)S(1)} %add.141), channel_id=1, source_target_pairs={{0,8},{4,12},{8,0},{12,4},{16,24},{20,28},{24,16},{28,20},{1,9},{5... | collective-permute-start | bytes 19976 | tf_op jit(solution)/shard_map/ppermute | solution.py:648
  259.4 7.7 %copy-start.25 = (bf16[2,96,768]{2,1,0:T(8,128)(2,1)S(1)}, bf16[2,96,768]{2,1,0:T(8,128)(2,1)}, u32[]{:S(2)}) copy-start(bf16[2,96,768]{2,1,0:T(8,128)(2,1)} %get-tuple-element.91) | copy-start | bytes 884740
  259.4 8.8 %copy-start.26 = (bf16[2,96,768]{2,1,0:T(8,128)(2,1)S(1)}, bf16[2,96,768]{2,1,0:T(8,128)(2,1)}, u32[]{:S(2)}) copy-start(bf16[2,96,768]{2,1,0:T(8,128)(2,1)} %get-tuple-element.93) | copy-start | bytes 884740
  263.1 7.7 %collective-permute-start.24 = (f32[1664]{0:T(1024)S(1)}, f32[1664]{0:T(1024)S(1)}, u32[]{:S(2)}, u32[]{:S(2)}) collective-permute-start(f32[1664]{0:T(1024)S(1)} %add.142), channel_id=1, source_target_pairs={{0,16},{4,20},{8,24},{12,28},{16,0},{20,4},{24,8},{28,12},{1,17},{... | collective-permute-start | bytes 19976 | tf_op jit(solution)/shard_map/ppermute | solution.py:648
  267.1 11.1 %collective-permute-start.25 = (bf16[2,96,768]{2,1,0:T(8,128)(2,1)S(1)}, bf16[2,96,768]{2,1,0:T(8,128)(2,1)S(1)}, u32[]{:S(2)}, u32[]{:S(2)}) collective-permute-start(bf16[2,96,768]{2,1,0:T(8,128)(2,1)S(1)} %copy-done.25), channel_id=1, source_target_pairs={{0,2},{1,3},{2,0},{3,1},{4,6},{5,7},{6,4},{7,5},{8,10},{9,11},{10,... | collective-permute-start | bytes 884744 | tf_op jit(solution)/shard_map/ppermute | solution.py:643
  268.2 7.8 %collective-permute-start.27 = (bf16[2,96,768]{2,1,0:T(8,128)(2,1)S(1)}, bf16[2,96,768]{2,1,0:T(8,128)(2,1)S(1)}, u32[]{:S(2)}, u32[]{:S(2)}) collective-permute-start(bf16[2,96,768]{2,1,0:T(8,128)(2,1)S(1)} %copy-done.26), channel_id=1, source_target_pairs={{0,4},{4,0},{8,12},{12,8},{16,20},{20,16},{24,28},{28,24},{1,5},{5... | collective-permute-start | bytes 884744 | tf_op jit(solution)/shard_map/ppermute | solution.py:648
  269.1 3.6 %copy-start.8 = (bf16[4,96,1536]{2,1,0:T(8,128)(2,1)S(1)}, bf16[4,96,1536]{2,1,0:T(8,128)(2,1)}, u32[]{:S(2)}) copy-start(bf16[4,96,1536]{2,1,0:T(8,128)(2,1)} %get-tuple-element.94) | copy-start | bytes 3538948
  270.8 33.7 %collective-permute-start.18 = (bf16[384,2048]{1,0:T(8,128)(2,1)S(1)}, bf16[384,2048]{1,0:T(8,128)(2,1)S(1)}, u32[]{:S(2)}, u32[]{:S(2)}) collective-permute-start(bf16[384,2048]{1,0:T(8,128)(2,1)S(1)} %slice.170), channel_id=1, source_target_pairs={{0,1},{1,0},{2,3},{3,2},{4,5},{5,4},{6,7},{7,6},{8,9},{9,8},{10,11... | collective-permute-start | bytes 4718600 | tf_op jit(solution)/shard_map/ppermute | solution.py:639
  274.5 15.8 %collective-permute-start.36 = (bf16[96,1536]{1,0:T(8,128)(2,1)S(1)}, bf16[96,1536]{1,0:T(8,128)(2,1)S(1)}, u32[]{:S(2)}, u32[]{:S(2)}) collective-permute-start(bf16[96,1536]{1,0:T(8,128)(2,1)S(1)} %get-tuple-element.124), channel_id=1, source_target_pairs={{0,8},{4,12},{8,0},{12,4},{16,24},{20,28},{24,16},{28,20},{1,9},{5... | collective-permute-start | bytes 884744 | tf_op jit(solution)/shard_map/ppermute | solution.py:648
  276.0 14.9 %collective-permute-start.38 = (bf16[96,1536]{1,0:T(8,128)(2,1)S(1)}, bf16[96,1536]{1,0:T(8,128)(2,1)S(1)}, u32[]{:S(2)}, u32[]{:S(2)}) collective-permute-start(bf16[96,1536]{1,0:T(8,128)(2,1)S(1)} %get-tuple-element.125), channel_id=1, source_target_pairs={{0,24},{4,28},{8,16},{12,20},{16,8},{20,12},{24,0},{28,4},{1,25},{... | collective-permute-start | bytes 884744 | tf_op jit(solution)/shard_map/ppermute | solution.py:648
  276.0 28.1 %collective-permute-start.37 = (bf16[96,1536]{1,0:T(8,128)(2,1)S(1)}, bf16[96,1536]{1,0:T(8,128)(2,1)S(1)}, u32[]{:S(2)}, u32[]{:S(2)}) collective-permute-start(bf16[96,1536]{1,0:T(8,128)(2,1)S(1)} %get-tuple-element.126), channel_id=1, source_target_pairs={{0,16},{4,20},{8,24},{12,28},{16,0},{20,4},{24,8},{28,12},{1,17},{... | collective-permute-start | bytes 884744 | tf_op jit(solution)/shard_map/ppermute | solution.py:648
  278.2 26.0 %collective-permute-start.28 = (bf16[4,96,768]{2,1,0:T(8,128)(2,1)S(1)}, bf16[4,96,768]{2,1,0:T(8,128)(2,1)S(1)}, u32[]{:S(2)}, u32[]{:S(2)}) collective-permute-start(bf16[4,96,768]{2,1,0:T(8,128)(2,1)S(1)} %pad_maximum_fusion.5), channel_id=1, source_target_pairs={{0,2},{1,3},{2,0},{3,1},{4,6},{5,7},{6,4},{7,5},{8,10},{9,11},{10,... | collective-permute-start | bytes 1769480 | tf_op jit(solution)/shard_map/ppermute | solution.py:643
  280.1 24.2 %copy-start.12 = (bf16[4,96,768]{2,1,0:T(8,128)(2,1)S(1)}, bf16[4,96,768]{2,1,0:T(8,128)(2,1)}, u32[]{:S(2)}) copy-start(bf16[4,96,768]{2,1,0:T(8,128)(2,1)} %get-tuple-element.89) | copy-start | bytes 1769476
  290.3 14.0 %collective-permute-start.26 = (bf16[4,96,768]{2,1,0:T(8,128)(2,1)S(1)}, bf16[4,96,768]{2,1,0:T(8,128)(2,1)S(1)}, u32[]{:S(2)}, u32[]{:S(2)}) collective-permute-start(bf16[4,96,768]{2,1,0:T(8,128)(2,1)S(1)} %pad_maximum_fusion.4), channel_id=1, source_target_pairs={{0,4},{4,0},{8,12},{12,8},{16,20},{20,16},{24,28},{28,24},{1,5},{5... | collective-permute-start | bytes 1769480 | tf_op jit(solution)/shard_map/ppermute | solution.py:648
  304.3 1.9 copy-start
  307.8 19.2 %collective-permute-start.19 = (bf16[192,2048]{1,0:T(8,128)(2,1)}, bf16[192,2048]{1,0:T(8,128)(2,1)}, u32[]{:S(2)}, u32[]{:S(2)}) collective-permute-start(bf16[192,2048]{1,0:T(8,128)(2,1)} %slice.285), channel_id=1, source_target_pairs={{0,2},{1,3},{2,0},{3,1},{4,6},{5,7},{6,4},{7,5},{8,10},{9,11},{10,... | collective-permute-start | bytes 2359304 | tf_op jit(solution)/shard_map/ppermute | solution.py:643
  309.5 7.9 %collective-permute-start.29 = (bf16[96,768]{1,0:T(8,128)(2,1)S(1)}, bf16[96,768]{1,0:T(8,128)(2,1)S(1)}, u32[]{:S(2)}, u32[]{:S(2)}) collective-permute-start(bf16[96,768]{1,0:T(8,128)(2,1)S(1)} %get-tuple-element.132), channel_id=1, source_target_pairs={{0,8},{4,12},{8,0},{12,4},{16,24},{20,28},{24,16},{28,20},{1,9},{5... | collective-permute-start | bytes 442376 | tf_op jit(solution)/shard_map/ppermute | solution.py:648
  309.6 8.8 %collective-permute-start.31 = (bf16[96,768]{1,0:T(8,128)(2,1)S(1)}, bf16[96,768]{1,0:T(8,128)(2,1)S(1)}, u32[]{:S(2)}, u32[]{:S(2)}) collective-permute-start(bf16[96,768]{1,0:T(8,128)(2,1)S(1)} %get-tuple-element.133), channel_id=1, source_target_pairs={{0,24},{4,28},{8,16},{12,20},{16,8},{20,12},{24,0},{28,4},{1,25},{... | collective-permute-start | bytes 442376 | tf_op jit(solution)/shard_map/ppermute | solution.py:648
  310.8 14.3 %collective-permute-start.30 = (bf16[96,768]{1,0:T(8,128)(2,1)S(1)}, bf16[96,768]{1,0:T(8,128)(2,1)S(1)}, u32[]{:S(2)}, u32[]{:S(2)}) collective-permute-start(bf16[96,768]{1,0:T(8,128)(2,1)S(1)} %get-tuple-element.134), channel_id=1, source_target_pairs={{0,16},{4,20},{8,24},{12,28},{16,0},{20,4},{24,8},{28,12},{1,17},{... | collective-permute-start | bytes 442376 | tf_op jit(solution)/shard_map/ppermute | solution.py:648
  (2 other events, 1.6 us)

commit v2 on v0

v2 whole, which is shorter than its diff:
```python
import functools

import jax
import jax.numpy as jnp
from jax import lax
from jax.experimental import pallas as pl
from jax.experimental.pallas import tpu as pltpu
from jax.sharding import PartitionSpec as P

f32 = jnp.float32
bf16 = jnp.bfloat16
HEAD_DIM = 64
UNIT = 512
LANES = 128
epsilon = 1e-06
BIG = 1e30
GELU_C = 0.7978845608028654
GELU_A = 0.044715
HEAD_VMEM, FEED_VMEM, MID_VMEM, BACK_VMEM, LAST_VMEM = 24, 40, 40, 40, 40

NT = (((1,), (1,)), ((), ()))
NN = (((1,), (0,)), ((), ()))
TN = (((0,), (0,)), ((), ()))


def mm(a, b, dims=NN):
    return lax.dot_general(a, b, dims, preferred_element_type=f32)


def split3(v):
    high = v.astype(bf16)
    rest = v - high.astype(f32)
    middle = rest.astype(bf16)
    low = (rest - middle.astype(f32)).astype(bf16)
    return high.astype(f32), middle.astype(f32), low.astype(f32)


def lane_halves():
    lane = lax.broadcasted_iota(jnp.int32, (1, LANES), 1)
    first = (lane < HEAD_DIM).astype(f32)
    return lane, first.astype(bf16), (1.0 - first).astype(bf16)


def block_rows(index, rows, step):
    return pl.ds(pl.multiple_of(index * rows, step), rows)


def block_copies(table, sources, target, wide_index, rows, sem, columns=None):
    step = 16 if rows % 16 == 0 else 8
    copies = []
    for k, (src, lead, half, offset) in enumerate(table):
        source = sources[src].at[lead]
        if columns is not None:
            source = source.at[:, pl.ds(0, columns)]
        copies.append(
            pltpu.make_async_copy(
                source, target.at[half, block_rows(wide_index ^ offset, rows, step), :], sem.at[k]
            )
        )
    return copies


def start_all(copies):
    for copy in copies:
        copy.start()
    return copies


def wait_all(copies):
    for copy in copies:
        copy.wait()


def load_blocks(*args):
    wait_all(start_all(block_copies(*args)))


def store_blocks(table, acc, targets, wide_index, rows):
    for src, lead, half, offset in table:
        targets[src][lead] = acc[half, block_rows(wide_index ^ offset, rows, 8), :].astype(bf16)


def padded(weights, width):
    return jnp.concatenate(
        [weights, jnp.zeros((weights.shape[0], width - weights.shape[1]), weights.dtype)], axis=1
    )


X_HALF, WIDE, NARROW, ITEMS = 0, 1, 2, 3


def unit_item(s_ref, unit, units):
    start = (unit * UNIT) & -s_ref[ITEMS + unit]
    return start, s_ref[ITEMS + units + unit]


def live_rows(s_ref, first, tile, units):
    start, valid = unit_item(s_ref, first // UNIT, units)
    return first - start + lax.broadcasted_iota(jnp.int32, (tile, 1), 0) < valid


def query_mask(s_ref, first, lane, units):
    start, _ = unit_item(s_ref, first // UNIT, units)
    column = lane & (HEAD_DIM - 1)
    named = (column < units) & (column != start // UNIT)
    return jnp.where(named | (column == units), 1.0, 0.0)


def key_mask(s_ref, unit, lane, units):
    start, valid = unit_item(s_ref, unit, units)
    column = lane & (HEAD_DIM - 1)
    row = unit * UNIT - start + lax.broadcasted_iota(jnp.int32, (UNIT, 1), 0)
    fixed = jnp.where(column == start // UNIT, -BIG, 0.0)
    fixed = jnp.where((column > units) & (column < units + 4), -1.0, fixed)
    return jnp.where((column == units) & (row >= valid), -BIG, fixed)


def any_specs(arrays):
    return [pl.BlockSpec(memory_space=pl.ANY)] * len(arrays)


def own_tile(i, s, half):
    return jnp.clip(i - s[0] * half, 0, half - 1)


def params(mebibytes):
    return pltpu.CompilerParams(vmem_limit_bytes=mebibytes << 20)


def cost(flops, moved, exps=0):
    return pl.CostEstimate(flops=flops, bytes_accessed=moved, transcendentals=exps)


def once(shape):
    return pl.BlockSpec(shape, lambda *_: (0,) * len(shape), pipeline_mode=pl.Buffered(1))


def head_list(share):
    return [(h // 2, h % 2) for h in range(share // HEAD_DIM)]


def head_lanes(share):
    return -(-share // LANES) * LANES


def head_kernel(
    tables, counts, rows, share, first_shard, sub, chunk, s_ref, x_ref, gain_ref, *refs
):
    heads = head_list(share)
    lane, first, second = lane_halves()
    final = len(tables) == 2
    if final:
        before_ref, refs = refs[0], refs[1:]
    sources = [refs[: counts[0]], refs[counts[0] : sum(counts)]]
    refs = refs[sum(counts) :]
    if first_shard:
        normed_out, refs = refs[0], refs[1:]
    q_out, k_out, v_out, o_ref, aux_ref = refs[:5]
    refs = refs[5:]
    if final:
        part_ref, refs = refs[0], refs[1:]
    buf, weights, values_in, normed, qs, ks, vs, keys, values, sem, in_sem, out_sem = refs[:12]
    n, d = normed.shape
    n_q = qs.shape[0]
    units = n // UNIT
    loads = start_all(block_copies(tables[0], sources[0], buf, s_ref[WIDE], rows, sem.at[0]))
    target = values_in if first_shard else normed
    unit_rows = [slice(u * UNIT, (u + 1) * UNIT) for u in range(units)]
    inputs = start_all(
        [
            pltpu.make_async_copy(x_ref.at[here, :], target.at[here, :], in_sem.at[u])
            for u, here in enumerate(unit_rows)
        ]
    )
    if final:
        other = start_all(
            block_copies(tables[1], sources[1], refs[12], s_ref[WIDE], rows, sem.at[1], refs[12].shape[2])
        )
    wait_all(loads)
    for at in range(3):
        weights[at] = padded(buf[0, :, (at + 1) * share : (at + 2) * share], weights.shape[2])
    outputs = []

    def send(source, to):
        copy = pltpu.make_async_copy(source, to, out_sem.at[len(outputs)])
        copy.start()
        outputs.append(copy)

    ones = [(lane == 64).astype(f32).astype(bf16), (lane == 0).astype(f32).astype(bf16)]
    for u, here in enumerate(unit_rows):
        inputs[u].wait()
        if first_shard:
            x = values_in[here, :].astype(f32)
            scale = lax.rsqrt(jnp.mean(x * x, axis=1, keepdims=True) + epsilon)
            normed[here, :] = (x * scale * gain_ref[...]).astype(bf16)
            send(normed.at[here, :], normed_out.at[here, :])
        rows_in = normed[here, :]
        k = mm(rows_in, weights[1]).astype(bf16)
        v = mm(rows_in, weights[2]).astype(bf16)
        ks[here, :] = k
        vs[here, :] = v
        mask = key_mask(s_ref, u, lane, units).astype(bf16)
        for at, (pair, side) in enumerate(heads):
            lanes = slice(pair * LANES, (pair + 1) * LANES)
            own, rest = (second, first) if side else (first, second)
            keys[at, here, :] = k[:, lanes] * own + mask * rest
            values[at, here, :] = v[:, lanes] * own + ones[side]
    send(ks, k_out)
    send(vs, v_out)
    qs[...] = mm(normed[block_rows(s_ref[X_HALF], n_q, UNIT), :], weights[0]).astype(bf16)
    send(qs, q_out)

    jobs = [(r, at) for r in range(0, n_q, sub) for at in range(len(heads))]
    marks = {
        r: query_mask(s_ref, s_ref[X_HALF] * n_q + r, lane, units) for r in range(0, n_q, sub)
    }

    def scores(job):
        r, at = job
        pair, side = heads[at]
        own, rest = (second, first) if side else (first, second)
        query = qs[r : r + sub, pair * LANES : (pair + 1) * LANES] * own + marks[r].astype(bf16) * rest
        return [lambda c=c: mm(query, keys[at, c : c + chunk, :], NT) for c in range(0, n, chunk)]

    outs, sums = {}, {}
    current = [f() for f in scores(jobs[0])]
    for j, (r, at) in enumerate(jobs):
        ahead = scores(jobs[j + 1]) if j + 1 < len(jobs) else []
        following = []
        top = functools.reduce(jnp.maximum, [jnp.max(s, axis=1, keepdims=True) for s in current])
        mixed = None
        for i, s in enumerate(current):
            if ahead:
                following.append(ahead[i]())
            part = mm(jnp.exp(s - top).astype(bf16), values[at, i * chunk : (i + 1) * chunk, :])
            mixed = part if mixed is None else mixed + part
        pair, side = heads[at]
        row_sum = mixed[:, 0:1] if side else mixed[:, HEAD_DIM : HEAD_DIM + 1]
        outs[side] = mixed / row_sum
        sums[side] = top + jnp.log(row_sum)
        current = following
        if side == 0 and (pair, 1) in heads:
            continue
        here, lanes = slice(r, r + sub), slice(pair * LANES, (pair + 1) * LANES)
        features = jnp.broadcast_to(marks[r], (sub, LANES))
        for which, value in sums.items():
            for i, piece in enumerate(split3(value)):
                features = jnp.where(lane == (units + 1 if which else 64 + units + 1) + i, piece, features)
        aux_ref[here, lanes] = features.astype(bf16)
        right = outs[1] if 1 in outs else 0.0
        o_ref[here, lanes] = jnp.where(lane < HEAD_DIM, outs[0], right).astype(bf16)
        outs, sums = {}, {}
    if final:
        wait_all(other)
        lanes = o_ref.shape[1]
        part = mm(before_ref[...], refs[12][0], NT) + mm(o_ref[...], buf[0, :, :lanes], NT)
        part_ref[...] = part.astype(bf16)
    wait_all(outputs)


def head_forward(scalars, values, gain, weights, rows, share, first_shard, before=None, sub=256, chunk=512):
    n, d = values.shape
    lanes = head_lanes(share)
    heads = share // HEAD_DIM
    tables, sources = [weights[0][0]], [weights[0][1]]
    args = [scalars, values, gain]
    in_specs = [pl.BlockSpec(memory_space=pl.ANY), once((1, d))]
    width = sources[0][0].shape[-1]
    q_shape, k_shape = (n // 2, lanes), (n, lanes)
    shapes = [q_shape, k_shape, k_shape, q_shape, q_shape]
    if first_shard:
        shapes = [(n, d)] + shapes
    out_specs = [pl.BlockSpec(memory_space=pl.ANY)] * (len(shapes) - 2) + [once(q_shape)] * 2
    scratch = [
        pltpu.VMEM((1, d, width), bf16),
        pltpu.VMEM((3, d, lanes), bf16),
        pltpu.VMEM((n, d) if first_shard else (16, LANES), bf16),
        pltpu.VMEM((n, d), bf16),
        pltpu.VMEM(q_shape, bf16),
        pltpu.VMEM(k_shape, bf16),
        pltpu.VMEM(k_shape, bf16),
        pltpu.VMEM((heads, n, LANES), bf16),
        pltpu.VMEM((heads, n, LANES), bf16),
        pltpu.SemaphoreType.DMA((2, len(tables[0]))),
        pltpu.SemaphoreType.DMA((n // UNIT,)),
        pltpu.SemaphoreType.DMA((n // UNIT + 3,)),
    ]
    if before is not None:
        tables.append(weights[1][0])
        sources.append(weights[1][1])
        args.append(before)
        in_specs.append(once(before.shape))
        shapes.append((n // 2, d))
        out_specs.append(once((n // 2, d)))
        scratch.append(pltpu.VMEM((1, d, lanes), bf16))
    counts = tuple(len(part) for part in sources)
    for part in sources:
        args += part
        in_specs += any_specs(part)
    return pl.pallas_call(
        functools.partial(head_kernel, tables, counts, rows, share, first_shard, sub, chunk),
        out_shape=tuple(jax.ShapeDtypeStruct(shape, bf16) for shape in shapes),
        grid_spec=pltpu.PrefetchScalarGridSpec(
            num_scalar_prefetch=1,
            grid=(1,),
            in_specs=in_specs,
            out_specs=out_specs,
            scratch_shapes=scratch,
        ),
        compiler_params=params(HEAD_VMEM),
        cost_estimate=cost(20 * n * n * share // 2, 8 * n * d, n * n * heads),
        name="head_forward",
    )(*args)


def mid_norm(x_ref, a_ref, b_ref):
    attn = a_ref[...].astype(f32) + b_ref[...].astype(f32)
    middle = x_ref[...].astype(f32) + attn
    scale = lax.rsqrt(jnp.mean(middle * middle, axis=1, keepdims=True) + epsilon)
    return attn, middle, scale


def store_quarters(narrow_index, value, keep_ref, send_ref):
    quarter = value.shape[0] // 4
    for block in range(4):
        at = narrow_index ^ block
        here = block_rows(at // 2, quarter, 16)
        piece = value[block * quarter : (block + 1) * quarter, :]

        @pl.when(at % 2 == 0)
        def _():
            keep_ref[here, :] = piece.astype(keep_ref.dtype)

        if send_ref is not None:

            @pl.when(at % 2 == 1)
            def _():
                send_ref[here, :] = piece.astype(send_ref.dtype)


def feed_half(normed, grad, buf, acc, first):
    ff = buf.shape[2] // 3
    w_gate, w_up, w_down = [buf[0, :, at * ff : (at + 1) * ff] for at in range(3)]
    gate = mm(normed, w_gate)
    up = mm(normed, w_up)
    back_hidden = mm(grad, w_down)
    square = gate * gate
    cdf = 0.5 + 0.5 * jnp.tanh(gate * (GELU_C + GELU_C * GELU_A * square))
    act = gate * cdf
    slope = cdf + act * (1.0 - cdf) * (2.0 * GELU_C + 6.0 * GELU_C * GELU_A * square)
    hidden = (act * up).astype(bf16)
    grad_gate = (back_hidden * up * slope).astype(bf16)
    grad_up = (back_hidden * act).astype(bf16)
    normed_t, grad_t = normed.T, grad.T
    for at, (left, right) in enumerate(((normed_t, grad_gate), (normed_t, grad_up), (grad_t, hidden))):
        lanes = slice(at * ff, (at + 1) * ff)
        part = mm(left, right)

        @pl.when(first)
        def _():
            acc[0, :, lanes] = part

        @pl.when(jnp.logical_not(first))
        def _():
            acc[0, :, lanes] += part

    back = mm(grad_gate, w_gate, NT) + mm(grad_up, w_up, NT)
    return back, mm(w_down, hidden, NT)


def feed_own_kernel(
    table, n_src, rows, out_table, n_out, units, s_ref, x_ref, a_ref, b_ref, cot_ref, gain_ref, *refs
):
    sources = refs[:n_src]
    normed_ref, grad_ref, back_ref, mlp_ref, mid_ref, stat_ref = refs[n_src : n_src + 6]
    targets = refs[n_src + 6 : n_src + 6 + n_out]
    buf, acc, stat, sem = refs[n_src + 6 + n_out :]
    i = pl.program_id(0)
    copies = block_copies(table, sources, buf, s_ref[WIDE], rows, sem)

    @pl.when(i == 0)
    def _():
        start_all(copies)
        stat[...] = jnp.zeros_like(stat)

    attn, middle, scale = mid_norm(x_ref, a_ref, b_ref)
    tile, half_rows = x_ref.shape[0], x_ref.shape[0] * pl.num_programs(0)
    live = live_rows(s_ref, s_ref[X_HALF] * half_rows + i * tile, tile, units)
    stat[...] += jnp.sum(jnp.where(live, attn * attn, 0.0), axis=0, keepdims=True)
    normed = (middle * scale * gain_ref[...]).astype(bf16)
    grad = jnp.where(live, cot_ref[...].astype(f32), 0.0).astype(bf16)
    normed_ref[...] = normed
    grad_ref[...] = grad
    store_quarters(s_ref[NARROW], middle.T, mid_ref, None)

    @pl.when(i == 0)
    def _():
        wait_all(copies)

    back_ref[...], mlp_ref[...] = feed_half(normed, grad, buf, acc, i == 0)

    @pl.when(i == pl.num_programs(0) - 1)
    def _():
        stat_ref[...] = jnp.full(stat_ref.shape, jnp.sum(stat[...]))
        store_blocks(out_table, acc, targets, s_ref[WIDE], rows)


def feed_other_kernel(table, n_src, rows, out_table, n_out, s_ref, normed_ref, grad_ref, before_ref, mlp_ref, *refs):
    sources = refs[:n_src]
    back_ref, keep_ref, send_ref = refs[n_src : n_src + 3]
    targets = refs[n_src + 3 : n_src + 3 + n_out]
    buf, acc, sem = refs[n_src + 3 + n_out :]
    i = pl.program_id(0)

    @pl.when(i == 0)
    def _():
        load_blocks(table, sources, buf, s_ref[WIDE], rows, sem)

    back, out = feed_half(normed_ref[...], grad_ref[...], buf, acc, i == 0)
    back_ref[...] = (before_ref[...] + back).astype(bf16)
    store_quarters(s_ref[NARROW], mlp_ref[...] + out, keep_ref, send_ref)

    @pl.when(i == pl.num_programs(0) - 1)
    def _():
        store_blocks(out_table, acc, targets, s_ref[WIDE], rows)


def feed_forward(scalars, inputs, weights, rows, out, own, tile=512):
    table, sources = weights
    out_table, out_leads = out
    n, d = inputs[1].shape
    width = sources[0].shape[-1]
    steps = n // tile
    own_spec = pl.BlockSpec((tile, d), lambda i, s: (s[X_HALF] * steps + i, 0))
    row_spec = pl.BlockSpec((tile, d), lambda i, s: (i, 0))
    full_spec = pl.BlockSpec((d, tile), lambda i, s: (0, i))
    half_spec = pl.BlockSpec((d // 2, tile), lambda i, s: (0, i))
    block_specs = [once((lead, rows, width)) for lead in out_leads]
    block_shapes = tuple(jax.ShapeDtypeStruct((lead, rows, width), bf16) for lead in out_leads)
    scratch = [pltpu.VMEM((1, d, width), bf16), pltpu.VMEM((1, d, width), f32)]
    counts = (table, len(sources), rows, out_table, len(out_leads))
    if own:
        kernel = functools.partial(feed_own_kernel, *counts, 2 * n // UNIT)
        in_specs = [own_spec, row_spec, row_spec, own_spec, once((1, d))]
        out_shape = (
            jax.ShapeDtypeStruct((n, d), bf16),
            jax.ShapeDtypeStruct((n, d), bf16),
            jax.ShapeDtypeStruct((n, d), f32),
            jax.ShapeDtypeStruct((d, n), f32),
            jax.ShapeDtypeStruct((d // 2, n), f32),
            jax.ShapeDtypeStruct((1, LANES), f32),
        )
        out_specs = [row_spec, row_spec, row_spec, full_spec, half_spec, once((1, LANES))]
        scratch.append(pltpu.VMEM((1, d), f32))
    else:
        kernel = functools.partial(feed_other_kernel, *counts)
        in_specs = [row_spec, row_spec, row_spec, full_spec]
        out_shape = (
            jax.ShapeDtypeStruct((n, d), bf16),
            jax.ShapeDtypeStruct((d // 2, n), bf16),
            jax.ShapeDtypeStruct((d // 2, n), bf16),
        )
        out_specs = [row_spec, half_spec, half_spec]
    return pl.pallas_call(
        kernel,
        out_shape=out_shape + block_shapes,
        grid_spec=pltpu.PrefetchScalarGridSpec(
            num_scalar_prefetch=1,
            grid=(steps,),
            in_specs=in_specs + any_specs(sources),
            out_specs=out_specs + block_specs,
            scratch_shapes=scratch + [pltpu.SemaphoreType.DMA((len(table),))],
        ),
        compiler_params=params(FEED_VMEM),
        cost_estimate=cost(2 * n * d * width * 3, 10 * n * d, n * width // 3),
        name="feed_forward",
    )(scalars, *inputs, *sources)


def mid_kernel(
    tables, counts, rows, units, s_ref, x_ref, a_ref, b_ref, g_ref, h_ref, cot_ref, gain_ref, o0_ref, o1_ref, *refs
):
    sources = [refs[: counts[0]], refs[counts[0] : sum(counts)]]
    gm_ref, do0_ref, do1_ref, dwo_ref, gain_out, buf, total, sem = refs[sum(counts) :]
    i = pl.program_id(0)

    @pl.when(i == 0)
    def _():
        for at in range(2):
            load_blocks(
                tables[at], sources[at], buf.at[pl.ds(at, 1)], s_ref[WIDE], rows, sem.at[at], buf.shape[2]
            )
        total[...] = jnp.zeros_like(total)

    _, middle, scale = mid_norm(x_ref, a_ref, b_ref)
    hat = middle * scale
    back = g_ref[...].astype(f32) + h_ref[...].astype(f32)
    tile, half_rows = x_ref.shape[0], x_ref.shape[0] * pl.num_programs(0)
    live = live_rows(s_ref, s_ref[X_HALF] * half_rows + i * tile, tile, units)
    cot = jnp.where(live, cot_ref[...].astype(f32), 0.0)
    total[...] += jnp.sum(back * hat, axis=0, keepdims=True)
    scaled = back * gain_ref[...]
    mean = jnp.mean(scaled * hat, axis=1, keepdims=True)
    grad_mid = cot + scale * (scaled - hat * mean)
    grad = grad_mid.astype(bf16)
    grad_t = grad_mid.T
    gm_ref[...] = grad_t
    grad_t = grad_t.astype(bf16)
    for at, (o_ref, do_ref) in enumerate(((o0_ref, do0_ref), (o1_ref, do1_ref))):
        do_ref[...] = mm(grad, buf[at]).astype(bf16)
        part = mm(grad_t, o_ref[...])

        @pl.when(i == 0)
        def _():
            dwo_ref[at] = part

        @pl.when(i > 0)
        def _():
            dwo_ref[at] += part

    @pl.when(i == pl.num_programs(0) - 1)
    def _():
        gain_out[...] = total[...]


def mid_backward(scalars, patches, a, b, g, h, cot, gain, o, own, other, rows, tile=512):
    n, d = a.shape
    lanes = o[0].shape[1]
    steps = n // tile
    own_spec = pl.BlockSpec((tile, d), lambda i, s: (s[X_HALF] * steps + i, 0))
    row_spec = pl.BlockSpec((tile, d), lambda i, s: (i, 0))
    head_spec = pl.BlockSpec((tile, lanes), lambda i, s: (i, 0))
    return pl.pallas_call(
        functools.partial(
            mid_kernel, (own[0], other[0]), (len(own[1]), len(other[1])), rows, 2 * n // UNIT
        ),
        out_shape=(
            jax.ShapeDtypeStruct((d, n), f32),
            jax.ShapeDtypeStruct((n, lanes), bf16),
            jax.ShapeDtypeStruct((n, lanes), bf16),
            jax.ShapeDtypeStruct((2, d, lanes), f32),
            jax.ShapeDtypeStruct((1, d), f32),
        ),
        grid_spec=pltpu.PrefetchScalarGridSpec(
            num_scalar_prefetch=1,
            grid=(steps,),
            in_specs=[own_spec, row_spec, row_spec, row_spec, row_spec, own_spec]
            + [once((1, d)), head_spec, head_spec]
            + any_specs(own[1])
            + any_specs(other[1]),
            out_specs=[
                pl.BlockSpec((d, tile), lambda i, s: (0, i)),
                head_spec,
                head_spec,
                once((2, d, lanes)),
                once((1, d)),
            ],
            scratch_shapes=[
                pltpu.VMEM((2, d, lanes), bf16),
                pltpu.VMEM((1, d), f32),
                pltpu.SemaphoreType.DMA((2, len(own[0]))),
            ],
        ),
        compiler_params=params(MID_VMEM),
        cost_estimate=cost(8 * n * d * lanes, 16 * n * d),
        name="mid_backward",
    )(scalars, patches, a, b, g, h, cot, gain, *o, *own[1], *other[1])


def head_back_kernel(
    table, n_out, rows, share, chunk, s_ref, q_ref, k_ref, v_ref, do_ref, o_ref, aux_ref, dwo_ref, normed_ref, *refs
):
    dq_out, dk_out, dv_out = refs[:3]
    targets = refs[3 : 3 + n_out]
    normed, dq_buf, dk_buf, dv_buf, pack, sem = refs[3 + n_out :]
    heads = head_list(share)
    lane, first, second = lane_halves()
    in_first = lane < HEAD_DIM
    n, n_q = dk_buf.shape[0], dq_buf.shape[0]
    units = n // UNIT
    load = pltpu.make_async_copy(normed_ref, normed, sem.at[0])
    load.start()
    minus = [
        -((lane >= 64) & (lane < 67)).astype(f32).astype(bf16),
        -(lane < 3).astype(f32).astype(bf16),
    ]
    masks = [key_mask(s_ref, u, lane, units).astype(bf16) for u in range(units)]
    for pair in range(q_ref.shape[1] // LANES):
        members = [side for p, side in heads if p == pair]
        lanes = slice(pair * LANES, (pair + 1) * LANES)
        q, aux, do = q_ref[:, lanes], aux_ref[:, lanes], do_ref[:, lanes]
        product = do.astype(f32) * o_ref[:, lanes].astype(f32)
        features = jnp.zeros(q.shape, f32)
        for side in members:
            inside = ~in_first if side else in_first
            row_sum = jnp.sum(jnp.where(inside, product, 0.0), axis=1, keepdims=True)
            for j, value in enumerate(split3(row_sum)):
                features = jnp.where(lane == (j if side else 64 + j), value, features)
        features = features.astype(bf16)
        sides = [(second, first) if side else (first, second) for side in members]
        q_own = [q * own for own, _ in sides]
        do_own = [do * own for own, _ in sides]
        queries = [part + aux * rest for part, (_, rest) in zip(q_own, sides)]
        grads = [part + features * rest for part, (_, rest) in zip(do_own, sides)]
        q_own, do_own = jnp.concatenate(q_own, axis=0), jnp.concatenate(do_own, axis=0)
        dq = None
        for c in range(0, n, chunk):
            k, v = k_ref[c : c + chunk, lanes], v_ref[c : c + chunk, lanes]
            mask = masks[c // UNIT]
            probs, backs, k_own = [], [], []
            for j, side in enumerate(members):
                own, rest = sides[j]
                k_own.append(k * own)
                p = jnp.exp(mm(k_own[j] + mask * rest, queries[j], NT))
                backs.append((p * mm(v * own + minus[side], grads[j], NT)).astype(bf16))
                probs.append(p.astype(bf16))
            part = mm(jnp.concatenate(k_own, axis=0).T, jnp.concatenate(backs, axis=0))
            dq = part if dq is None else dq + part
            dv_buf[c : c + chunk, lanes] = mm(jnp.concatenate(probs, axis=1), do_own).astype(bf16)
            dk_buf[c : c + chunk, lanes] = mm(jnp.concatenate(backs, axis=1), q_own).astype(bf16)
        dq_buf[:, lanes] = dq.T.astype(bf16)
    copies = start_all(
        [
            pltpu.make_async_copy(source, to, sem.at[1 + at])
            for at, (source, to) in enumerate(((dq_buf, dq_out), (dk_buf, dk_out), (dv_buf, dv_out)))
        ]
    )
    load.wait()
    pack[0, :, 0:share] = dwo_ref[0, :, 0:share]
    mine = normed[block_rows(s_ref[X_HALF], n_q, UNIT), :]
    pack[0, :, share : 2 * share] = mm(mine, dq_buf[...], TN)[:, 0:share]
    both = mm(normed[...], jnp.concatenate([dk_buf[...], dv_buf[...]], axis=1), TN)
    pack[0, :, 2 * share : 3 * share] = both[:, 0:share]
    pack[0, :, 3 * share : 4 * share] = both[:, dk_buf.shape[1] : dk_buf.shape[1] + share]
    store_blocks(table, pack, targets, s_ref[WIDE], rows)
    wait_all(copies)


def head_backward(scalars, q, k, v, do, o, aux, dwo, which, normed, out, rows, share, chunk=512):
    n, d = normed.shape
    n_q, lanes = q.shape
    out_table, out_leads = out
    shapes = [(n_q, lanes), (n, lanes), (n, lanes)]
    blocks = [(lead, rows, 4 * share) for lead in out_leads]
    q_spec, k_spec = once((n_q, lanes)), once((n, lanes))
    any_spec = pl.BlockSpec(memory_space=pl.ANY)
    return pl.pallas_call(
        functools.partial(head_back_kernel, out_table, len(blocks), rows, share, chunk),
        out_shape=tuple(jax.ShapeDtypeStruct(shape, bf16) for shape in shapes + blocks),
        grid_spec=pltpu.PrefetchScalarGridSpec(
            num_scalar_prefetch=1,
            grid=(1,),
            in_specs=[q_spec, k_spec, k_spec, q_spec, q_spec, q_spec]
            + [
                pl.BlockSpec((1, d, lanes), lambda i, s: (which, 0, 0), pipeline_mode=pl.Buffered(1)),
                any_spec,
            ],
            out_specs=[any_spec] * 3 + [once(block) for block in blocks],
            scratch_shapes=[pltpu.VMEM((n, d), bf16)]
            + [pltpu.VMEM(shape, bf16) for shape in shapes]
            + [pltpu.VMEM((1, d, 4 * share), f32), pltpu.SemaphoreType.DMA((4,))],
        ),
        compiler_params=params(BACK_VMEM),
        cost_estimate=cost(20 * n * n * share, 8 * n * d, n * n * share // 128),
        name="head_backward",
    )(scalars, q, k, v, do, o, aux, dwo, normed)


def last_kernel(tables, counts, rows, share, s_ref, x_ref, gain_ref, gm_ref, *refs):
    grads = refs[:6]
    refs = refs[6:]
    sources = [refs[: counts[0]], refs[counts[0] : sum(counts)]]
    keep_ref, send_ref, gain_out, buf, weights, total, gain, sem = refs[sum(counts) :]
    i = pl.program_id(0)
    half = pl.num_programs(0) // 2
    d = x_ref.shape[1]

    @pl.when(i == 0)
    def _():
        for at in range(2):
            load_blocks(tables[at], sources[at], buf.at[pl.ds(at, 1)], s_ref[WIDE], rows, sem.at[at])
        for at in range(2):
            for j in range(3):
                weights[3 * at + j] = padded(
                    buf[at, :, (j + 1) * share : (j + 2) * share], weights.shape[2]
                )
        total[...] = jnp.zeros_like(total)
        gain[...] = jnp.broadcast_to(gain_ref[...], (LANES, d)).T[:, :1]

    mine = i // half == s_ref[X_HALF]
    x = x_ref[...].T.astype(f32)
    scale = lax.rsqrt(jnp.mean(x * x, axis=0, keepdims=True) + epsilon)
    hat = x * scale
    back = None
    for at in range(2):
        for j in range(3):
            value = grads[3 * at + j][...]
            if j == 0:
                value = jnp.where(mine, value.astype(f32), 0.0).astype(bf16)
            part = mm(weights[3 * at + j], value, NT)
            back = part if back is None else back + part
    total[...] += jnp.sum(back * hat, axis=1, keepdims=True)
    scaled = back * gain[...]
    mean = jnp.mean(scaled * hat, axis=0, keepdims=True)
    grad = scale * (scaled - hat * mean) + jnp.where(mine, 0.5, 0.0) * gm_ref[...]
    store_quarters(s_ref[NARROW], grad, keep_ref, send_ref)

    @pl.when(i == pl.num_programs(0) - 1)
    def _():
        gain_out[...] = jnp.broadcast_to(total[...], (d, LANES)).T[:1, :]


def last_backward(scalars, patches, gain, gm_t, grads, own, other, rows, share, tile=512):
    n, d = patches.shape
    width = own[1][0].shape[-1]
    lanes = grads[0].shape[1]
    steps = n // tile
    half = steps // 2
    key_spec = pl.BlockSpec((tile, lanes), lambda i, s: (i, 0))
    own_spec = pl.BlockSpec((tile, lanes), lambda i, s: (own_tile(i, s, half), 0))
    half_spec = pl.BlockSpec((d // 2, tile), lambda i, s: (0, i))
    return pl.pallas_call(
        functools.partial(last_kernel, (own[0], other[0]), (len(own[1]), len(other[1])), rows, share),
        out_shape=(
            jax.ShapeDtypeStruct((d // 2, n), bf16),
            jax.ShapeDtypeStruct((d // 2, n), bf16),
            jax.ShapeDtypeStruct((1, d), f32),
        ),
        grid_spec=pltpu.PrefetchScalarGridSpec(
            num_scalar_prefetch=1,
            grid=(steps,),
            in_specs=[
                pl.BlockSpec((tile, d), lambda i, s: (i, 0)),
                once((1, d)),
                pl.BlockSpec((d, tile), lambda i, s: (0, own_tile(i, s, half))),
            ]
            + [own_spec, key_spec, key_spec] * 2
            + any_specs(own[1])
            + any_specs(other[1]),
            out_specs=[half_spec, half_spec, once((1, d))],
            scratch_shapes=[
                pltpu.VMEM((2, d, width), bf16),
                pltpu.VMEM((6, d, lanes), bf16),
                pltpu.VMEM((d, 1), f32),
                pltpu.VMEM((d, 1), f32),
                pltpu.SemaphoreType.DMA((2, len(own[0]))),
            ],
        ),
        compiler_params=params(LAST_VMEM),
        cost_estimate=cost(2 * n * d * lanes * 5, 10 * n * d),
        name="last_backward",
    )(scalars, patches, gain, gm_t, *grads, *own[1], *other[1])


def swap_core(value):
    return lax.ppermute(value, "narrow", [(i, i ^ 1) for i in range(4)])


def swap_x(value):
    return lax.ppermute(value, "narrow", [(i, i ^ 2) for i in range(4)])


def swap_wide(value, offset):
    n = lax.axis_size("wide")
    return lax.ppermute(value, "wide", [(i, i ^ offset) for i in range(n)])


def after(value, *others):
    return lax.optimization_barrier((value,) + others)[0]


def small_slice():
    return lax.axis_size("wide") == 8


def along_z(first, second, half, flip):
    return [(first, 0, half, flip)] + [(second, z - 1, half, 2 * z + flip) for z in (1, 2, 3)]


OWN_TABLE = along_z(0, 1, 0, 0) + along_z(2, 3, 0, 1)
OTHER_TABLE = along_z(0, 1, 0, 0) + along_z(2, 3, 0, 1)
CORNER = ((2, 0, 1), (3, 0, 3), (3, 1, 5), (4, 0, 7))
FF_TABLE = along_z(0, 1, 0, 0) + [(src, lead, 0, offset) for src, lead, offset in CORNER]
FLAT_TABLE = [(0, r, 0, r) for r in range(8)]
COLUMN_TABLE = [(0, z, 0, 2 * z) for z in range(4)] + [(1, z, 0, 2 * z + 1) for z in range(4)]
ACROSS_TABLE = (
    [(0, z, 0, 2 * z) for z in range(4)]
    + [(1, z, 0, 2 * z + 1) for z in range(2)]
    + [(2, z, 0, 2 * z + 5) for z in range(2)]
)
WHOLE_TABLE = [(0, 0, 0, 0)]


def gather_whole(shard):
    full = lax.all_gather(shard, "wide", axis=0, tiled=True)[None]
    return full, swap_x(full)


def total(*terms):
    return functools.reduce(jnp.add, [t.astype(f32) for t in terms])


def sum_all(value):
    if not small_slice():
        return lax.psum(value, ("wide", "narrow"))
    value = value + swap_core(value)
    value = value + swap_x(value)
    for offset in (1, 2, 4):
        value = value + swap_wide(value, offset)
    return value


def reduce_whole(part):
    return lax.psum_scatter(part, "wide", scatter_dimension=0, tiled=True).astype(f32)


def body(
    patches,
    norm_gain_attn,
    norm_gain_mlp,
    w_query,
    w_key,
    w_value,
    w_out,
    w_gate,
    w_up,
    w_down,
    cotangent,
    item_slots,
    valid_counts,
):
    rows, d = patches.shape
    share = w_query.shape[1]
    ff = w_gate.shape[1]
    half_rows = rows // 2
    quarter = d // 4
    small = small_slice()
    narrow = lax.axis_index("narrow")
    wide = lax.axis_index("wide")
    x_half = narrow // 2
    scalars = jnp.concatenate(
        [jnp.stack([x_half, wide if small else 0 * wide, narrow]), item_slots, valid_counts]
    ).astype(jnp.int32)
    gain_in, gain_mid = norm_gain_attn[None, :], norm_gain_mlp[None, :]

    def own_units(counts):
        units = half_rows // UNIT
        mine = lax.dynamic_slice_in_dim(counts, x_half * units, units)
        return (mine[:, None] + jnp.zeros((1, UNIT), jnp.int32)).reshape(1, half_rows)

    position = x_half * half_rows + jnp.arange(half_rows, dtype=jnp.int32)[None, :]
    live_own = (position & (own_units(item_slots) - 1)) < own_units(valid_counts)
    live_count = 0.5 * jnp.sum(live_own.astype(f32))

    head_shard = jnp.concatenate([w_out.T, w_query, w_key, w_value], axis=1)[None]
    ff_shard = jnp.concatenate([w_gate, w_up, w_down.T], axis=1)[None]
    if small:
        block = head_shard.shape[1]
        first = [swap_wide(head_shard, 2 * z) for z in (1, 2, 3)]
        first += [swap_wide(head_shard, 1), swap_x(head_shard)]
        ff_early = after(ff_shard, head_shard)
        first += [swap_wide(ff_early, 1), swap_x(ff_early)]
        z1, z2, z4, y0, x0, ff_y0, ff_x0 = lax.optimization_barrier(first)
        z3 = jnp.concatenate([z1, z2, z4])
        y3, x3 = swap_wide(z3, 1), swap_x(z3)
        own = (OWN_TABLE, [head_shard, z3, y0, y3])
        other = (OTHER_TABLE, [x0, x3, swap_wide(x0, 1), swap_x(y3)])
        ff_late = after(ff_shard, z3)
        ff_z = [swap_wide(ff_late, 2 * z) for z in (1, 2, 3)]
        early = (y3,)
        own_out = (COLUMN_TABLE, (4, 4))
        other_out = (FLAT_TABLE, (8,))
        across_out = (ACROSS_TABLE, (4, 2, 2))
    else:
        block = d
        own, other = [(WHOLE_TABLE, [full]) for full in gather_whole(head_shard[0])]
        ff_own_weights, ff_other_weights = [(WHOLE_TABLE, [full]) for full in gather_whole(ff_shard[0])]
        own_out = other_out = across_out = (WHOLE_TABLE, (1,))
        early = ()

    values = after(patches, scalars, gain_in, gain_mid, live_own, live_count, *early)
    normed, q0, k0, v0, o0, aux0 = head_forward(scalars, values, gain_in, [own], block, share, True)
    normed = after(normed, o0)
    if small:
        *ff_z, normed = lax.optimization_barrier((*ff_z, normed))
        ff_z3 = jnp.concatenate(ff_z)
        ff_z3, normed = lax.optimization_barrier((ff_z3, normed))
        ff_y3, ff_x3 = swap_wide(ff_z3, 1), swap_x(ff_z3)
        ff_own_weights = (OWN_TABLE, [ff_shard, ff_z3, ff_y0, ff_y3])
    q1, k1, v1, o1, aux1, attn_part = head_forward(
        scalars, normed, gain_in, [other, own], block, share, False, before=o0
    )
    if small:
        ff_y3, ff_x3, ff_x0, attn_part = lax.optimization_barrier((ff_y3, ff_x3, ff_x0, attn_part))
        ff_own_weights[1][3] = ff_y3
        corner = [swap_wide(ff_x0, 1), swap_x(ff_y3[:2]), swap_wide(ff_x3[2:], 1)]
        ff_other_weights = (FF_TABLE, [ff_x0, ff_x3, *corner])
    attn_other = swap_core(attn_part)
    normed_mid, grad_mlp, back_own, mlp_own, mid_keep, attn_square, *ff_own_grads = feed_forward(
        scalars, (values, attn_part, attn_other, cotangent, gain_mid), ff_own_weights, block, own_out, True
    )
    back_part, mlp_keep, mlp_send, *ff_other_grads = feed_forward(
        scalars, (normed_mid, grad_mlp, back_own, mlp_own), ff_other_weights, block, across_out, False
    )
    back_other = swap_core(back_part)
    if small:
        column, to_y = ff_own_grads
        to_x, corner_x, corner_y = ff_other_grads
        got_x, got_y = swap_x(corner_x), swap_wide(corner_y, 1)
    gm_t, do0, do1, dwo, gain_mid_sum = mid_backward(
        scalars, values, attn_part, attn_other, back_part, back_other, cotangent, gain_mid,
        (o0, o1), own, other, block,
    )
    if small:
        got_x, got_y, to_x, to_y = lax.optimization_barrier((got_x, got_y, to_x, to_y, do1))[:4]
        to_y = jnp.concatenate([total(to_y[:2], got_x).astype(bf16), to_y[2:]])
        to_x = jnp.concatenate([to_x[:2], total(to_x[2:], got_y).astype(bf16)])
        got_y, got_x = swap_wide(to_y, 1), swap_x(to_x)
        do1 = after(do1, to_y, to_x)
    *grads1, head1 = head_backward(
        scalars, q1, k1, v1, do1, o1, aux1, dwo, 1, normed, other_out, block, share
    )

    mlp = total(mlp_keep, after(swap_core(after(mlp_send, do1)), head1))
    layer = jnp.where(live_own, mid_keep + mlp, 0.0)
    layer16 = layer.astype(bf16)
    mlp_square = jnp.sum(jnp.where(live_own, mlp * mlp, 0.0))
    layer_square = jnp.sum(layer * layer)
    stats = jnp.stack([mlp_square, layer_square, live_count])[None]
    stats = jnp.concatenate(
        [0.5 * gain_mid_sum, 0.5 * attn_square[:, :1], jnp.pad(stats, ((0, 0), (0, LANES - 4)))],
        axis=1,
    )

    head1_other = swap_x(head1)
    layer_mine, layer_sent = layer16[:quarter], layer16[quarter:]
    layer_got = swap_x(layer_sent)
    do0 = after(do0, head1, stats, layer_mine, layer_sent)
    if small:
        column = total(column, after(got_y, head1), after(got_x, head1))
        sent = [column[z].astype(bf16) for z in (1, 2, 3)]
        do0 = after(do0, *sent)
        back = [swap_wide(sent[z - 1], 2 * z) for z in (1, 2, 3)]
    *grads0, head0, head0_y = head_backward(
        scalars, q0, k0, v0, do0, o0, aux0, dwo, 0, normed, own_out, block, share
    ) + (() if small else (None,))
    dq0, head1_other = lax.optimization_barrier((grads0[0], head1_other))
    if small:
        head_y = total(head0_y, head1_other[1::2]).astype(bf16)
        dq0 = after(dq0, head_y)
        head_y = swap_wide(head_y, 1)
    grad_keep, grad_send, gain_in_sum = last_backward(
        scalars, values, gain_in, gm_t, [dq0, *grads0[1:], *grads1], own, other, block, share
    )

    if small:
        grad_keep, grad_send, gain_in_sum, head_y = lax.optimization_barrier(
            (grad_keep, grad_send, gain_in_sum, head_y)
        )
    grad_got = swap_core(grad_send)
    grad_sent = total(grad_keep[quarter:], grad_got[quarter:]).astype(bf16)
    if small:
        head_column = total(head0, head1_other[::2], head_y)
        head_sent = [head_column[z].astype(bf16) for z in (1, 2, 3)]
        gain_in_sum, layer_got, *back = lax.optimization_barrier(
            (gain_in_sum, layer_got, *back, grad_sent, *head_sent)
        )[: 2 + len(back)]
        head_own = total(
            head_column[0], *[swap_wide(head_sent[z - 1], 2 * z) for z in (1, 2, 3)]
        )
        ff_own = total(column[0], *back)
    else:
        both = total(ff_own_grads[0][0], swap_x(ff_other_grads[0][0])).astype(bf16)
        ff_own = reduce_whole(both)
        head_own = reduce_whole(total(head0[0], head1_other[0]).astype(bf16))
    output = jnp.where(
        x_half == 0,
        jnp.concatenate([layer_mine, layer_got], axis=1),
        jnp.concatenate([layer_got, layer_mine], axis=1),
    )
    grad_patches = total(grad_keep[:quarter], grad_got[:quarter], swap_x(grad_sent))

    sums = sum_all(jnp.concatenate([gain_in_sum, stats], axis=1))[0]
    total_in, total_mid, totals = sums[:d], sums[d : 2 * d], sums[2 * d : 2 * d + 4]
    rms_values = jnp.sqrt(totals[:3] / (totals[3] * d))
    return (
        output.T,
        grad_patches.T,
        total_in,
        total_mid,
        head_own[:, share : 2 * share],
        head_own[:, 2 * share : 3 * share],
        head_own[:, 3 * share :],
        head_own[:, :share].T,
        ff_own[:, :ff],
        ff_own[:, ff : 2 * ff],
        ff_own[:, 2 * ff :].T,
        rms_values,
    )


def solution(mesh):
    return jax.shard_map(
        body,
        mesh=mesh,
        in_specs=(
            P("wide", None),
            P(),
            P(),
            P("wide", "narrow"),
            P("wide", "narrow"),
            P("wide", "narrow"),
            P("narrow", "wide"),
            P("wide", "narrow"),
            P("wide", "narrow"),
            P("narrow", "wide"),
            P("wide", None),
            P("wide"),
            P("wide"),
        ),
        out_specs=(
            P("wide", "narrow"),
            P("wide", "narrow"),
            P(),
            P(),
            P("wide", "narrow"),
            P("wide", "narrow"),
            P("wide", "narrow"),
            P("narrow", "wide"),
            P("wide", "narrow"),
            P("wide", "narrow"),
            P("narrow", "wide"),
            P(),
        ),
        check_vma=False,
    )
```

time: 1220 us -> 288 us (0.24)
  waiting for transfers between devices: 544 us -> 52.9 us
  blocking collectives: 294 us -> 0 us
  matrix products: 200 us -> 0 us
  Pallas kernels: 0 us -> 129 us
  other arithmetic: 101 us -> 20.1 us
  starting transfers between devices: 0.54 us -> 52 us
  local copies, waits for them, and re-layouts: 53.2 us -> 26.1 us
    reduce_scatter x10 -> x0, waiting for transfers between devices: 514 us -> none  [the longest x1 68 us: body(): lax.psum_scatter(grad_w_down, 'wide', scatter_dimension=1, tiled=True)]
    all_gather x7 -> x0, blocking collectives: 234 us -> none  [the longest x1 35.1 us: body(): lax.all_gather(w_out, 'wide', axis=1, tiled=True)]
    dot_general x48 -> x0, matrix products: 196 us -> none  [the longest x8 34 us: block_scores(): jnp.einsum('qhe,khe->hqk', query_heads, key_heads, preferred_element_type...]
    pallas_call x0 -> x8, Pallas kernels: none -> 129 us  [the longest x2 40.1 us: head_backward(): pl.pallas_call(functools.partial(head_back_kernel, out_table, len(blocks)...]
    psum x4 -> x0, blocking collectives: 59.4 us -> none  [the longest x1 40.1 us: body(): lax.psum((placed_in, placed_mid, stat_terms), ('wide', 'narrow'))]
    ppermute x0 -> x42, waiting for transfers between devices: none -> 52.9 us  [the longest x25 42.5 us: swap_wide(): return lax.ppermute(value, 'wide', [(i, i ^ offset) for i in range(n)])]
    ppermute x0 -> x42, starting transfers between devices: none -> 52 us  [the longest x25 38 us: swap_wide(): return lax.ppermute(value, 'wide', [(i, i ^ offset) for i in range(n)])]
    reduce_sum x9 -> x2, other arithmetic: 41.6 us -> 2.01 us  [the longest x1 1.33 us: body(): mlp_square = jnp.sum(jnp.where(live_own, mlp * mlp, 0.0))]
  transfers between devices with their start and end apart: 13 -> 42, of which waited for: 11 -> 19; matrix products, arithmetic and copies ran while one was open for 16% -> 8% of each run, Pallas kernels for 0% -> 41%
where the time goes in v2:
time: 288 us; the launch traced here: 283 us
  Pallas kernels  129 us (45%)
  waiting for transfers between devices  52.9 us (18%)
  starting transfers between devices  52 us (18%)
  local copies, waits for them, and re-layouts  26.1 us (9%)
  other arithmetic  20.1 us (7%)
  between operations  3.1 us (1%)
    ppermute x25, waiting for transfers between devices, swap_wide(): return lax.ppermute(value, 'wide', [(i, i ^ offset) for i in range(n)])  42.5 us
    pallas_call x2, Pallas kernels, head_backward(): pl.pallas_call(functools.partial(head_back_kernel, out_table, len(blocks)...  40.1 us
    ppermute x25, starting transfers between devices, swap_wide(): return lax.ppermute(value, 'wide', [(i, i ^ offset) for i in range(n)])  38 us
    pallas_call x2, Pallas kernels, head_forward(): pl.pallas_call(functools.partial(head_kernel, tables, counts, rows, share...  32.9 us
    pallas_call x2, Pallas kernels, feed_forward(): pl.pallas_call(kernel, out_shape=out_shape + block_shapes, grid_spec=pltp...  31 us
    unnamed x150, local copies, waits for them, and re-layouts  20.3 us
    pallas_call x1, Pallas kernels, last_backward(): pl.pallas_call(functools.partial(last_kernel, (own[0], other[0]), (len(ow...  16.6 us
    ppermute x12, starting transfers between devices, swap_x(): return lax.ppermute(value, 'narrow', [(i, i ^ 2) for i in range(4)])  13.8 us
  transfers between devices with their start and end apart: 42, of which 19 were waited for; matrix products, arithmetic and copies ran while one was open for 8% of the time, Pallas kernels for 41%

profile of v2, /device:TPU:0, one launch (start us, length us, event | category | flops | bytes accessed | tf_op | source)
XLA Modules:
  0.0 282.9 jit_solution(1354949875595021466)
XLA Ops:
  2.6 3.0 %collective-permute-start.4 = (bf16[1,96,768]{2,1,0:T(8,128)(2,1)S(1)}, bf16[1,96,768]{2,1,0:T(8,128)(2,1)S(1)}, u32[]{:S(2)}, u32[]{:S(2)}) collective-permute-start(bf16[1,96,768]{2,1,0:T(8,128)(2,1)S(1)} %maximum_bitcast_fusion.1.refs_0_.refs_5_.refs_6_), channel_id=1, source_target_pairs={{0,2},{1,3},{2,0},{3,1},{4,6},{5,7},{6,4},{7,5},{8,10},{9,11},{10,... | collective-permute-start | bytes 442376 | tf_op jit(solution)/shard_map/ppermute | solution.py:760
  5.6 1.5 collective-permute-start.3
  7.1 1.0 maximum_bitcast_fusion.refs_0_
  8.7 4.1 %collective-permute-start.2 = (bf16[1,96,768]{2,1,0:T(8,128)(2,1)S(1)}, bf16[1,96,768]{2,1,0:T(8,128)(2,1)S(1)}, u32[]{:S(2)}, u32[]{:S(2)}) collective-permute-start(bf16[1,96,768]{2,1,0:T(8,128)(2,1)S(1)} %maximum_bitcast_fusion.1.refs_0_.refs_5_.refs_6_), channel_id=1, source_target_pairs={{0,24},{4,28},{8,16},{12,20},{16,8},{20,12},{24,0},{28,4},{1,25},{... | collective-permute-start | bytes 442376 | tf_op jit(solution)/shard_map/ppermute | solution.py:765
  12.8 1.0 collective-permute-start
  13.8 3.7 %collective-permute-done.2 = bf16[1,96,768]{2,1,0:T(8,128)(2,1)S(1)} collective-permute-done((bf16[1,96,768]{2,1,0:T(8,128)(2,1)S(1)}, bf16[1,96,768]{2,1,0:T(8,128)(2,1)S(1)}, u32[]{:S(2)}, u32[]{:S(2)}) %collective-permute-start.2) | collective-permute-done | bytes 147488 | tf_op jit(solution)/shard_map/ppermute | solution.py:765
  17.6 6.6 %collective-permute-done.1 = bf16[1,96,768]{2,1,0:T(8,128)(2,1)S(1)} collective-permute-done((bf16[1,96,768]{2,1,0:T(8,128)(2,1)S(1)}, bf16[1,96,768]{2,1,0:T(8,128)(2,1)S(1)}, u32[]{:S(2)}, u32[]{:S(2)}) %collective-permute-start.1) | collective-permute-done | bytes 147488 | tf_op jit(solution)/shard_map/ppermute | solution.py:765
  24.2 1.6 collective-permute-start.7
  27.4 2.6 collective-permute-start.10
  30.1 1.8 collective-permute-start.8
  31.8 1.5 collective-permute-start.13
  33.3 2.2 collective-permute-done.7.refs_3_.refs_8_.refs_9_
  35.5 1.5 collective-permute-start.15
  37.0 1.9 copy-done
  38.9 16.5 %head_forward.2 = (bf16[2048,768]{1,0:T(8,128)(2,1)S(1)}, bf16[1024,256]{1,0:T(8,128)(2,1)S(1)}, bf16[2048,256]{1,0:T(8,128)(2,1)S(1)}, bf16[2048,256]{1,0:T(8,1...) custom-call(s32[11]{0:T(128)S(1)} %concatenate.32.s_ref, bf16[2048,768]{1,0:T(8,128)(2,1)S(1)} %copy-done, ...), custom_call_target="tpu_custom_call" | custom-call | flops 8053063680 | bytes 12582912 | tf_op jit(solution)/shard_map/head_forward/pallas_call | solution.py:300
  56.4 1.6 collective-permute-start.14
  59.2 4.0 %collective-permute-done.14.refs_3_.refs_6_.refs_12_ = bf16[1,96,768]{2,1,0:T(8,128)(2,1)S(1)} collective-permute-done((bf16[1,96,768]{2,1,0:T(8,128)(2,1)S(1)}, bf16[1,96,768]{2,1,0:T(8,128)(2,1)S(1)}, u32[]{:S(2)}, u32[]{:S(2)}) %collective-permute-start.14) | collective-permute-done | bytes 147488 | tf_op jit(solution)/shard_map/ppermute | solution.py:765
  63.2 16.4 %head_forward.3 = (bf16[1024,256]{1,0:T(8,128)(2,1)S(1)}, bf16[2048,256]{1,0:T(8,128)(2,1)S(1)}, bf16[2048,256]{1,0:T(8,128)(2,1)S(1)}, bf16[1024,256]{1,0:T(8,1...) custom-call(s32[11]{0:T(128)S(1)} %concatenate.32.s_ref, ...), custom_call_target="tpu_custom_call" | custom-call | flops 8053063680 | bytes 12582912 | tf_op jit(solution)/shard_map/head_forward/pallas_call | solution.py:300
  79.7 1.0 copy-done.44
  80.7 1.0 copy-done.46
  83.4 1.6 collective-permute-start.19
  86.8 17.6 %feed_forward.2 = (bf16[1024,768]{1,0:T(8,128)(2,1)S(1)}, bf16[1024,768]{1,0:T(8,128)(2,1)S(1)}, f32[1024,768]{1,0:T(8,128)}, f32[768,1024]{1,0:T(8,128)}, f32[3...) custom-call(s32[11]{0:T(128)S(1)} %concatenate.32.s_ref, ...), custom_call_target="tpu_custom_call" | custom-call | flops 7247757312 | bytes 7864320 | tf_op jit(solution)/shard_map/feed_forward/pallas_call | solution.py:464
  105.1 1.2 copy-done.26
  106.3 1.0 copy-done.38
  107.2 1.9 copy-done.41
  109.1 13.4 %feed_forward.3 = (bf16[1024,768]{1,0:T(8,128)(2,1)S(1)}, bf16[384,1024]{1,0:T(8,128)(2,1)S(1)}, bf16[384,1024]{1,0:T(8,128)(2,1)S(1)}, bf16[4,96,1536]{2,1,0:T(...) custom-call(s32[11]{0:T(128)S(1)} %concatenate.32.s_ref, ...), custom_call_target="tpu_custom_call" | custom-call | flops 7247757312 | bytes 7864320 | tf_op jit(solution)/shard_map/feed_forward/pallas_call | solution.py:464
  125.3 1.5 collective-permute-start.22
  127.8 1.0 copy-done.11
  128.8 1.0 copy-done.14
  130.7 8.2 %mid_backward.1 = (f32[768,1024]{1,0:T(8,128)}, bf16[1024,256]{1,0:T(8,128)(2,1)S(1)}, bf16[1024,256]{1,0:T(8,128)(2,1)S(1)}, f32[2,768,256]{2,1,0:T(8,128)S(1)}, f32[1,768]{1,0:T(1,128)S(1)}) custom-call(s32[11]{0:T(128)S(1)} %concatenate.32.s_ref, bf16[2048,768]{1,0:T(8,128)(2,1)} %x_ref.3, bf16[1024,768]{1,0:T(8,128)(2,1)S(1)} %get-tuple-element.118.a_ref, ...), custom_call_target="tpu_custom_call" | custom-call | flops 1610612736 | bytes 12582912 | tf_op jit(solution)/shard_map/mid_backward/pallas_call | solution.py:533
  138.9 1.2 collective-permute-done.21
  141.3 1.3 pad_maximum_fusion
  142.6 1.5 collective-permute-start.24
  144.1 1.1 collective-permute-start.25
  145.3 20.2 %head_backward.2 = (bf16[1024,256]{1,0:T(8,128)(2,1)S(1)}, bf16[2048,256]{1,0:T(8,128)(2,1)S(1)}, bf16[2048,256]{1,0:T(8,128)(2,1)S(1)}, bf16[8,96,768]{2,1,0:T(8,128)(2,1)S(1)}) custom-call(s32[11]{0:T(128)S(1)} %concatenate.32.s_ref, bf16[1024,256]{1,0:T(8,128)(2,1)S(1)} %copy-done.53, bf16[2048,256]{1,0:T(8,128)(2,1)S(1)} %copy-done.45, ...), custom_call_target="tpu_custom_call" | custom-call | flops 16106127360 | bytes 12582912 | tf_op jit(solution)/shard_map/head_backward/pallas_call | solution.py:647
  165.6 1.0 collective-permute-start.26
  166.5 1.3 select_reduce_fusion
  168.8 1.3 collective-permute-done.24
  170.1 2.9 %collective-permute-done.25 = bf16[4,96,1536]{2,1,0:T(8,128)(2,1)S(1)} collective-permute-done((bf16[4,96,1536]{2,1,0:T(8,128)(2,1)S(1)}, bf16[4,96,1536]{2,1,0:T(8,128)(2,1)S(1)}, u32[]{:S(2)}, u32[]{:S(2)}) %collective-permute-start.25) | collective-permute-done | bytes 1179680 | tf_op jit(solution)/shard_map/ppermute | solution.py:760
  173.0 2.0 fusion.12
  176.6 19.9 %head_backward.3 = (bf16[1024,256]{1,0:T(8,128)(2,1)S(1)}, bf16[2048,256]{1,0:T(8,128)(2,1)S(1)}, bf16[2048,256]{1,0:T(8,128)(2,1)S(1)}, bf16[4,96,768]{2,1,0:T(8,128)(2,1)S(1)}, bf16[4,96,768]{2,1,0:T(8,128)(2,1)S(1)}) custom-call(s32[11]{0:T(128)S(1)} %concatenate.32.s_ref, bf16[1024,256]{1,0:T(8,128)(2,1)S(1)} %copy-done.57, ...), custom_call_target="tpu_custom_call" | custom-call | flops 16106127360 | bytes 12582912 | tf_op jit(solution)/shard_map/head_backward/pallas_call | solution.py:647
  198.2 16.6 %last_backward.1 = (bf16[384,2048]{1,0:T(8,128)(2,1)S(1)}, bf16[384,2048]{1,0:T(8,128)(2,1)}, f32[1,768]{1,0:T(1,128)S(1)}) custom-call(s32[11]{0:T(128)S(1)} %concatenate.32.s_ref, bf16[2048,768]{1,0:T(8,128)(2,1)S(1)} %copy-done.1, f32[1,768]{1,0:T(1,128)S(1)} %broadcast_in_dim.35.gain_ref, f32[768,1024]{1,0:T(8,128)} %get-tuple-element.150.gm_ref, ...), custom_call_target="tpu_custom_call" | custom-call | flops 4026531840 | bytes 15728640 | tf_op jit(solution)/shard_map/last_backward/pallas_call | solution.py:722
  215.6 1.2 collective-permute-start.28
  216.8 1.4 maximum_bitcast_fusion.2
  218.2 1.5 collective-permute-start.31
  219.7 2.9 %collective-permute-start.29 = (bf16[96,1536]{1,0:T(8,128)(2,1)S(1)}, bf16[96,1536]{1,0:T(8,128)(2,1)}, u32[]{:S(2)}, u32[]{:S(2)}) collective-permute-start(bf16[96,1536]{1,0:T(8,128)(2,1)S(1)} %get-tuple-element.221), channel_id=1, source_target_pairs={{0,8},{4,12},{8,0},{12,4},{16,24},{20,28},{24,16},{28,20},{1,9},{5... | collective-permute-start | bytes 884744 | tf_op jit(solution)/shard_map/ppermute | solution.py:765
  222.6 2.5 fusion.11
  225.8 1.7 collective-permute-done.28
  227.4 1.4 collective-permute-start.41
  228.9 1.3 collective-permute-done.31
  230.2 10.2 %collective-permute-start.40 = (bf16[96,768]{1,0:T(8,128)(2,1)S(1)}, bf16[96,768]{1,0:T(8,128)(2,1)}, u32[]{:S(2)}, u32[]{:S(2)}) collective-permute-start(bf16[96,768]{1,0:T(8,128)(2,1)S(1)} %get-tuple-element.228), channel_id=1, source_target_pairs={{0,16},{4,20},{8,24},{12,28},{16,0},{20,4},{24,8},{28,12},{1,17},{... | collective-permute-start | bytes 442376 | tf_op jit(solution)/shard_map/ppermute | solution.py:765
  240.5 1.4 add_convert_fusion
  241.9 10.2 %collective-permute-done.30 = bf16[96,1536]{1,0:T(8,128)(2,1)} collective-permute-done((bf16[96,1536]{1,0:T(8,128)(2,1)}, bf16[96,1536]{1,0:T(8,128)(2,1)}, u32[]{:S(2)}, u32[]{:S(2)}) %collective-permute-start.30) | collective-permute-done | bytes 294944 | tf_op jit(solution)/shard_map/ppermute | solution.py:765
  252.2 5.5 %collective-permute-done.40 = bf16[96,768]{1,0:T(8,128)(2,1)} collective-permute-done((bf16[96,768]{1,0:T(8,128)(2,1)S(1)}, bf16[96,768]{1,0:T(8,128)(2,1)}, u32[]{:S(2)}, u32[]{:S(2)}) %collective-permute-start.40) | collective-permute-done | bytes 147488 | tf_op jit(solution)/shard_map/ppermute | solution.py:765
  257.7 1.2 fusion.7
  258.9 1.0 collective-permute-start.35
  261.4 1.1 collective-permute-start.33
  263.4 1.4 fusion.3
  264.8 1.5 collective-permute-done.36
  267.2 2.8 collective-permute-done.37
  270.7 1.2 fusion
  271.9 2.7 collective-permute-done.38
  277.0 2.9 %collective-permute-done.33 = bf16[192,2048]{1,0:T(8,128)(2,1)S(1)} collective-permute-done((bf16[192,2048]{1,0:T(8,128)(2,1)S(1)}, bf16[192,2048]{1,0:T(8,128)(2,1)S(1)}, u32[]{:S(2)}, u32[]{:S(2)}) %collective-permute-start.33) | collective-permute-done | bytes 786464 | tf_op jit(solution)/shard_map/ppermute | solution.py:760
  280.0 2.6 add_bitcast_fusion
  (222 shorter events, 27.1 us)
Async XLA Ops:
  0.6 25.2 %copy-start.67 = (f32[768]{0:T(1024)S(1)}, f32[768]{0:T(1024)}, u32[]{:S(2)}) copy-start(f32[768]{0:T(1024)} %param.14) | copy-start | bytes 9220
  0.7 25.2 %copy-start.68 = (f32[768]{0:T(1024)S(1)}, f32[768]{0:T(1024)}, u32[]{:S(2)}) copy-start(f32[768]{0:T(1024)} %param.15) | copy-start | bytes 9220
  0.7 25.2 %copy-start.70 = (s32[4]{0:T(128)S(1)}, s32[4]{0:T(128)}, u32[]{:S(2)}) copy-start(s32[4]{0:T(128)} %param.25) | copy-start | bytes 52
  0.7 25.3 %copy-start.69 = (s32[4]{0:T(128)S(1)}, s32[4]{0:T(128)}, u32[]{:S(2)}) copy-start(s32[4]{0:T(128)} %param.24) | copy-start | bytes 52
  2.6 10.2 %collective-permute-start.4 = (bf16[1,96,768]{2,1,0:T(8,128)(2,1)S(1)}, bf16[1,96,768]{2,1,0:T(8,128)(2,1)S(1)}, u32[]{:S(2)}, u32[]{:S(2)}) collective-permute-start(bf16[1,96,768]{2,1,0:T(8,128)(2,1)S(1)} %maximum_bitcast_fusion.1.refs_0_.refs_5_.refs_6_), channel_id=1, source_target_pairs={{0,2},{1,3},{2,0},{3,1},{4,6},{5,7},{6,4},{7,5},{8,10},{9,11},{10,... | collective-permute-start | bytes 442376 | tf_op jit(solution)/shard_map/ppermute | solution.py:760
  5.6 7.3 %collective-permute-start.3 = (bf16[1,96,768]{2,1,0:T(8,128)(2,1)S(1)}, bf16[1,96,768]{2,1,0:T(8,128)(2,1)S(1)}, u32[]{:S(2)}, u32[]{:S(2)}) collective-permute-start(bf16[1,96,768]{2,1,0:T(8,128)(2,1)S(1)} %maximum_bitcast_fusion.1.refs_0_.refs_5_.refs_6_), channel_id=1, source_target_pairs={{0,4},{4,0},{8,12},{12,8},{16,20},{20,16},{24,28},{28,24},{1,5},{5... | collective-permute-start | bytes 442376 | tf_op jit(solution)/shard_map/ppermute | solution.py:765
  8.1 16.1 %collective-permute-start.6 = (bf16[1,96,1536]{2,1,0:T(8,128)(2,1)S(1)}, bf16[1,96,1536]{2,1,0:T(8,128)(2,1)S(1)}, u32[]{:S(2)}, u32[]{:S(2)}) collective-permute-start(bf16[1,96,1536]{2,1,0:T(8,128)(2,1)S(1)} %maximum_bitcast_fusion.refs_0_), channel_id=1, source_target_pairs={{0,2},{1,3},{2,0},{3,1},{4,6},{5,7},{6,4},{7,5},{8,10},{9,11},{10,... | collective-permute-start | bytes 884744 | tf_op jit(solution)/shard_map/ppermute | solution.py:760
  8.7 15.5 %collective-permute-start.5 = (bf16[1,96,1536]{2,1,0:T(8,128)(2,1)S(1)}, bf16[1,96,1536]{2,1,0:T(8,128)(2,1)S(1)}, u32[]{:S(2)}, u32[]{:S(2)}) collective-permute-start(bf16[1,96,1536]{2,1,0:T(8,128)(2,1)S(1)} %maximum_bitcast_fusion.refs_0_), channel_id=1, source_target_pairs={{0,4},{4,0},{8,12},{12,8},{16,20},{20,16},{24,28},{28,24},{1,5},{5... | collective-permute-start | bytes 884744 | tf_op jit(solution)/shard_map/ppermute | solution.py:765
  8.7 8.8 %collective-permute-start.2 = (bf16[1,96,768]{2,1,0:T(8,128)(2,1)S(1)}, bf16[1,96,768]{2,1,0:T(8,128)(2,1)S(1)}, u32[]{:S(2)}, u32[]{:S(2)}) collective-permute-start(bf16[1,96,768]{2,1,0:T(8,128)(2,1)S(1)} %maximum_bitcast_fusion.1.refs_0_.refs_5_.refs_6_), channel_id=1, source_target_pairs={{0,24},{4,28},{8,16},{12,20},{16,8},{20,12},{24,0},{28,4},{1,25},{... | collective-permute-start | bytes 442376 | tf_op jit(solution)/shard_map/ppermute | solution.py:765
  12.8 50.4 %copy-start.16 = (bf16[1,96,768]{2,1,0:T(8,128)(2,1)}, bf16[1,96,768]{2,1,0:T(8,128)(2,1)S(1)}, u32[]{:S(2)}) copy-start(bf16[1,96,768]{2,1,0:T(8,128)(2,1)S(1)} %collective-permute-done.4.refs_1_.refs_4_.refs_10_) | copy-start | bytes 442372
  12.8 11.4 %collective-permute-start.1 = (bf16[1,96,768]{2,1,0:T(8,128)(2,1)S(1)}, bf16[1,96,768]{2,1,0:T(8,128)(2,1)S(1)}, u32[]{:S(2)}, u32[]{:S(2)}) collective-permute-start(bf16[1,96,768]{2,1,0:T(8,128)(2,1)S(1)} %maximum_bitcast_fusion.1.refs_0_.refs_5_.refs_6_), channel_id=1, source_target_pairs={{0,16},{4,20},{8,24},{12,28},{16,0},{20,4},{24,8},{28,12},{1,17},{... | collective-permute-start | bytes 442376 | tf_op jit(solution)/shard_map/ppermute | solution.py:765
  12.8 50.4 %copy-start.19 = (bf16[1,96,768]{2,1,0:T(8,128)(2,1)}, bf16[1,96,768]{2,1,0:T(8,128)(2,1)S(1)}, u32[]{:S(2)}) copy-start(bf16[1,96,768]{2,1,0:T(8,128)(2,1)S(1)} %collective-permute-done.3.refs_2_.refs_7_.refs_8_) | copy-start | bytes 442372
  12.8 11.3 %collective-permute-start = (bf16[1,96,768]{2,1,0:T(8,128)(2,1)S(1)}, bf16[1,96,768]{2,1,0:T(8,128)(2,1)S(1)}, u32[]{:S(2)}, u32[]{:S(2)}) collective-permute-start(bf16[1,96,768]{2,1,0:T(8,128)(2,1)S(1)} %maximum_bitcast_fusion.1.refs_0_.refs_5_.refs_6_), channel_id=1, source_target_pairs={{0,8},{4,12},{8,0},{12,4},{16,24},{20,28},{24,16},{28,20},{1,9},{5... | collective-permute-start | bytes 442376 | tf_op jit(solution)/shard_map/ppermute | solution.py:765
  24.2 60.8 %copy-start.35 = (bf16[1,96,1536]{2,1,0:T(8,128)(2,1)}, bf16[1,96,1536]{2,1,0:T(8,128)(2,1)S(1)}, u32[]{:S(2)}) copy-start(bf16[1,96,1536]{2,1,0:T(8,128)(2,1)S(1)} %collective-permute-done.6.refs_0_) | copy-start | bytes 884740
  24.2 11.2 %collective-permute-start.7 = (bf16[3,96,768]{2,1,0:T(8,128)(2,1)S(1)}, bf16[3,96,768]{2,1,0:T(8,128)(2,1)S(1)}, u32[]{:S(2)}, u32[]{:S(2)}) collective-permute-start(bf16[3,96,768]{2,1,0:T(8,128)(2,1)S(1)} %constant_dynamic-update-slice_fusion.refs_1_.refs_6_.refs_7_), channel_id=1, source_target_pairs={{0,4},{4,0},{8,12},{12,8},{16,20},{20,16},{24,28},{28,24},{1,5},{5... | collective-permute-start | bytes 1327112 | tf_op jit(solution)/shard_map/ppermute | solution.py:765
  27.4 28.9 %collective-permute-start.10 = (bf16[1,96,1536]{2,1,0:T(8,128)(2,1)S(1)}, bf16[1,96,1536]{2,1,0:T(8,128)(2,1)S(1)}, u32[]{:S(2)}, u32[]{:S(2)}) collective-permute-start(bf16[1,96,1536]{2,1,0:T(8,128)(2,1)S(1)} %maximum_bitcast_fusion.refs_0_), channel_id=1, source_target_pairs={{0,24},{4,28},{8,16},{12,20},{16,8},{20,12},{24,0},{28,4},{1,25},{... | collective-permute-start | bytes 884744 | tf_op jit(solution)/shard_map/ppermute | solution.py:765
  30.1 27.9 %collective-permute-start.9 = (bf16[1,96,1536]{2,1,0:T(8,128)(2,1)S(1)}, bf16[1,96,1536]{2,1,0:T(8,128)(2,1)S(1)}, u32[]{:S(2)}, u32[]{:S(2)}) collective-permute-start(bf16[1,96,1536]{2,1,0:T(8,128)(2,1)S(1)} %maximum_bitcast_fusion.refs_0_), channel_id=1, source_target_pairs={{0,16},{4,20},{8,24},{12,28},{16,0},{20,4},{24,8},{28,12},{1,17},{... | collective-permute-start | bytes 884744 | tf_op jit(solution)/shard_map/ppermute | solution.py:765
  30.1 27.9 %collective-permute-start.8 = (bf16[1,96,1536]{2,1,0:T(8,128)(2,1)S(1)}, bf16[1,96,1536]{2,1,0:T(8,128)(2,1)S(1)}, u32[]{:S(2)}, u32[]{:S(2)}) collective-permute-start(bf16[1,96,1536]{2,1,0:T(8,128)(2,1)S(1)} %maximum_bitcast_fusion.refs_0_), channel_id=1, source_target_pairs={{0,8},{4,12},{8,0},{12,4},{16,24},{20,28},{24,16},{28,20},{1,9},{5... | collective-permute-start | bytes 884744 | tf_op jit(solution)/shard_map/ppermute | solution.py:765
  31.8 31.4 %collective-permute-start.13 = (bf16[3,96,768]{2,1,0:T(8,128)(2,1)S(1)}, bf16[3,96,768]{2,1,0:T(8,128)(2,1)S(1)}, u32[]{:S(2)}, u32[]{:S(2)}) collective-permute-start(bf16[3,96,768]{2,1,0:T(8,128)(2,1)S(1)} %constant_dynamic-update-slice_fusion.refs_1_.refs_6_.refs_7_), channel_id=1, source_target_pairs={{0,2},{1,3},{2,0},{3,1},{4,6},{5,7},{6,4},{7,5},{8,10},{9,11},{10,... | collective-permute-start | bytes 1327112 | tf_op jit(solution)/shard_map/ppermute | solution.py:760
  35.5 27.7 %collective-permute-start.15 = (bf16[3,96,768]{2,1,0:T(8,128)(2,1)S(1)}, bf16[3,96,768]{2,1,0:T(8,128)(2,1)S(1)}, u32[]{:S(2)}, u32[]{:S(2)}) collective-permute-start(bf16[3,96,768]{2,1,0:T(8,128)(2,1)S(1)} %collective-permute-done.7.refs_3_.refs_8_.refs_9_), channel_id=1, source_target_pairs={{0,2},{1,3},{2,0},{3,1},{4,6},{5,7},{6,4},{7,5},{8,10},{9,11},{10,... | collective-permute-start | bytes 1327112 | tf_op jit(solution)/shard_map/ppermute | solution.py:760
  56.3 23.3 %copy-start.4 = (bf16[1024,256]{1,0:T(8,128)(2,1)}, bf16[1024,256]{1,0:T(8,128)(2,1)S(1)}, u32[]{:S(2)}) copy-start(bf16[1024,256]{1,0:T(8,128)(2,1)S(1)} %get-tuple-element.107.refs_0_.o0_ref.o_ref) | copy-start | bytes 1572868
  56.3 23.3 %copy-start.42 = (bf16[2048,768]{1,0:T(8,128)(2,1)}, bf16[2048,768]{1,0:T(8,128)(2,1)S(1)}, u32[]{:S(2)}) copy-start(bf16[2048,768]{1,0:T(8,128)(2,1)S(1)} %get-tuple-element.115.x_ref.normed_ref) | copy-start | bytes 9437188
  56.3 23.3 %copy-start.48 = (bf16[2048,256]{1,0:T(8,128)(2,1)}, bf16[2048,256]{1,0:T(8,128)(2,1)S(1)}, u32[]{:S(2)}) copy-start(bf16[2048,256]{1,0:T(8,128)(2,1)S(1)} %get-tuple-element.152.k_ref) | copy-start | bytes 3145732
  56.3 23.3 %copy-start.56 = (bf16[1024,256]{1,0:T(8,128)(2,1)}, bf16[1024,256]{1,0:T(8,128)(2,1)S(1)}, u32[]{:S(2)}) copy-start(bf16[1024,256]{1,0:T(8,128)(2,1)S(1)} %get-tuple-element.151.q_ref) | copy-start | bytes 1572868
  56.3 23.3 %copy-start.58 = (bf16[1024,256]{1,0:T(8,128)(2,1)}, bf16[1024,256]{1,0:T(8,128)(2,1)S(1)}, u32[]{:S(2)}) copy-start(bf16[1024,256]{1,0:T(8,128)(2,1)S(1)} %get-tuple-element.160.aux_ref) | copy-start | bytes 1572868
  56.4 6.8 %collective-permute-start.14 = (bf16[1,96,768]{2,1,0:T(8,128)(2,1)S(1)}, bf16[1,96,768]{2,1,0:T(8,128)(2,1)S(1)}, u32[]{:S(2)}, u32[]{:S(2)}) collective-permute-start(bf16[1,96,768]{2,1,0:T(8,128)(2,1)S(1)} %collective-permute-done.4.refs_1_.refs_4_.refs_10_), channel_id=1, source_target_pairs={{0,4},{4,0},{8,12},{12,8},{16,20},{20,16},{24,28},{28,24},{1,5},{5... | collective-permute-start | bytes 442376 | tf_op jit(solution)/shard_map/ppermute | solution.py:765
  58.1 25.2 %collective-permute-start.12 = (bf16[3,96,1536]{2,1,0:T(8,128)(2,1)S(1)}, bf16[3,96,1536]{2,1,0:T(8,128)(2,1)S(1)}, u32[]{:S(2)}, u32[]{:S(2)}) collective-permute-start(bf16[3,96,1536]{2,1,0:T(8,128)(2,1)S(1)} %pad_maximum_fusion.2.refs_1_), channel_id=1, source_target_pairs={{0,2},{1,3},{2,0},{3,1},{4,6},{5,7},{6,4},{7,5},{8,10},{9,11},{10,... | collective-permute-start | bytes 2654216 | tf_op jit(solution)/shard_map/ppermute | solution.py:760
  58.6 24.6 %collective-permute-start.11 = (bf16[3,96,1536]{2,1,0:T(8,128)(2,1)S(1)}, bf16[3,96,1536]{2,1,0:T(8,128)(2,1)S(1)}, u32[]{:S(2)}, u32[]{:S(2)}) collective-permute-start(bf16[3,96,1536]{2,1,0:T(8,128)(2,1)S(1)} %pad_maximum_fusion.2.refs_1_), channel_id=1, source_target_pairs={{0,4},{4,0},{8,12},{12,8},{16,20},{20,16},{24,28},{28,24},{1,5},{5... | collective-permute-start | bytes 2654216 | tf_op jit(solution)/shard_map/ppermute | solution.py:765
  83.3 3.5 %collective-permute-start.16 = (bf16[1024,768]{1,0:T(8,128)(2,1)S(1)}, bf16[1024,768]{1,0:T(8,128)(2,1)S(1)}, u32[]{:S(2)}, u32[]{:S(2)}) collective-permute-start(bf16[1024,768]{1,0:T(8,128)(2,1)S(1)} %get-tuple-element.118.a_ref), channel_id=1, source_target_pairs={{0,1},{1,0},{2,3},{3,2},{4,5},{5,4},{6,7},{7,6},{8,9},{9,8},{10,11... | collective-permute-start | bytes 4718600 | tf_op jit(solution)/shard_map/ppermute | solution.py:756
  83.4 20.9 %collective-permute-start.19 = (bf16[1,96,1536]{2,1,0:T(8,128)(2,1)S(1)}, bf16[1,96,1536]{2,1,0:T(8,128)(2,1)S(1)}, u32[]{:S(2)}, u32[]{:S(2)}) collective-permute-start(bf16[1,96,1536]{2,1,0:T(8,128)(2,1)S(1)} %slice.121), channel_id=1, source_target_pairs={{0,4},{4,0},{8,12},{12,8},{16,20},{20,16},{24,28},{28,24},{1,5},{5... | collective-permute-start | bytes 884744 | tf_op jit(solution)/shard_map/ppermute | solution.py:765
  85.0 19.3 %collective-permute-start.17 = (bf16[1,96,1536]{2,1,0:T(8,128)(2,1)S(1)}, bf16[1,96,1536]{2,1,0:T(8,128)(2,1)S(1)}, u32[]{:S(2)}, u32[]{:S(2)}) collective-permute-start(bf16[1,96,1536]{2,1,0:T(8,128)(2,1)S(1)} %collective-permute-done.6.refs_0_), channel_id=1, source_target_pairs={{0,4},{4,0},{8,12},{12,8},{16,20},{20,16},{24,28},{28,24},{1,5},{5... | collective-permute-start | bytes 884744 | tf_op jit(solution)/shard_map/ppermute | solution.py:765
  85.5 19.6 %copy-start.36 = (bf16[1,96,1536]{2,1,0:T(8,128)(2,1)S(1)}, bf16[1,96,1536]{2,1,0:T(8,128)(2,1)}, u32[]{:S(2)}) copy-start(bf16[1,96,1536]{2,1,0:T(8,128)(2,1)} %copy-done.35) | copy-start | bytes 884740
  85.5 19.5 %collective-permute-start.18 = (bf16[2,96,1536]{2,1,0:T(8,128)(2,1)S(1)}, bf16[2,96,1536]{2,1,0:T(8,128)(2,1)S(1)}, u32[]{:S(2)}, u32[]{:S(2)}) collective-permute-start(bf16[2,96,1536]{2,1,0:T(8,128)(2,1)S(1)} %slice.120), channel_id=1, source_target_pairs={{0,2},{1,3},{2,0},{3,1},{4,6},{5,7},{6,4},{7,5},{8,10},{9,11},{10,... | collective-permute-start | bytes 1769480 | tf_op jit(solution)/shard_map/ppermute | solution.py:760
  109.1 18.6 %copy-start.5 = (bf16[1024,256]{1,0:T(8,128)(2,1)S(1)}, bf16[1024,256]{1,0:T(8,128)(2,1)}, u32[]{:S(2)}) copy-start(bf16[1024,256]{1,0:T(8,128)(2,1)} %copy-done.4) | copy-start | bytes 1572868
  109.1 18.6 %copy-start.8 = (bf16[1024,256]{1,0:T(8,128)(2,1)S(1)}, bf16[1024,256]{1,0:T(8,128)(2,1)}, u32[]{:S(2)}) copy-start(bf16[1024,256]{1,0:T(8,128)(2,1)} %copy-done.7) | copy-start | bytes 1572868
  109.1 18.6 %copy-start.17 = (bf16[1,96,768]{2,1,0:T(8,128)(2,1)S(1)}, bf16[1,96,768]{2,1,0:T(8,128)(2,1)}, u32[]{:S(2)}) copy-start(bf16[1,96,768]{2,1,0:T(8,128)(2,1)} %copy-done.16) | copy-start | bytes 442372
  109.1 18.6 %copy-start.20 = (bf16[1,96,768]{2,1,0:T(8,128)(2,1)S(1)}, bf16[1,96,768]{2,1,0:T(8,128)(2,1)}, u32[]{:S(2)}) copy-start(bf16[1,96,768]{2,1,0:T(8,128)(2,1)} %copy-done.19) | copy-start | bytes 442372
  124.3 3.4 %collective-permute-start.20 = (bf16[1024,768]{1,0:T(8,128)(2,1)S(1)}, bf16[1024,768]{1,0:T(8,128)(2,1)S(1)}, u32[]{:S(2)}, u32[]{:S(2)}) collective-permute-start(bf16[1024,768]{1,0:T(8,128)(2,1)S(1)} %get-tuple-element.130.g_ref), channel_id=1, source_target_pairs={{0,1},{1,0},{2,3},{3,2},{4,5},{5,4},{6,7},{7,6},{8,9},{9,8},{10,11... | collective-permute-start | bytes 4718600 | tf_op jit(solution)/shard_map/ppermute | solution.py:756
  124.6 15.6 %collective-permute-start.21 = (bf16[2,96,1536]{2,1,0:T(8,128)(2,1)S(1)}, bf16[2,96,1536]{2,1,0:T(8,128)(2,1)S(1)}, u32[]{:S(2)}, u32[]{:S(2)}) collective-permute-start(bf16[2,96,1536]{2,1,0:T(8,128)(2,1)S(1)} %get-tuple-element.133), channel_id=1, source_target_pairs={{0,2},{1,3},{2,0},{3,1},{4,6},{5,7},{6,4},{7,5},{8,10},{9,11},{10,... | collective-permute-start | bytes 1769480 | tf_op jit(solution)/shard_map/ppermute | solution.py:760
  125.3 15.5 %collective-permute-start.22 = (bf16[2,96,1536]{2,1,0:T(8,128)(2,1)S(1)}, bf16[2,96,1536]{2,1,0:T(8,128)(2,1)S(1)}, u32[]{:S(2)}, u32[]{:S(2)}) collective-permute-start(bf16[2,96,1536]{2,1,0:T(8,128)(2,1)S(1)} %get-tuple-element.134), channel_id=1, source_target_pairs={{0,4},{4,0},{8,12},{12,8},{16,20},{20,16},{24,28},{28,24},{1,5},{5... | collective-permute-start | bytes 1769480 | tf_op jit(solution)/shard_map/ppermute | solution.py:765
  142.6 27.6 %collective-permute-start.24 = (bf16[4,96,1536]{2,1,0:T(8,128)(2,1)}, bf16[4,96,1536]{2,1,0:T(8,128)(2,1)S(1)}, u32[]{:S(2)}, u32[]{:S(2)}) collective-permute-start(bf16[4,96,1536]{2,1,0:T(8,128)(2,1)} %get-tuple-element.234), channel_id=1, source_target_pairs={{0,4},{4,0},{8,12},{12,8},{16,20},{20,16},{24,28},{28,24},{1,5},{5... | collective-permute-start | bytes 3538952 | tf_op jit(solution)/shard_map/ppermute | solution.py:765
  144.1 28.9 %collective-permute-start.25 = (bf16[4,96,1536]{2,1,0:T(8,128)(2,1)S(1)}, bf16[4,96,1536]{2,1,0:T(8,128)(2,1)S(1)}, u32[]{:S(2)}, u32[]{:S(2)}) collective-permute-start(bf16[4,96,1536]{2,1,0:T(8,128)(2,1)S(1)} %get-tuple-element.235), channel_id=1, source_target_pairs={{0,2},{1,3},{2,0},{3,1},{4,6},{5,7},{6,4},{7,5},{8,10},{9,11},{10,... | collective-permute-start | bytes 3538952 | tf_op jit(solution)/shard_map/ppermute | solution.py:760
  145.2 21.3 %collective-permute-start.23 = (bf16[384,1024]{1,0:T(8,128)(2,1)S(1)}, bf16[384,1024]{1,0:T(8,128)(2,1)S(1)}, u32[]{:S(2)}, u32[]{:S(2)}) collective-permute-start(bf16[384,1024]{1,0:T(8,128)(2,1)S(1)} %copy-done.30), channel_id=1, source_target_pairs={{0,1},{1,0},{2,3},{3,2},{4,5},{5,4},{6,7},{7,6},{8,9},{9,8},{10,11... | collective-permute-start | bytes 2359304 | tf_op jit(solution)/shard_map/ppermute | solution.py:756
  145.3 21.2 %copy-start.3 = (bf16[384,1024]{1,0:T(8,128)(2,1)S(1)}, bf16[384,1024]{1,0:T(8,128)(2,1)}, u32[]{:S(2)}) copy-start(bf16[384,1024]{1,0:T(8,128)(2,1)} %copy-done.2) | copy-start | bytes 2359300
  165.6 31.0 %collective-permute-start.26 = (bf16[8,96,768]{2,1,0:T(8,128)(2,1)S(1)}, bf16[8,96,768]{2,1,0:T(8,128)(2,1)S(1)}, u32[]{:S(2)}, u32[]{:S(2)}) collective-permute-start(bf16[8,96,768]{2,1,0:T(8,128)(2,1)S(1)} %get-tuple-element.148), channel_id=1, source_target_pairs={{0,2},{1,3},{2,0},{3,1},{4,6},{5,7},{6,4},{7,5},{8,10},{9,11},{10,... | collective-permute-start | bytes 3538952 | tf_op jit(solution)/shard_map/ppermute | solution.py:760
  176.6 20.7 %copy-start.1 = (bf16[2048,768]{1,0:T(8,128)(2,1)S(1)}, bf16[2048,768]{1,0:T(8,128)(2,1)}, u32[]{:S(2)}) copy-start(bf16[2048,768]{1,0:T(8,128)(2,1)} %x_ref.3) | copy-start | bytes 9437188
  176.6 20.7 %copy-start.40 = (bf16[2048,256]{1,0:T(8,128)(2,1)S(1)}, bf16[2048,256]{1,0:T(8,128)(2,1)}, u32[]{:S(2)}) copy-start(bf16[2048,256]{1,0:T(8,128)(2,1)} %copy-done.39) | copy-start | bytes 3145732
  196.5 18.2 %copy-start.61 = (bf16[8,96,768]{2,1,0:T(8,128)(2,1)}, bf16[8,96,768]{2,1,0:T(8,128)(2,1)S(1)}, u32[]{:S(2)}) copy-start(bf16[8,96,768]{2,1,0:T(8,128)(2,1)S(1)} %collective-permute-done.26) | copy-start | bytes 3538948
  196.7 18.1 %collective-permute-start.27 = (bf16[4,96,768]{2,1,0:T(8,128)(2,1)S(1)}, bf16[4,96,768]{2,1,0:T(8,128)(2,1)S(1)}, u32[]{:S(2)}, u32[]{:S(2)}) collective-permute-start(bf16[4,96,768]{2,1,0:T(8,128)(2,1)S(1)} %add_convert_fusion.1), channel_id=1, source_target_pairs={{0,4},{4,0},{8,12},{12,8},{16,20},{20,16},{24,28},{28,24},{1,5},{5... | collective-permute-start | bytes 1769480 | tf_op jit(solution)/shard_map/ppermute | solution.py:765
  215.6 24.9 %collective-permute-start.32 = (bf16[384,2048]{1,0:T(8,128)(2,1)}, bf16[384,2048]{1,0:T(8,128)(2,1)}, u32[]{:S(2)}, u32[]{:S(2)}) collective-permute-start(bf16[384,2048]{1,0:T(8,128)(2,1)} %get-tuple-element.176), channel_id=1, source_target_pairs={{0,1},{1,0},{2,3},{3,2},{4,5},{5,4},{6,7},{7,6},{8,9},{9,8},{10,11... | collective-permute-start | bytes 4718600 | tf_op jit(solution)/shard_map/ppermute | solution.py:756
  215.6 11.8 %collective-permute-start.28 = (bf16[192,1024]{1,0:T(8,128)(2,1)}, bf16[192,1024]{1,0:T(8,128)(2,1)S(1)}, u32[]{:S(2)}, u32[]{:S(2)}) collective-permute-start(bf16[192,1024]{1,0:T(8,128)(2,1)} %get-tuple-element.222), channel_id=1, source_target_pairs={{0,2},{1,3},{2,0},{3,1},{4,6},{5,7},{6,4},{7,5},{8,10},{9,11},{10,... | collective-permute-start | bytes 1179656 | tf_op jit(solution)/shard_map/ppermute | solution.py:760
  218.2 12.0 %collective-permute-start.31 = (bf16[96,1536]{1,0:T(8,128)(2,1)}, bf16[96,1536]{1,0:T(8,128)(2,1)S(1)}, u32[]{:S(2)}, u32[]{:S(2)}) collective-permute-start(bf16[96,1536]{1,0:T(8,128)(2,1)} %get-tuple-element.219), channel_id=1, source_target_pairs={{0,24},{4,28},{8,16},{12,20},{16,8},{20,12},{24,0},{28,4},{1,25},{... | collective-permute-start | bytes 884744 | tf_op jit(solution)/shard_map/ppermute | solution.py:765
  219.7 32.4 %collective-permute-start.30 = (bf16[96,1536]{1,0:T(8,128)(2,1)}, bf16[96,1536]{1,0:T(8,128)(2,1)}, u32[]{:S(2)}, u32[]{:S(2)}) collective-permute-start(bf16[96,1536]{1,0:T(8,128)(2,1)} %get-tuple-element.220), channel_id=1, source_target_pairs={{0,16},{4,20},{8,24},{12,28},{16,0},{20,4},{24,8},{28,12},{1,17},{... | collective-permute-start | bytes 884744 | tf_op jit(solution)/shard_map/ppermute | solution.py:765
  219.7 32.4 %collective-permute-start.29 = (bf16[96,1536]{1,0:T(8,128)(2,1)S(1)}, bf16[96,1536]{1,0:T(8,128)(2,1)}, u32[]{:S(2)}, u32[]{:S(2)}) collective-permute-start(bf16[96,1536]{1,0:T(8,128)(2,1)S(1)} %get-tuple-element.221), channel_id=1, source_target_pairs={{0,8},{4,12},{8,0},{12,4},{16,24},{20,28},{24,16},{28,20},{1,9},{5... | collective-permute-start | bytes 884744 | tf_op jit(solution)/shard_map/ppermute | solution.py:765
  227.4 24.7 %collective-permute-start.41 = (bf16[96,768]{1,0:T(8,128)(2,1)}, bf16[96,768]{1,0:T(8,128)(2,1)}, u32[]{:S(2)}, u32[]{:S(2)}) collective-permute-start(bf16[96,768]{1,0:T(8,128)(2,1)} %get-tuple-element.227), channel_id=1, source_target_pairs={{0,24},{4,28},{8,16},{12,20},{16,8},{20,12},{24,0},{28,4},{1,25},{... | collective-permute-start | bytes 442376 | tf_op jit(solution)/shard_map/ppermute | solution.py:765
  230.2 27.5 %collective-permute-start.40 = (bf16[96,768]{1,0:T(8,128)(2,1)S(1)}, bf16[96,768]{1,0:T(8,128)(2,1)}, u32[]{:S(2)}, u32[]{:S(2)}) collective-permute-start(bf16[96,768]{1,0:T(8,128)(2,1)S(1)} %get-tuple-element.228), channel_id=1, source_target_pairs={{0,16},{4,20},{8,24},{12,28},{16,0},{20,4},{24,8},{28,12},{1,17},{... | collective-permute-start | bytes 442376 | tf_op jit(solution)/shard_map/ppermute | solution.py:765
  240.5 17.2 %collective-permute-start.39 = (bf16[96,768]{1,0:T(8,128)(2,1)S(1)}, bf16[96,768]{1,0:T(8,128)(2,1)}, u32[]{:S(2)}, u32[]{:S(2)}) collective-permute-start(bf16[96,768]{1,0:T(8,128)(2,1)S(1)} %get-tuple-element.229), channel_id=1, source_target_pairs={{0,8},{4,12},{8,0},{12,4},{16,24},{20,28},{24,16},{28,20},{1,9},{5... | collective-permute-start | bytes 442376 | tf_op jit(solution)/shard_map/ppermute | solution.py:765
  241.9 21.5 %copy-start.66 = (bf16[96,1536]{1,0:T(8,128)(2,1)S(1)}, bf16[96,1536]{1,0:T(8,128)(2,1)}, u32[]{:S(2)}) copy-start(bf16[96,1536]{1,0:T(8,128)(2,1)} %copy-done.65) | copy-start | bytes 884740
  252.2 6.7 %collective-permute-start.34 = (f32[1,1664]{1,0:T(1,128)S(1)}, f32[1,1664]{1,0:T(1,128)S(1)}, u32[]{:S(2)}, u32[]{:S(2)}) collective-permute-start(f32[1,1664]{1,0:T(1,128)S(1)} %concatenate.41), channel_id=1, source_target_pairs={{0,1},{1,0},{2,3},{3,2},{4,5},{5,4},{6,7},{7,6},{8,9},{9,8},{10,11... | collective-permute-start | bytes 19976 | tf_op jit(solution)/shard_map/ppermute | solution.py:756
  258.9 3.7 %collective-permute-start.35 = (f32[1,1664]{1,0:T(1,128)S(1)}, f32[1,1664]{1,0:T(1,128)S(1)}, u32[]{:S(2)}, u32[]{:S(2)}) collective-permute-start(f32[1,1664]{1,0:T(1,128)S(1)} %add.134), channel_id=1, source_target_pairs={{0,2},{1,3},{2,0},{3,1},{4,6},{5,7},{6,4},{7,5},{8,10},{9,11},{10,... | collective-permute-start | bytes 19976 | tf_op jit(solution)/shard_map/ppermute | solution.py:760
  261.4 18.6 %collective-permute-start.33 = (bf16[192,2048]{1,0:T(8,128)(2,1)S(1)}, bf16[192,2048]{1,0:T(8,128)(2,1)S(1)}, u32[]{:S(2)}, u32[]{:S(2)}) collective-permute-start(bf16[192,2048]{1,0:T(8,128)(2,1)S(1)} %add_convert_fusion), channel_id=1, source_target_pairs={{0,2},{1,3},{2,0},{3,1},{4,6},{5,7},{6,4},{7,5},{8,10},{9,11},{10,... | collective-permute-start | bytes 2359304 | tf_op jit(solution)/shard_map/ppermute | solution.py:760
  262.6 3.7 %collective-permute-start.36 = (f32[1,1664]{1,0:T(1,128)S(1)}, f32[1,1664]{1,0:T(1,128)S(1)}, u32[]{:S(2)}, u32[]{:S(2)}) collective-permute-start(f32[1,1664]{1,0:T(1,128)S(1)} %add.135), channel_id=1, source_target_pairs={{0,4},{4,0},{8,12},{12,8},{16,20},{20,16},{24,28},{28,24},{1,5},{5... | collective-permute-start | bytes 19976 | tf_op jit(solution)/shard_map/ppermute | solution.py:765
  266.3 3.7 %collective-permute-start.37 = (f32[1,1664]{1,0:T(1,128)S(1)}, f32[1,1664]{1,0:T(1,128)S(1)}, u32[]{:S(2)}, u32[]{:S(2)}) collective-permute-start(f32[1,1664]{1,0:T(1,128)S(1)} %add.136), channel_id=1, source_target_pairs={{0,8},{4,12},{8,0},{12,4},{16,24},{20,28},{24,16},{28,20},{1,9},{5... | collective-permute-start | bytes 19976 | tf_op jit(solution)/shard_map/ppermute | solution.py:765
  270.1 4.6 %collective-permute-start.38 = (f32[1,1664]{1,0:T(1,128)S(1)}, f32[1,1664]{1,0:T(1,128)S(1)}, u32[]{:S(2)}, u32[]{:S(2)}) collective-permute-start(f32[1,1664]{1,0:T(1,128)S(1)} %add.137), channel_id=1, source_target_pairs={{0,16},{4,20},{8,24},{12,28},{16,0},{20,4},{24,8},{28,12},{1,17},{... | collective-permute-start | bytes 19976 | tf_op jit(solution)/shard_map/ppermute | solution.py:765
  (49 other events, 176.8 us)

commit v3 on v2

--- a/solution.py
+++ b/solution.py
@@ -116,11 +116,15 @@
 
 
 def any_specs(arrays):
-    return [pl.BlockSpec(memory_space=pl.ANY)] * len(arrays)
+    return [pl.BlockSpec(memory_space=pltpu.HBM)] * len(arrays)
 
 
 def own_tile(i, s, half):
     return jnp.clip(i - s[0] * half, 0, half - 1)
+
+
+def keep_in_hbm(value):
+    return pltpu.with_memory_space_constraint(value, pltpu.HBM)
 
 
 def params(mebibytes):
@@ -270,7 +274,7 @@
     shapes = [q_shape, k_shape, k_shape, q_shape, q_shape]
     if first_shard:
         shapes = [(n, d)] + shapes
-    out_specs = [pl.BlockSpec(memory_space=pl.ANY)] * (len(shapes) - 2) + [once(q_shape)] * 2
+    out_specs = [pl.BlockSpec(memory_space=pltpu.HBM)] * (len(shapes) - 2) + [once(q_shape)] * 2
     scratch = [
         pltpu.VMEM((1, d, width), bf16),
         pltpu.VMEM((3, d, lanes), bf16),
@@ -474,7 +478,7 @@
         compiler_params=params(FEED_VMEM),
         cost_estimate=cost(2 * n * d * width * 3, 10 * n * d, n * width // 3),
         name="feed_forward",
-    )(scalars, *inputs, *sources)
+    )(scalars, *[keep_in_hbm(x) for x in inputs], *sources)
 
 
 def mid_kernel(
@@ -564,7 +568,7 @@
         compiler_params=params(MID_VMEM),
         cost_estimate=cost(8 * n * d * lanes, 16 * n * d),
         name="mid_backward",
-    )(scalars, patches, a, b, g, h, cot, gain, *o, *own[1], *other[1])
+    )(scalars, *[keep_in_hbm(t) for t in (patches, a, b, g, h, cot)], gain, *o, *own[1], *other[1])
 
 
 def head_back_kernel(
@@ -663,7 +667,7 @@
         compiler_params=params(BACK_VMEM),
         cost_estimate=cost(20 * n * n * share, 8 * n * d, n * n * share // 128),
         name="head_backward",
-    )(scalars, q, k, v, do, o, aux, dwo, normed)
+    )(scalars, *[keep_in_hbm(t) for t in (q, k, v, do, o, aux, dwo)], normed)
 
 
 def last_kernel(tables, counts, rows, share, s_ref, x_ref, gain_ref, gm_ref, *refs):
@@ -783,10 +787,16 @@
 FF_TABLE = along_z(0, 1, 0, 0) + [(src, lead, 0, offset) for src, lead, offset in CORNER]
 FLAT_TABLE = [(0, r, 0, r) for r in range(8)]
 COLUMN_TABLE = [(0, z, 0, 2 * z) for z in range(4)] + [(1, z, 0, 2 * z + 1) for z in range(4)]
-ACROSS_TABLE = (
+FF_COLUMN_TABLE = (
     [(0, z, 0, 2 * z) for z in range(4)]
     + [(1, z, 0, 2 * z + 1) for z in range(2)]
     + [(2, z, 0, 2 * z + 5) for z in range(2)]
+)
+ACROSS_TABLE = (
+    [(0, z, 0, 2 * z) for z in range(2)]
+    + [(1, z, 0, 2 * z + 4) for z in range(2)]
+    + [(2, z, 0, 2 * z + 1) for z in range(2)]
+    + [(3, z, 0, 2 * z + 5) for z in range(2)]
 )
 WHOLE_TABLE = [(0, 0, 0, 0)]
 
@@ -863,19 +873,21 @@
         z1, z2, z4, y0, x0, ff_y0, ff_x0 = lax.optimization_barrier(first)
         z3 = jnp.concatenate([z1, z2, z4])
         y3, x3 = swap_wide(z3, 1), swap_x(z3)
+        corner = swap_wide(x0, 1)
         own = (OWN_TABLE, [head_shard, z3, y0, y3])
-        other = (OTHER_TABLE, [x0, x3, swap_wide(x0, 1), swap_x(y3)])
+        other = (OTHER_TABLE, [x0, x3, corner, swap_x(y3)])
         ff_late = after(ff_shard, z3)
         ff_z = [swap_wide(ff_late, 2 * z) for z in (1, 2, 3)]
-        early = (y3,)
+        early = (y3, corner)
         own_out = (COLUMN_TABLE, (4, 4))
         other_out = (FLAT_TABLE, (8,))
-        across_out = (ACROSS_TABLE, (4, 2, 2))
+        ff_out = (FF_COLUMN_TABLE, (4, 2, 2))
+        across_out = (ACROSS_TABLE, (2, 2, 2, 2))
     else:
         block = d
         own, other = [(WHOLE_TABLE, [full]) for full in gather_whole(head_shard[0])]
         ff_own_weights, ff_other_weights = [(WHOLE_TABLE, [full]) for full in gather_whole(ff_shard[0])]
-        own_out = other_out = across_out = (WHOLE_TABLE, (1,))
+        own_out = other_out = ff_out = across_out = (WHOLE_TABLE, (1,))
         early = ()
 
     values = after(patches, scalars, gain_in, gain_mid, live_own, live_count, *early)
@@ -897,24 +909,25 @@
         ff_other_weights = (FF_TABLE, [ff_x0, ff_x3, *corner])
     attn_other = swap_core(attn_part)
     normed_mid, grad_mlp, back_own, mlp_own, mid_keep, attn_square, *ff_own_grads = feed_forward(
-        scalars, (values, attn_part, attn_other, cotangent, gain_mid), ff_own_weights, block, own_out, True
+        scalars, (values, attn_part, attn_other, cotangent, gain_mid), ff_own_weights, block, ff_out, True
     )
     back_part, mlp_keep, mlp_send, *ff_other_grads = feed_forward(
         scalars, (normed_mid, grad_mlp, back_own, mlp_own), ff_other_weights, block, across_out, False
     )
     back_other = swap_core(back_part)
     if small:
-        column, to_y = ff_own_grads
-        to_x, corner_x, corner_y = ff_other_grads
+        column, to_y, early_y = ff_own_grads
+        early_x, to_x, corner_x, corner_y = ff_other_grads
+        got_early_y = swap_wide(early_y, 1)
         got_x, got_y = swap_x(corner_x), swap_wide(corner_y, 1)
+        got_early_x = swap_x(after(early_x, back_other))
     gm_t, do0, do1, dwo, gain_mid_sum = mid_backward(
         scalars, values, attn_part, attn_other, back_part, back_other, cotangent, gain_mid,
         (o0, o1), own, other, block,
     )
     if small:
         got_x, got_y, to_x, to_y = lax.optimization_barrier((got_x, got_y, to_x, to_y, do1))[:4]
-        to_y = jnp.concatenate([total(to_y[:2], got_x).astype(bf16), to_y[2:]])
-        to_x = jnp.concatenate([to_x[:2], total(to_x[2:], got_y).astype(bf16)])
+        to_y, to_x = total(to_y, got_x).astype(bf16), total(to_x, got_y).astype(bf16)
         got_y, got_x = swap_wide(to_y, 1), swap_x(to_x)
         do1 = after(do1, to_y, to_x)
     *grads1, head1 = head_backward(
@@ -934,10 +947,17 @@
 
     head1_other = swap_x(head1)
     layer_mine, layer_sent = layer16[:quarter], layer16[quarter:]
+    do0, stats, layer_mine, layer_sent = lax.optimization_barrier(
+        (do0, stats, layer_mine, layer_sent, head1)
+    )[:4]
     layer_got = swap_x(layer_sent)
-    do0 = after(do0, head1, stats, layer_mine, layer_sent)
     if small:
-        column = total(column, after(got_y, head1), after(got_x, head1))
+        got_x, got_y, got_early_x, got_early_y = lax.optimization_barrier(
+            (got_x, got_y, got_early_x, got_early_y, head1)
+        )[:4]
+        column = total(
+            column, jnp.concatenate([got_y, got_early_y]), jnp.concatenate([got_early_x, got_x])
+        )
         sent = [column[z].astype(bf16) for z in (1, 2, 3)]
         do0 = after(do0, *sent)
         back = [swap_wide(sent[z - 1], 2 * z) for z in (1, 2, 3)]
@@ -947,27 +967,25 @@
     dq0, head1_other = lax.optimization_barrier((grads0[0], head1_other))
     if small:
         head_y = total(head0_y, head1_other[1::2]).astype(bf16)
-        dq0 = after(dq0, head_y)
+        dq0, head_y, *back = lax.optimization_barrier((dq0, head_y, *back))
         head_y = swap_wide(head_y, 1)
     grad_keep, grad_send, gain_in_sum = last_backward(
         scalars, values, gain_in, gm_t, [dq0, *grads0[1:], *grads1], own, other, block, share
     )
 
     if small:
-        grad_keep, grad_send, gain_in_sum, head_y = lax.optimization_barrier(
-            (grad_keep, grad_send, gain_in_sum, head_y)
+        grad_keep, grad_send, gain_in_sum, head_y, layer_got = lax.optimization_barrier(
+            (grad_keep, grad_send, gain_in_sum, head_y, layer_got)
         )
     grad_got = swap_core(grad_send)
     grad_sent = total(grad_keep[quarter:], grad_got[quarter:]).astype(bf16)
     if small:
         head_column = total(head0, head1_other[::2], head_y)
         head_sent = [head_column[z].astype(bf16) for z in (1, 2, 3)]
-        gain_in_sum, layer_got, *back = lax.optimization_barrier(
-            (gain_in_sum, layer_got, *back, grad_sent, *head_sent)
-        )[: 2 + len(back)]
-        head_own = total(
-            head_column[0], *[swap_wide(head_sent[z - 1], 2 * z) for z in (1, 2, 3)]
-        )
+        gain_in_sum, grad_sent = lax.optimization_barrier(
+            (gain_in_sum, grad_sent, *head_sent)
+        )[:2]
+        head_got = [swap_wide(head_sent[z - 1], 2 * z) for z in (1, 2, 3)]
         ff_own = total(column[0], *back)
     else:
         both = total(ff_own_grads[0][0], swap_x(ff_other_grads[0][0])).astype(bf16)
@@ -980,7 +998,11 @@
     )
     grad_patches = total(grad_keep[:quarter], grad_got[:quarter], swap_x(grad_sent))
 
-    sums = sum_all(jnp.concatenate([gain_in_sum, stats], axis=1))[0]
+    sums = sum_all(jnp.concatenate([gain_in_sum, stats], axis=1))
+    if small:
+        sums, *head_got = lax.optimization_barrier((sums, *head_got))
+        head_own = total(head_column[0], *head_got)
+    sums = sums[0]
     total_in, total_mid, totals = sums[:d], sums[d : 2 * d], sums[2 * d : 2 * d + 4]
     rms_values = jnp.sqrt(totals[:3] / (totals[3] * d))
     return (

time: 288 us -> 264 us (0.917)
  waiting for transfers between devices: 52.9 us -> 34.6 us
  Pallas kernels: 129 us -> 134 us
  starting transfers between devices: 52 us -> 47.6 us
  other arithmetic: 20.1 us -> 16.5 us
    ppermute x25 -> x26, waiting for transfers between devices: 42.5 us -> 25.5 us  [swap_wide(): return lax.ppermute(value, 'wide', [(i, i ^ offset) for i in range(n)])]
    ppermute x25 -> x26, starting transfers between devices: 38 us -> 31.7 us  [swap_wide(): return lax.ppermute(value, 'wide', [(i, i ^ offset) for i in range(n)])]
    pallas_call x2, Pallas kernels: 40.1 us -> 45.1 us  [head_backward(): pl.pallas_call(functools.partial(head_back_kernel, out_table, len(blocks)...]
    ppermute x12 -> x13, waiting for transfers between devices: 8.83 us -> 5.79 us  [swap_x(): return lax.ppermute(value, 'narrow', [(i, i ^ 2) for i in range(4)])]
    ppermute x12 -> x13, starting transfers between devices: 13.8 us -> 15.4 us  [swap_x(): return lax.ppermute(value, 'narrow', [(i, i ^ 2) for i in range(4)])]
    unnamed x150 -> x89, local copies, waits for them, and re-layouts: 20.3 us -> 19.2 us
  transfers between devices with their start and end apart: 42 -> 44, of which waited for: 19 -> 13; matrix products, arithmetic and copies ran while one was open for 8% -> 7% of each run, Pallas kernels for 41% -> 46%
where the time goes in v3:
time: 264 us; the launch traced here: 260 us
  Pallas kernels  134 us (51%)
  starting transfers between devices  47.6 us (18%)
  waiting for transfers between devices  34.6 us (13%)
  local copies, waits for them, and re-layouts  23.7 us (9%)
  other arithmetic  16.5 us (6%)
  between operations  2.81 us (1%)
    pallas_call x2, Pallas kernels, head_backward(): pl.pallas_call(functools.partial(head_back_kernel, out_table, len(blocks)...  45.1 us
    pallas_call x2, Pallas kernels, head_forward(): pl.pallas_call(functools.partial(head_kernel, tables, counts, rows, share...  32.9 us
    pallas_call x2, Pallas kernels, feed_forward(): pl.pallas_call(kernel, out_shape=out_shape + block_shapes, grid_spec=pltp...  32.2 us
    ppermute x26, starting transfers between devices, swap_wide(): return lax.ppermute(value, 'wide', [(i, i ^ offset) for i in range(n)])  31.7 us
    ppermute x26, waiting for transfers between devices, swap_wide(): return lax.ppermute(value, 'wide', [(i, i ^ offset) for i in range(n)])  25.5 us
    unnamed x89, local copies, waits for them, and re-layouts  19.2 us
    pallas_call x1, Pallas kernels, last_backward(): pl.pallas_call(functools.partial(last_kernel, (own[0], other[0]), (len(ow...  16 us
    ppermute x13, starting transfers between devices, swap_x(): return lax.ppermute(value, 'narrow', [(i, i ^ 2) for i in range(4)])  15.4 us
  transfers between devices with their start and end apart: 44, of which 13 were waited for; matrix products, arithmetic and copies ran while one was open for 7% of the time, Pallas kernels for 46%

profile of v3, /device:TPU:0, one launch (start us, length us, event | category | flops | bytes accessed | tf_op | source)
XLA Modules:
  0.0 259.6 jit_solution(5154090101463260620)
XLA Ops:
  0.7 0.9 copy.27
  1.6 1.0 maximum_bitcast_fusion.1.refs_0_.refs_5_.refs_6_
  2.6 3.0 %collective-permute-start.4 = (bf16[1,96,768]{2,1,0:T(8,128)(2,1)S(1)}, bf16[1,96,768]{2,1,0:T(8,128)(2,1)S(1)}, u32[]{:S(2)}, u32[]{:S(2)}) collective-permute-start(bf16[1,96,768]{2,1,0:T(8,128)(2,1)S(1)} %maximum_bitcast_fusion.1.refs_0_.refs_5_.refs_6_), channel_id=1, source_target_pairs={{0,2},{1,3},{2,0},{3,1},{4,6},{5,7},{6,4},{7,5},{8,10},{9,11},{10,... | collective-permute-start | bytes 442376 | tf_op jit(solution)/shard_map/ppermute | solution.py:764
  5.6 1.5 collective-permute-start.3
  7.1 1.0 maximum_bitcast_fusion.refs_0_
  8.7 4.1 %collective-permute-start.2 = (bf16[1,96,768]{2,1,0:T(8,128)(2,1)S(1)}, bf16[1,96,768]{2,1,0:T(8,128)(2,1)S(1)}, u32[]{:S(2)}, u32[]{:S(2)}) collective-permute-start(bf16[1,96,768]{2,1,0:T(8,128)(2,1)S(1)} %maximum_bitcast_fusion.1.refs_0_.refs_5_.refs_6_), channel_id=1, source_target_pairs={{0,24},{4,28},{8,16},{12,20},{16,8},{20,12},{24,0},{28,4},{1,25},{... | collective-permute-start | bytes 442376 | tf_op jit(solution)/shard_map/ppermute | solution.py:769
  12.8 1.0 collective-permute-start
  13.8 3.7 %collective-permute-done.2 = bf16[1,96,768]{2,1,0:T(8,128)(2,1)S(1)} collective-permute-done((bf16[1,96,768]{2,1,0:T(8,128)(2,1)S(1)}, bf16[1,96,768]{2,1,0:T(8,128)(2,1)S(1)}, u32[]{:S(2)}, u32[]{:S(2)}) %collective-permute-start.2) | collective-permute-done | bytes 147488 | tf_op jit(solution)/shard_map/ppermute | solution.py:769
  17.6 6.6 %collective-permute-done.1 = bf16[1,96,768]{2,1,0:T(8,128)(2,1)S(1)} collective-permute-done((bf16[1,96,768]{2,1,0:T(8,128)(2,1)S(1)}, bf16[1,96,768]{2,1,0:T(8,128)(2,1)S(1)}, u32[]{:S(2)}, u32[]{:S(2)}) %collective-permute-start.1) | collective-permute-done | bytes 147488 | tf_op jit(solution)/shard_map/ppermute | solution.py:769
  24.2 1.6 collective-permute-start.7
  28.5 2.6 %collective-permute-start.11 = (bf16[1,96,1536]{2,1,0:T(8,128)(2,1)S(1)}, bf16[1,96,1536]{2,1,0:T(8,128)(2,1)S(1)}, u32[]{:S(2)}, u32[]{:S(2)}) collective-permute-start(bf16[1,96,1536]{2,1,0:T(8,128)(2,1)S(1)} %maximum_bitcast_fusion.refs_0_), channel_id=1, source_target_pairs={{0,24},{4,28},{8,16},{12,20},{16,8},{20,12},{24,0},{28,4},{1,25},{... | collective-permute-start | bytes 884744 | tf_op jit(solution)/shard_map/ppermute | solution.py:769
  31.1 1.8 collective-permute-start.9
  32.9 5.8 %collective-permute-done.8.refs_3_.refs_6_.refs_12_ = bf16[1,96,768]{2,1,0:T(8,128)(2,1)S(1)} collective-permute-done((bf16[1,96,768]{2,1,0:T(8,128)(2,1)S(1)}, bf16[1,96,768]{2,1,0:T(8,128)(2,1)S(1)}, u32[]{:S(2)}, u32[]{:S(2)}) %collective-permute-start.8) | collective-permute-done | bytes 147488 | tf_op jit(solution)/shard_map/ppermute | solution.py:769
  38.6 1.5 collective-permute-start.14
  40.7 1.9 copy-done
  42.6 16.5 %head_forward.2 = (bf16[2048,768]{1,0:T(8,128)(2,1)S(1)}, bf16[1024,256]{1,0:T(8,128)(2,1)S(1)}, bf16[2048,256]{1,0:T(8,128)(2,1)S(1)}, bf16[2048,256]{1,0:T(8,1...) custom-call(s32[11]{0:T(128)S(1)} %concatenate.33.s_ref, bf16[2048,768]{1,0:T(8,128)(2,1)S(1)} %copy-done, ...), custom_call_target="tpu_custom_call" | custom-call | flops 8053063680 | bytes 12582912 | tf_op jit(solution)/shard_map/head_forward/pallas_call | solution.py:304
  59.1 1.0 copy-done.19
  61.0 1.6 collective-permute-start.13
  62.5 1.5 collective-permute-start.12
  64.1 16.4 %head_forward.3 = (bf16[1024,256]{1,0:T(8,128)(2,1)S(1)}, bf16[2048,256]{1,0:T(8,128)(2,1)S(1)}, bf16[2048,256]{1,0:T(8,128)(2,1)S(1)}, bf16[1024,256]{1,0:T(8,1...) custom-call(s32[11]{0:T(128)S(1)} %concatenate.33.s_ref, ...), custom_call_target="tpu_custom_call" | custom-call | flops 8053063680 | bytes 12582912 | tf_op jit(solution)/shard_map/head_forward/pallas_call | solution.py:304
  80.5 1.0 copy-done.16
  81.5 1.0 copy-done.17
  84.8 1.5 collective-permute-start.17
  87.6 1.1 copy-done.24
  88.7 17.7 %feed_forward.2 = (bf16[1024,768]{1,0:T(8,128)(2,1)S(1)}, bf16[1024,768]{1,0:T(8,128)(2,1)S(1)}, f32[1024,768]{1,0:T(8,128)S(1)}, f32[768,1024]{1,0:T(8,128)}, f...) custom-call(s32[11]{0:T(128)S(1)} %concatenate.33.s_ref, ...), custom_call_target="tpu_custom_call" | custom-call | flops 7247757312 | bytes 7864320 | tf_op jit(solution)/shard_map/feed_forward/pallas_call | solution.py:468
  106.4 1.7 copy-done.11
  108.2 1.2 copy-done.12
  109.4 1.1 copy-done.13
  110.6 14.4 %feed_forward.3 = (bf16[1024,768]{1,0:T(8,128)(2,1)S(1)}, bf16[384,1024]{1,0:T(8,128)(2,1)S(1)}, bf16[384,1024]{1,0:T(8,128)(2,1)S(1)}, bf16[2,96,1536]{2,1,0:T(...) custom-call(s32[11]{0:T(128)S(1)} %concatenate.33.s_ref, ...), custom_call_target="tpu_custom_call" | custom-call | flops 7247757312 | bytes 7864320 | tf_op jit(solution)/shard_map/feed_forward/pallas_call | solution.py:468
  126.6 1.6 collective-permute-start.27
  128.5 1.2 copy-done.25
  129.7 8.2 %mid_backward.1 = (f32[768,1024]{1,0:T(8,128)S(1)}, bf16[1024,256]{1,0:T(8,128)(2,1)S(1)}, bf16[1024,256]{1,0:T(8,128)(2,1)S(1)}, f32[2,768,256]{2,1,0:T(8,128)S(1)}, f32[1,768]{1,0:T(1,128)S(1)}) custom-call(s32[11]{0:T(128)S(1)} %concatenate.33.s_ref, bf16[2048,768]{1,0:T(8,128)(2,1)} %x_ref.3, bf16[1024,768]{1,0:T(8,128)(2,1)} %copy-done.2, ...), custom_call_target="tpu_custom_call" | custom-call | flops 1610612736 | bytes 12582912 | tf_op jit(solution)/shard_map/mid_backward/pallas_call | solution.py:537
  137.9 1.1 copy-done.8
  139.9 0.8 copy-done.10
  140.9 1.3 collective-permute-done.22
  142.4 1.4 collective-permute-start.24
  145.2 22.6 %head_backward.2 = (bf16[1024,256]{1,0:T(8,128)(2,1)S(1)}, bf16[2048,256]{1,0:T(8,128)(2,1)S(1)}, bf16[2048,256]{1,0:T(8,128)(2,1)S(1)}, bf16[8,96,768]{2,1,0:T(8,128)(2,1)S(1)}) custom-call(s32[11]{0:T(128)S(1)} %concatenate.33.s_ref, bf16[1024,256]{1,0:T(8,128)(2,1)} %copy-done.20, bf16[2048,256]{1,0:T(8,128)(2,1)} %copy-done.16, ...), custom_call_target="tpu_custom_call" | custom-call | flops 16106127360 | bytes 12582912 | tf_op jit(solution)/shard_map/head_backward/pallas_call | solution.py:651
  167.8 1.4 collective-permute-start.28
  169.2 1.9 fusion.11
  171.1 1.5 collective-permute-start.31
  172.7 2.9 %collective-permute-start.29 = (bf16[96,1536]{1,0:T(8,128)(2,1)S(1)}, bf16[96,1536]{1,0:T(8,128)(2,1)S(1)}, u32[]{:S(2)}, u32[]{:S(2)}) collective-permute-start(bf16[96,1536]{1,0:T(8,128)(2,1)S(1)} %get-tuple-element.249), channel_id=1, source_target_pairs={{0,8},{4,12},{8,0},{12,4},{16,24},{20,28},{24,16},{28,20},{1,9},{5... | collective-permute-start | bytes 884744 | tf_op jit(solution)/shard_map/ppermute | solution.py:769
  175.6 1.4 select_reduce_fusion
  177.0 1.4 maximum_bitcast_fusion.2
  178.5 22.5 %head_backward.3 = (bf16[1024,256]{1,0:T(8,128)(2,1)S(1)}, bf16[2048,256]{1,0:T(8,128)(2,1)S(1)}, bf16[2048,256]{1,0:T(8,128)(2,1)S(1)}, bf16[4,96,768]{2,1,0:T(8,128)(2,1)S(1)}, bf16[4,96,768]{2,1,0:T(8,128)(2,1)S(1)}) custom-call(s32[11]{0:T(128)S(1)} %concatenate.33.s_ref, bf16[1024,256]{1,0:T(8,128)(2,1)} %copy-done.22, bf16[2048,256]{1,0:T(8,128)(2,1)} %copy-done.18, ...), custom_call_target="tpu_custom_call" | custom-call | flops 16106127360 | bytes 12582912 | tf_op jit(solution)/shard_map/head_backward/pallas_call | solution.py:651
  201.2 1.6 collective-permute-start.32
  203.5 16.0 %last_backward.1 = (bf16[384,2048]{1,0:T(8,128)(2,1)S(1)}, bf16[384,2048]{1,0:T(8,128)(2,1)S(1)}, f32[1,768]{1,0:T(1,128)S(1)}) custom-call(s32[11]{0:T(128)S(1)} %concatenate.33.s_ref, bf16[2048,768]{1,0:T(8,128)(2,1)S(1)} %copy-done.1, f32[1,768]{1,0:T(1,128)S(1)} %broadcast_in_dim.34.gain_ref, f32[768,1024]{1,0:T(8,128)} %copy-done.7, ...), custom_call_target="tpu_custom_call" | custom-call | flops 4026531840 | bytes 15728640 | tf_op jit(solution)/shard_map/last_backward/pallas_call | solution.py:726
  219.7 1.2 fusion.10
  221.7 1.4 collective-permute-done.34
  223.4 0.9 copy-done.26
  224.4 1.0 collective-permute-done.36
  225.4 1.4 collective-permute-start.37
  226.8 2.3 collective-permute-done.37
  229.8 1.4 fusion.3
  231.2 1.6 collective-permute-done.38
  233.7 1.5 collective-permute-start.43
  235.2 2.0 collective-permute-start.42
  237.2 0.9 collective-permute-start.41
  238.1 1.2 collective-permute-start.40
  239.3 1.2 fusion
  240.5 1.3 collective-permute-start.35
  241.8 6.5 %collective-permute-done.40 = f32[1,1664]{1,0:T(1,128)S(1)} collective-permute-done((f32[1,1664]{1,0:T(1,128)S(1)}, f32[1,1664]{1,0:T(1,128)S(1)}, u32[]{:S(2)}, u32[]{:S(2)}) %collective-permute-start.40) | collective-permute-done | bytes 6688 | tf_op jit(solution)/shard_map/ppermute | solution.py:769
  248.9 1.0 fusion.7
  253.3 3.2 %collective-permute-done.35 = bf16[192,2048]{1,0:T(8,128)(2,1)} collective-permute-done((bf16[192,2048]{1,0:T(8,128)(2,1)S(1)}, bf16[192,2048]{1,0:T(8,128)(2,1)}, u32[]{:S(2)}, u32[]{:S(2)}) %collective-permute-start.35) | collective-permute-done | bytes 786464 | tf_op jit(solution)/shard_map/ppermute | solution.py:764
  256.5 2.9 %add_bitcast_fusion = f32[2048,192]{0,1:T(8,128)} fusion(bf16[192,2048]{1,0:T(8,128)(2,1)} %collective-permute-done.35, bf16[384,2048]{1,0:T(8,128)(2,1)} %copy-done.26, bf16[384,2048]{1,0:T(8,128)(2,1)S(1)} %get-tuple-element.199), kind=kLoop, calls=%fused_computation.1 | loop fusion | flops 1966080 | bytes 3932160 | tf_op jit(solution)/shard_map/transpose | solution.py:1010
  (162 shorter events, 19.4 us)
Async XLA Ops:
  0.6 25.7 %copy-start.38 = (s32[4]{0:T(128)S(1)}, s32[4]{0:T(128)}, u32[]{:S(2)}) copy-start(s32[4]{0:T(128)} %param.24) | copy-start | bytes 52
  0.7 25.8 %copy-start.39 = (s32[4]{0:T(128)S(1)}, s32[4]{0:T(128)}, u32[]{:S(2)}) copy-start(s32[4]{0:T(128)} %param.25) | copy-start | bytes 52
  0.7 25.8 %copy-start.36 = (f32[768]{0:T(1024)S(1)}, f32[768]{0:T(1024)}, u32[]{:S(2)}) copy-start(f32[768]{0:T(1024)} %param.14) | copy-start | bytes 9220
  0.7 25.8 %copy-start.37 = (f32[768]{0:T(1024)S(1)}, f32[768]{0:T(1024)}, u32[]{:S(2)}) copy-start(f32[768]{0:T(1024)} %param.15) | copy-start | bytes 9220
  2.6 10.2 %collective-permute-start.4 = (bf16[1,96,768]{2,1,0:T(8,128)(2,1)S(1)}, bf16[1,96,768]{2,1,0:T(8,128)(2,1)S(1)}, u32[]{:S(2)}, u32[]{:S(2)}) collective-permute-start(bf16[1,96,768]{2,1,0:T(8,128)(2,1)S(1)} %maximum_bitcast_fusion.1.refs_0_.refs_5_.refs_6_), channel_id=1, source_target_pairs={{0,2},{1,3},{2,0},{3,1},{4,6},{5,7},{6,4},{7,5},{8,10},{9,11},{10,... | collective-permute-start | bytes 442376 | tf_op jit(solution)/shard_map/ppermute | solution.py:764
  5.6 7.2 %collective-permute-start.3 = (bf16[1,96,768]{2,1,0:T(8,128)(2,1)S(1)}, bf16[1,96,768]{2,1,0:T(8,128)(2,1)S(1)}, u32[]{:S(2)}, u32[]{:S(2)}) collective-permute-start(bf16[1,96,768]{2,1,0:T(8,128)(2,1)S(1)} %maximum_bitcast_fusion.1.refs_0_.refs_5_.refs_6_), channel_id=1, source_target_pairs={{0,4},{4,0},{8,12},{12,8},{16,20},{20,16},{24,28},{28,24},{1,5},{5... | collective-permute-start | bytes 442376 | tf_op jit(solution)/shard_map/ppermute | solution.py:769
  8.1 16.1 %collective-permute-start.6 = (bf16[1,96,1536]{2,1,0:T(8,128)(2,1)S(1)}, bf16[1,96,1536]{2,1,0:T(8,128)(2,1)S(1)}, u32[]{:S(2)}, u32[]{:S(2)}) collective-permute-start(bf16[1,96,1536]{2,1,0:T(8,128)(2,1)S(1)} %maximum_bitcast_fusion.refs_0_), channel_id=1, source_target_pairs={{0,2},{1,3},{2,0},{3,1},{4,6},{5,7},{6,4},{7,5},{8,10},{9,11},{10,... | collective-permute-start | bytes 884744 | tf_op jit(solution)/shard_map/ppermute | solution.py:764
  8.7 15.5 %collective-permute-start.5 = (bf16[1,96,1536]{2,1,0:T(8,128)(2,1)S(1)}, bf16[1,96,1536]{2,1,0:T(8,128)(2,1)S(1)}, u32[]{:S(2)}, u32[]{:S(2)}) collective-permute-start(bf16[1,96,1536]{2,1,0:T(8,128)(2,1)S(1)} %maximum_bitcast_fusion.refs_0_), channel_id=1, source_target_pairs={{0,4},{4,0},{8,12},{12,8},{16,20},{20,16},{24,28},{28,24},{1,5},{5... | collective-permute-start | bytes 884744 | tf_op jit(solution)/shard_map/ppermute | solution.py:769
  8.7 8.8 %collective-permute-start.2 = (bf16[1,96,768]{2,1,0:T(8,128)(2,1)S(1)}, bf16[1,96,768]{2,1,0:T(8,128)(2,1)S(1)}, u32[]{:S(2)}, u32[]{:S(2)}) collective-permute-start(bf16[1,96,768]{2,1,0:T(8,128)(2,1)S(1)} %maximum_bitcast_fusion.1.refs_0_.refs_5_.refs_6_), channel_id=1, source_target_pairs={{0,24},{4,28},{8,16},{12,20},{16,8},{20,12},{24,0},{28,4},{1,25},{... | collective-permute-start | bytes 442376 | tf_op jit(solution)/shard_map/ppermute | solution.py:769
  12.8 11.4 %collective-permute-start.1 = (bf16[1,96,768]{2,1,0:T(8,128)(2,1)S(1)}, bf16[1,96,768]{2,1,0:T(8,128)(2,1)S(1)}, u32[]{:S(2)}, u32[]{:S(2)}) collective-permute-start(bf16[1,96,768]{2,1,0:T(8,128)(2,1)S(1)} %maximum_bitcast_fusion.1.refs_0_.refs_5_.refs_6_), channel_id=1, source_target_pairs={{0,16},{4,20},{8,24},{12,28},{16,0},{20,4},{24,8},{28,12},{1,17},{... | collective-permute-start | bytes 442376 | tf_op jit(solution)/shard_map/ppermute | solution.py:769
  12.8 11.3 %collective-permute-start = (bf16[1,96,768]{2,1,0:T(8,128)(2,1)S(1)}, bf16[1,96,768]{2,1,0:T(8,128)(2,1)S(1)}, u32[]{:S(2)}, u32[]{:S(2)}) collective-permute-start(bf16[1,96,768]{2,1,0:T(8,128)(2,1)S(1)} %maximum_bitcast_fusion.1.refs_0_.refs_5_.refs_6_), channel_id=1, source_target_pairs={{0,8},{4,12},{8,0},{12,4},{16,24},{20,28},{24,16},{28,20},{1,9},{5... | collective-permute-start | bytes 442376 | tf_op jit(solution)/shard_map/ppermute | solution.py:769
  24.2 15.9 %collective-permute-start.7 = (bf16[3,96,768]{2,1,0:T(8,128)(2,1)S(1)}, bf16[3,96,768]{2,1,0:T(8,128)(2,1)S(1)}, u32[]{:S(2)}, u32[]{:S(2)}) collective-permute-start(bf16[3,96,768]{2,1,0:T(8,128)(2,1)S(1)} %constant_dynamic-update-slice_fusion.refs_1_.refs_6_.refs_7_), channel_id=1, source_target_pairs={{0,4},{4,0},{8,12},{12,8},{16,20},{20,16},{24,28},{28,24},{1,5},{5... | collective-permute-start | bytes 1327112 | tf_op jit(solution)/shard_map/ppermute | solution.py:769
  25.8 12.8 %collective-permute-start.8 = (bf16[1,96,768]{2,1,0:T(8,128)(2,1)S(1)}, bf16[1,96,768]{2,1,0:T(8,128)(2,1)S(1)}, u32[]{:S(2)}, u32[]{:S(2)}) collective-permute-start(bf16[1,96,768]{2,1,0:T(8,128)(2,1)S(1)} %collective-permute-done.4.refs_1_.refs_4_.refs_10_), channel_id=1, source_target_pairs={{0,4},{4,0},{8,12},{12,8},{16,20},{20,16},{24,28},{28,24},{1,5},{5... | collective-permute-start | bytes 442376 | tf_op jit(solution)/shard_map/ppermute | solution.py:769
  28.5 32.4 %collective-permute-start.11 = (bf16[1,96,1536]{2,1,0:T(8,128)(2,1)S(1)}, bf16[1,96,1536]{2,1,0:T(8,128)(2,1)S(1)}, u32[]{:S(2)}, u32[]{:S(2)}) collective-permute-start(bf16[1,96,1536]{2,1,0:T(8,128)(2,1)S(1)} %maximum_bitcast_fusion.refs_0_), channel_id=1, source_target_pairs={{0,24},{4,28},{8,16},{12,20},{16,8},{20,12},{24,0},{28,4},{1,25},{... | collective-permute-start | bytes 884744 | tf_op jit(solution)/shard_map/ppermute | solution.py:769
  31.1 29.8 %collective-permute-start.10 = (bf16[1,96,1536]{2,1,0:T(8,128)(2,1)S(1)}, bf16[1,96,1536]{2,1,0:T(8,128)(2,1)S(1)}, u32[]{:S(2)}, u32[]{:S(2)}) collective-permute-start(bf16[1,96,1536]{2,1,0:T(8,128)(2,1)S(1)} %maximum_bitcast_fusion.refs_0_), channel_id=1, source_target_pairs={{0,16},{4,20},{8,24},{12,28},{16,0},{20,4},{24,8},{28,12},{1,17},{... | collective-permute-start | bytes 884744 | tf_op jit(solution)/shard_map/ppermute | solution.py:769
  31.1 29.8 %collective-permute-start.9 = (bf16[1,96,1536]{2,1,0:T(8,128)(2,1)S(1)}, bf16[1,96,1536]{2,1,0:T(8,128)(2,1)S(1)}, u32[]{:S(2)}, u32[]{:S(2)}) collective-permute-start(bf16[1,96,1536]{2,1,0:T(8,128)(2,1)S(1)} %maximum_bitcast_fusion.refs_0_), channel_id=1, source_target_pairs={{0,8},{4,12},{8,0},{12,4},{16,24},{20,28},{24,16},{28,20},{1,9},{5... | collective-permute-start | bytes 884744 | tf_op jit(solution)/shard_map/ppermute | solution.py:769
  38.6 25.4 %collective-permute-start.14 = (bf16[3,96,768]{2,1,0:T(8,128)(2,1)S(1)}, bf16[3,96,768]{2,1,0:T(8,128)(2,1)S(1)}, u32[]{:S(2)}, u32[]{:S(2)}) collective-permute-start(bf16[3,96,768]{2,1,0:T(8,128)(2,1)S(1)} %constant_dynamic-update-slice_fusion.refs_1_.refs_6_.refs_7_), channel_id=1, source_target_pairs={{0,2},{1,3},{2,0},{3,1},{4,6},{5,7},{6,4},{7,5},{8,10},{9,11},{10,... | collective-permute-start | bytes 1327112 | tf_op jit(solution)/shard_map/ppermute | solution.py:764
  40.1 23.9 %collective-permute-start.15 = (bf16[3,96,768]{2,1,0:T(8,128)(2,1)S(1)}, bf16[3,96,768]{2,1,0:T(8,128)(2,1)S(1)}, u32[]{:S(2)}, u32[]{:S(2)}) collective-permute-start(bf16[3,96,768]{2,1,0:T(8,128)(2,1)S(1)} %collective-permute-done.7.refs_3_.refs_8_.refs_9_), channel_id=1, source_target_pairs={{0,2},{1,3},{2,0},{3,1},{4,6},{5,7},{6,4},{7,5},{8,10},{9,11},{10,... | collective-permute-start | bytes 1327112 | tf_op jit(solution)/shard_map/ppermute | solution.py:764
  60.8 19.6 %copy-start.14 = (bf16[2048,768]{1,0:T(8,128)(2,1)}, bf16[2048,768]{1,0:T(8,128)(2,1)S(1)}, u32[]{:S(2)}) copy-start(bf16[2048,768]{1,0:T(8,128)(2,1)S(1)} %get-tuple-element.130.x_ref.normed_ref) | copy-start | bytes 9437188
  60.8 19.6 %copy-start.18 = (bf16[2048,256]{1,0:T(8,128)(2,1)}, bf16[2048,256]{1,0:T(8,128)(2,1)S(1)}, u32[]{:S(2)}) copy-start(bf16[2048,256]{1,0:T(8,128)(2,1)S(1)} %get-tuple-element.170.k_ref) | copy-start | bytes 3145732
  60.8 19.6 %copy-start.23 = (bf16[1024,256]{1,0:T(8,128)(2,1)}, bf16[1024,256]{1,0:T(8,128)(2,1)S(1)}, u32[]{:S(2)}) copy-start(bf16[1024,256]{1,0:T(8,128)(2,1)S(1)} %get-tuple-element.182.aux_ref) | copy-start | bytes 1572868
  60.8 67.7 %copy-start.4 = (bf16[1024,256]{1,0:T(8,128)(2,1)}, bf16[1024,256]{1,0:T(8,128)(2,1)S(1)}, u32[]{:S(2)}) copy-start(bf16[1024,256]{1,0:T(8,128)(2,1)S(1)} %get-tuple-element.122.refs_0_.o0_ref.o_ref) | copy-start | bytes 1572868
  61.0 23.1 %collective-permute-start.13 = (bf16[3,96,1536]{2,1,0:T(8,128)(2,1)S(1)}, bf16[3,96,1536]{2,1,0:T(8,128)(2,1)S(1)}, u32[]{:S(2)}, u32[]{:S(2)}) collective-permute-start(bf16[3,96,1536]{2,1,0:T(8,128)(2,1)S(1)} %pad_maximum_fusion.refs_1_), channel_id=1, source_target_pairs={{0,2},{1,3},{2,0},{3,1},{4,6},{5,7},{6,4},{7,5},{8,10},{9,11},{10,... | collective-permute-start | bytes 2654216 | tf_op jit(solution)/shard_map/ppermute | solution.py:764
  62.5 21.5 %collective-permute-start.12 = (bf16[3,96,1536]{2,1,0:T(8,128)(2,1)S(1)}, bf16[3,96,1536]{2,1,0:T(8,128)(2,1)S(1)}, u32[]{:S(2)}, u32[]{:S(2)}) collective-permute-start(bf16[3,96,1536]{2,1,0:T(8,128)(2,1)S(1)} %pad_maximum_fusion.refs_1_), channel_id=1, source_target_pairs={{0,4},{4,0},{8,12},{12,8},{16,20},{20,16},{24,28},{28,24},{1,5},{5... | collective-permute-start | bytes 2654216 | tf_op jit(solution)/shard_map/ppermute | solution.py:769
  84.1 3.5 %copy-start.2 = (bf16[1024,768]{1,0:T(8,128)(2,1)}, bf16[1024,768]{1,0:T(8,128)(2,1)S(1)}, u32[]{:S(2)}) copy-start(bf16[1024,768]{1,0:T(8,128)(2,1)S(1)} %get-tuple-element.132.a_ref) | copy-start | bytes 4718596
  84.1 44.4 %copy-start.5 = (bf16[1024,256]{1,0:T(8,128)(2,1)}, bf16[1024,256]{1,0:T(8,128)(2,1)S(1)}, u32[]{:S(2)}) copy-start(bf16[1024,256]{1,0:T(8,128)(2,1)S(1)} %get-tuple-element.142.o1_ref.o_ref) | copy-start | bytes 1572868
  84.1 3.5 %collective-permute-start.16 = (bf16[1024,768]{1,0:T(8,128)(2,1)S(1)}, bf16[1024,768]{1,0:T(8,128)(2,1)S(1)}, u32[]{:S(2)}, u32[]{:S(2)}) collective-permute-start(bf16[1024,768]{1,0:T(8,128)(2,1)S(1)} %get-tuple-element.132.a_ref), channel_id=1, source_target_pairs={{0,1},{1,0},{2,3},{3,2},{4,5},{5,4},{6,7},{7,6},{8,9},{9,8},{10,11... | collective-permute-start | bytes 4718600 | tf_op jit(solution)/shard_map/ppermute | solution.py:760
  84.2 26.4 %collective-permute-start.19 = (bf16[1,96,1536]{2,1,0:T(8,128)(2,1)S(1)}, bf16[1,96,1536]{2,1,0:T(8,128)(2,1)S(1)}, u32[]{:S(2)}, u32[]{:S(2)}) collective-permute-start(bf16[1,96,1536]{2,1,0:T(8,128)(2,1)S(1)} %slice.109), channel_id=1, source_target_pairs={{0,4},{4,0},{8,12},{12,8},{16,20},{20,16},{24,28},{28,24},{1,5},{5... | collective-permute-start | bytes 884744 | tf_op jit(solution)/shard_map/ppermute | solution.py:769
  84.8 25.8 %collective-permute-start.17 = (bf16[1,96,1536]{2,1,0:T(8,128)(2,1)S(1)}, bf16[1,96,1536]{2,1,0:T(8,128)(2,1)S(1)}, u32[]{:S(2)}, u32[]{:S(2)}) collective-permute-start(bf16[1,96,1536]{2,1,0:T(8,128)(2,1)S(1)} %collective-permute-done.6.refs_0_), channel_id=1, source_target_pairs={{0,4},{4,0},{8,12},{12,8},{16,20},{20,16},{24,28},{28,24},{1,5},{5... | collective-permute-start | bytes 884744 | tf_op jit(solution)/shard_map/ppermute | solution.py:769
  86.3 24.2 %collective-permute-start.18 = (bf16[2,96,1536]{2,1,0:T(8,128)(2,1)S(1)}, bf16[2,96,1536]{2,1,0:T(8,128)(2,1)S(1)}, u32[]{:S(2)}, u32[]{:S(2)}) collective-permute-start(bf16[2,96,1536]{2,1,0:T(8,128)(2,1)S(1)} %slice.108), channel_id=1, source_target_pairs={{0,2},{1,3},{2,0},{3,1},{4,6},{5,7},{6,4},{7,5},{8,10},{9,11},{10,... | collective-permute-start | bytes 1769480 | tf_op jit(solution)/shard_map/ppermute | solution.py:764
  110.6 19.1 %copy-start.6 = (f32[1,768]{1,0:T(1,128)S(1)}, f32[1,768]{1,0:T(1,128)}, u32[]{:S(2)}) copy-start(f32[1,768]{1,0:T(1,128)} %broadcast_in_dim.35.gain_ref) | copy-start | bytes 9220
  125.0 3.5 %copy-start.3 = (bf16[1024,768]{1,0:T(8,128)(2,1)}, bf16[1024,768]{1,0:T(8,128)(2,1)S(1)}, u32[]{:S(2)}) copy-start(bf16[1024,768]{1,0:T(8,128)(2,1)S(1)} %get-tuple-element.141.g_ref) | copy-start | bytes 4718596
  125.0 3.5 %collective-permute-start.20 = (bf16[1024,768]{1,0:T(8,128)(2,1)S(1)}, bf16[1024,768]{1,0:T(8,128)(2,1)S(1)}, u32[]{:S(2)}, u32[]{:S(2)}) collective-permute-start(bf16[1024,768]{1,0:T(8,128)(2,1)S(1)} %get-tuple-element.141.g_ref), channel_id=1, source_target_pairs={{0,1},{1,0},{2,3},{3,2},{4,5},{5,4},{6,7},{7,6},{8,9},{9,8},{10,11... | collective-permute-start | bytes 4718600 | tf_op jit(solution)/shard_map/ppermute | solution.py:760
  125.3 15.6 %collective-permute-start.21 = (bf16[2,96,1536]{2,1,0:T(8,128)(2,1)S(1)}, bf16[2,96,1536]{2,1,0:T(8,128)(2,1)S(1)}, u32[]{:S(2)}, u32[]{:S(2)}) collective-permute-start(bf16[2,96,1536]{2,1,0:T(8,128)(2,1)S(1)} %get-tuple-element.149), channel_id=1, source_target_pairs={{0,2},{1,3},{2,0},{3,1},{4,6},{5,7},{6,4},{7,5},{8,10},{9,11},{10,... | collective-permute-start | bytes 1769480 | tf_op jit(solution)/shard_map/ppermute | solution.py:764
  126.0 16.2 %collective-permute-start.22 = (bf16[2,96,1536]{2,1,0:T(8,128)(2,1)S(1)}, bf16[2,96,1536]{2,1,0:T(8,128)(2,1)S(1)}, u32[]{:S(2)}, u32[]{:S(2)}) collective-permute-start(bf16[2,96,1536]{2,1,0:T(8,128)(2,1)S(1)} %get-tuple-element.150), channel_id=1, source_target_pairs={{0,4},{4,0},{8,12},{12,8},{16,20},{20,16},{24,28},{28,24},{1,5},{5... | collective-permute-start | bytes 1769480 | tf_op jit(solution)/shard_map/ppermute | solution.py:769
  126.6 41.1 %collective-permute-start.27 = (bf16[2,96,1536]{2,1,0:T(8,128)(2,1)}, bf16[2,96,1536]{2,1,0:T(8,128)(2,1)S(1)}, u32[]{:S(2)}, u32[]{:S(2)}) collective-permute-start(bf16[2,96,1536]{2,1,0:T(8,128)(2,1)} %get-tuple-element.176), channel_id=1, source_target_pairs={{0,4},{4,0},{8,12},{12,8},{16,20},{20,16},{24,28},{28,24},{1,5},{5... | collective-permute-start | bytes 1769480 | tf_op jit(solution)/shard_map/ppermute | solution.py:769
  142.4 26.8 %collective-permute-start.24 = (bf16[2,96,1536]{2,1,0:T(8,128)(2,1)S(1)}, bf16[2,96,1536]{2,1,0:T(8,128)(2,1)S(1)}, u32[]{:S(2)}, u32[]{:S(2)}) collective-permute-start(bf16[2,96,1536]{2,1,0:T(8,128)(2,1)S(1)} %add_convert_fusion.2), channel_id=1, source_target_pairs={{0,2},{1,3},{2,0},{3,1},{4,6},{5,7},{6,4},{7,5},{8,10},{9,11},{10,... | collective-permute-start | bytes 1769480 | tf_op jit(solution)/shard_map/ppermute | solution.py:764
  143.9 25.3 %collective-permute-start.25 = (bf16[2,96,1536]{2,1,0:T(8,128)(2,1)S(1)}, bf16[2,96,1536]{2,1,0:T(8,128)(2,1)S(1)}, u32[]{:S(2)}, u32[]{:S(2)}) collective-permute-start(bf16[2,96,1536]{2,1,0:T(8,128)(2,1)S(1)} %add_convert_fusion.3), channel_id=1, source_target_pairs={{0,4},{4,0},{8,12},{12,8},{16,20},{20,16},{24,28},{28,24},{1,5},{5... | collective-permute-start | bytes 1769480 | tf_op jit(solution)/shard_map/ppermute | solution.py:769
  144.5 24.7 %collective-permute-start.26 = (bf16[2,96,1536]{2,1,0:T(8,128)(2,1)S(1)}, bf16[2,96,1536]{2,1,0:T(8,128)(2,1)S(1)}, u32[]{:S(2)}, u32[]{:S(2)}) collective-permute-start(bf16[2,96,1536]{2,1,0:T(8,128)(2,1)S(1)} %get-tuple-element.175), channel_id=1, source_target_pairs={{0,2},{1,3},{2,0},{3,1},{4,6},{5,7},{6,4},{7,5},{8,10},{9,11},{10,... | collective-permute-start | bytes 1769480 | tf_op jit(solution)/shard_map/ppermute | solution.py:764
  145.2 30.4 %collective-permute-start.23 = (bf16[384,1024]{1,0:T(8,128)(2,1)S(1)}, bf16[384,1024]{1,0:T(8,128)(2,1)S(1)}, u32[]{:S(2)}, u32[]{:S(2)}) collective-permute-start(bf16[384,1024]{1,0:T(8,128)(2,1)S(1)} %get-tuple-element.158), channel_id=1, source_target_pairs={{0,1},{1,0},{2,3},{3,2},{4,5},{5,4},{6,7},{7,6},{8,9},{9,8},{10,11... | collective-permute-start | bytes 2359304 | tf_op jit(solution)/shard_map/ppermute | solution.py:760
  167.8 33.2 %collective-permute-start.28 = (bf16[8,96,768]{2,1,0:T(8,128)(2,1)S(1)}, bf16[8,96,768]{2,1,0:T(8,128)(2,1)S(1)}, u32[]{:S(2)}, u32[]{:S(2)}) collective-permute-start(bf16[8,96,768]{2,1,0:T(8,128)(2,1)S(1)} %get-tuple-element.164), channel_id=1, source_target_pairs={{0,2},{1,3},{2,0},{3,1},{4,6},{5,7},{6,4},{7,5},{8,10},{9,11},{10,... | collective-permute-start | bytes 3538952 | tf_op jit(solution)/shard_map/ppermute | solution.py:764
  171.1 30.0 %collective-permute-start.31 = (bf16[96,1536]{1,0:T(8,128)(2,1)S(1)}, bf16[96,1536]{1,0:T(8,128)(2,1)S(1)}, u32[]{:S(2)}, u32[]{:S(2)}) collective-permute-start(bf16[96,1536]{1,0:T(8,128)(2,1)S(1)} %get-tuple-element.247), channel_id=1, source_target_pairs={{0,24},{4,28},{8,16},{12,20},{16,8},{20,12},{24,0},{28,4},{1,25},{... | collective-permute-start | bytes 884744 | tf_op jit(solution)/shard_map/ppermute | solution.py:769
  172.7 28.5 %collective-permute-start.30 = (bf16[96,1536]{1,0:T(8,128)(2,1)S(1)}, bf16[96,1536]{1,0:T(8,128)(2,1)S(1)}, u32[]{:S(2)}, u32[]{:S(2)}) collective-permute-start(bf16[96,1536]{1,0:T(8,128)(2,1)S(1)} %get-tuple-element.248), channel_id=1, source_target_pairs={{0,16},{4,20},{8,24},{12,28},{16,0},{20,4},{24,8},{28,12},{1,17},{... | collective-permute-start | bytes 884744 | tf_op jit(solution)/shard_map/ppermute | solution.py:769
  172.7 28.5 %collective-permute-start.29 = (bf16[96,1536]{1,0:T(8,128)(2,1)S(1)}, bf16[96,1536]{1,0:T(8,128)(2,1)S(1)}, u32[]{:S(2)}, u32[]{:S(2)}) collective-permute-start(bf16[96,1536]{1,0:T(8,128)(2,1)S(1)} %get-tuple-element.249), channel_id=1, source_target_pairs={{0,8},{4,12},{8,0},{12,4},{16,24},{20,28},{24,16},{28,20},{1,9},{5... | collective-permute-start | bytes 884744 | tf_op jit(solution)/shard_map/ppermute | solution.py:769
  178.5 25.0 %copy-start.1 = (bf16[2048,768]{1,0:T(8,128)(2,1)S(1)}, bf16[2048,768]{1,0:T(8,128)(2,1)}, u32[]{:S(2)}) copy-start(bf16[2048,768]{1,0:T(8,128)(2,1)} %x_ref.3) | copy-start | bytes 9437188
  201.2 18.4 %copy-start.31 = (bf16[96,1536]{1,0:T(8,128)(2,1)}, bf16[96,1536]{1,0:T(8,128)(2,1)S(1)}, u32[]{:S(2)}) copy-start(bf16[96,1536]{1,0:T(8,128)(2,1)S(1)} %collective-permute-done.30) | copy-start | bytes 884740
  201.2 18.4 %copy-start.32 = (bf16[96,1536]{1,0:T(8,128)(2,1)}, bf16[96,1536]{1,0:T(8,128)(2,1)S(1)}, u32[]{:S(2)}) copy-start(bf16[96,1536]{1,0:T(8,128)(2,1)S(1)} %collective-permute-done.29) | copy-start | bytes 884740
  201.2 18.4 %collective-permute-start.32 = (bf16[4,96,768]{2,1,0:T(8,128)(2,1)S(1)}, bf16[4,96,768]{2,1,0:T(8,128)(2,1)S(1)}, u32[]{:S(2)}, u32[]{:S(2)}) collective-permute-start(bf16[4,96,768]{2,1,0:T(8,128)(2,1)S(1)} %add_convert_fusion.1), channel_id=1, source_target_pairs={{0,4},{4,0},{8,12},{12,8},{16,20},{20,16},{24,28},{28,24},{1,5},{5... | collective-permute-start | bytes 1769480 | tf_op jit(solution)/shard_map/ppermute | solution.py:769
  202.8 16.8 %collective-permute-start.33 = (bf16[192,1024]{1,0:T(8,128)(2,1)S(1)}, bf16[192,1024]{1,0:T(8,128)(2,1)S(1)}, u32[]{:S(2)}, u32[]{:S(2)}) collective-permute-start(bf16[192,1024]{1,0:T(8,128)(2,1)S(1)} %get-tuple-element.197), channel_id=1, source_target_pairs={{0,2},{1,3},{2,0},{3,1},{4,6},{5,7},{6,4},{7,5},{8,10},{9,11},{10,... | collective-permute-start | bytes 1179656 | tf_op jit(solution)/shard_map/ppermute | solution.py:764
  219.6 3.5 %collective-permute-start.34 = (bf16[384,2048]{1,0:T(8,128)(2,1)S(1)}, bf16[384,2048]{1,0:T(8,128)(2,1)S(1)}, u32[]{:S(2)}, u32[]{:S(2)}) collective-permute-start(bf16[384,2048]{1,0:T(8,128)(2,1)S(1)} %get-tuple-element.200), channel_id=1, source_target_pairs={{0,1},{1,0},{2,3},{3,2},{4,5},{5,4},{6,7},{7,6},{8,9},{9,8},{10,11... | collective-permute-start | bytes 4718600 | tf_op jit(solution)/shard_map/ppermute | solution.py:760
  220.9 8.9 %copy-start.30 = (bf16[96,1536]{1,0:T(8,128)(2,1)S(1)}, bf16[96,1536]{1,0:T(8,128)(2,1)}, u32[]{:S(2)}) copy-start(bf16[96,1536]{1,0:T(8,128)(2,1)} %copy-done.29) | copy-start | bytes 884740
  224.2 1.2 collective-permute-start.36
  225.4 3.7 %collective-permute-start.37 = (f32[1,1664]{1,0:T(1,128)S(1)}, f32[1,1664]{1,0:T(1,128)S(1)}, u32[]{:S(2)}, u32[]{:S(2)}) collective-permute-start(f32[1,1664]{1,0:T(1,128)S(1)} %add.134), channel_id=1, source_target_pairs={{0,2},{1,3},{2,0},{3,1},{4,6},{5,7},{6,4},{7,5},{8,10},{9,11},{10,... | collective-permute-start | bytes 19976 | tf_op jit(solution)/shard_map/ppermute | solution.py:764
  229.1 3.7 %collective-permute-start.38 = (f32[1,1664]{1,0:T(1,128)S(1)}, f32[1,1664]{1,0:T(1,128)S(1)}, u32[]{:S(2)}, u32[]{:S(2)}) collective-permute-start(f32[1,1664]{1,0:T(1,128)S(1)} %add.135), channel_id=1, source_target_pairs={{0,4},{4,0},{8,12},{12,8},{16,20},{20,16},{24,28},{28,24},{1,5},{5... | collective-permute-start | bytes 19976 | tf_op jit(solution)/shard_map/ppermute | solution.py:769
  229.8 4.0 %copy-start.35 = (bf16[96,768]{1,0:T(8,128)(2,1)S(1)}, bf16[96,768]{1,0:T(8,128)(2,1)}, u32[]{:S(2)}) copy-start(bf16[96,768]{1,0:T(8,128)(2,1)} %get-tuple-element.255) | copy-start | bytes 442372
  229.8 5.4 %copy-start.34 = (bf16[96,768]{1,0:T(8,128)(2,1)S(1)}, bf16[96,768]{1,0:T(8,128)(2,1)}, u32[]{:S(2)}) copy-start(bf16[96,768]{1,0:T(8,128)(2,1)} %get-tuple-element.256) | copy-start | bytes 442372
  229.8 7.4 %copy-start.33 = (bf16[96,768]{1,0:T(8,128)(2,1)S(1)}, bf16[96,768]{1,0:T(8,128)(2,1)}, u32[]{:S(2)}) copy-start(bf16[96,768]{1,0:T(8,128)(2,1)} %get-tuple-element.257) | copy-start | bytes 442372
  229.8 9.6 %copy-start.28 = (bf16[192,1024]{1,0:T(8,128)(2,1)S(1)}, bf16[192,1024]{1,0:T(8,128)(2,1)}, u32[]{:S(2)}) copy-start(bf16[192,1024]{1,0:T(8,128)(2,1)} %copy-done.27) | copy-start | bytes 1179652
  232.8 5.3 %collective-permute-start.39 = (f32[1,1664]{1,0:T(1,128)S(1)}, f32[1,1664]{1,0:T(1,128)S(1)}, u32[]{:S(2)}, u32[]{:S(2)}) collective-permute-start(f32[1,1664]{1,0:T(1,128)S(1)} %add.136), channel_id=1, source_target_pairs={{0,8},{4,12},{8,0},{12,4},{16,24},{20,28},{24,16},{28,20},{1,9},{5... | collective-permute-start | bytes 19976 | tf_op jit(solution)/shard_map/ppermute | solution.py:769
  233.7 14.6 %collective-permute-start.43 = (bf16[96,768]{1,0:T(8,128)(2,1)S(1)}, bf16[96,768]{1,0:T(8,128)(2,1)S(1)}, u32[]{:S(2)}, u32[]{:S(2)}) collective-permute-start(bf16[96,768]{1,0:T(8,128)(2,1)S(1)} %copy-done.35), channel_id=1, source_target_pairs={{0,24},{4,28},{8,16},{12,20},{16,8},{20,12},{24,0},{28,4},{1,25},{... | collective-permute-start | bytes 442376 | tf_op jit(solution)/shard_map/ppermute | solution.py:769
  235.2 13.1 %collective-permute-start.42 = (bf16[96,768]{1,0:T(8,128)(2,1)S(1)}, bf16[96,768]{1,0:T(8,128)(2,1)S(1)}, u32[]{:S(2)}, u32[]{:S(2)}) collective-permute-start(bf16[96,768]{1,0:T(8,128)(2,1)S(1)} %copy-done.34), channel_id=1, source_target_pairs={{0,16},{4,20},{8,24},{12,28},{16,0},{20,4},{24,8},{28,12},{1,17},{... | collective-permute-start | bytes 442376 | tf_op jit(solution)/shard_map/ppermute | solution.py:769
  237.2 11.1 %collective-permute-start.41 = (bf16[96,768]{1,0:T(8,128)(2,1)S(1)}, bf16[96,768]{1,0:T(8,128)(2,1)S(1)}, u32[]{:S(2)}, u32[]{:S(2)}) collective-permute-start(bf16[96,768]{1,0:T(8,128)(2,1)S(1)} %copy-done.33), channel_id=1, source_target_pairs={{0,8},{4,12},{8,0},{12,4},{16,24},{20,28},{24,16},{28,20},{1,9},{5... | collective-permute-start | bytes 442376 | tf_op jit(solution)/shard_map/ppermute | solution.py:769
  238.1 10.1 %collective-permute-start.40 = (f32[1,1664]{1,0:T(1,128)S(1)}, f32[1,1664]{1,0:T(1,128)S(1)}, u32[]{:S(2)}, u32[]{:S(2)}) collective-permute-start(f32[1,1664]{1,0:T(1,128)S(1)} %add.137), channel_id=1, source_target_pairs={{0,16},{4,20},{8,24},{12,28},{16,0},{20,4},{24,8},{28,12},{1,17},{... | collective-permute-start | bytes 19976 | tf_op jit(solution)/shard_map/ppermute | solution.py:769
  240.5 16.0 %collective-permute-start.35 = (bf16[192,2048]{1,0:T(8,128)(2,1)S(1)}, bf16[192,2048]{1,0:T(8,128)(2,1)}, u32[]{:S(2)}, u32[]{:S(2)}) collective-permute-start(bf16[192,2048]{1,0:T(8,128)(2,1)S(1)} %add_convert_fusion), channel_id=1, source_target_pairs={{0,2},{1,3},{2,0},{3,1},{4,6},{5,7},{6,4},{7,5},{8,10},{9,11},{10,... | collective-permute-start | bytes 2359304 | tf_op jit(solution)/shard_map/ppermute | solution.py:764
  (20 other events, 27.4 us)

commit v4 on v3

--- a/solution.py
+++ b/solution.py
@@ -299,7 +299,7 @@
         scratch.append(pltpu.VMEM((1, d, lanes), bf16))
     counts = tuple(len(part) for part in sources)
     for part in sources:
-        args += part
+        args += [keep_in_hbm(t) for t in part]
         in_specs += any_specs(part)
     return pl.pallas_call(
         functools.partial(head_kernel, tables, counts, rows, share, first_shard, sub, chunk),
@@ -401,7 +401,9 @@
     def _():
         wait_all(copies)
 
-    back_ref[...], mlp_ref[...] = feed_half(normed, grad, buf, acc, i == 0)
+    back, out = feed_half(normed, grad, buf, acc, i == 0)
+    back_ref[...] = back.astype(bf16)
+    mlp_ref[...] = out.astype(bf16)
 
     @pl.when(i == pl.num_programs(0) - 1)
     def _():
@@ -421,8 +423,8 @@
         load_blocks(table, sources, buf, s_ref[WIDE], rows, sem)
 
     back, out = feed_half(normed_ref[...], grad_ref[...], buf, acc, i == 0)
-    back_ref[...] = (before_ref[...] + back).astype(bf16)
-    store_quarters(s_ref[NARROW], mlp_ref[...] + out, keep_ref, send_ref)
+    back_ref[...] = (before_ref[...].astype(f32) + back).astype(bf16)
+    store_quarters(s_ref[NARROW], mlp_ref[...].astype(f32) + out, keep_ref, send_ref)
 
     @pl.when(i == pl.num_programs(0) - 1)
     def _():
@@ -449,8 +451,8 @@
         out_shape = (
             jax.ShapeDtypeStruct((n, d), bf16),
             jax.ShapeDtypeStruct((n, d), bf16),
-            jax.ShapeDtypeStruct((n, d), f32),
-            jax.ShapeDtypeStruct((d, n), f32),
+            jax.ShapeDtypeStruct((n, d), bf16),
+            jax.ShapeDtypeStruct((d, n), bf16),
             jax.ShapeDtypeStruct((d // 2, n), f32),
             jax.ShapeDtypeStruct((1, LANES), f32),
         )
@@ -478,7 +480,7 @@
         compiler_params=params(FEED_VMEM),
         cost_estimate=cost(2 * n * d * width * 3, 10 * n * d, n * width // 3),
         name="feed_forward",
-    )(scalars, *[keep_in_hbm(x) for x in inputs], *sources)
+    )(scalars, *[keep_in_hbm(x) for x in (*inputs, *sources)])
 
 
 def mid_kernel(
@@ -539,8 +541,8 @@
             mid_kernel, (own[0], other[0]), (len(own[1]), len(other[1])), rows, 2 * n // UNIT
         ),
         out_shape=(
-            jax.ShapeDtypeStruct((d, n), f32),
-            jax.ShapeDtypeStruct((n, lanes), bf16),
+            pltpu.HBM((d, n), f32),
+            pltpu.HBM((n, lanes), bf16),
             jax.ShapeDtypeStruct((n, lanes), bf16),
             jax.ShapeDtypeStruct((2, d, lanes), f32),
             jax.ShapeDtypeStruct((1, d), f32),
@@ -568,15 +570,16 @@
         compiler_params=params(MID_VMEM),
         cost_estimate=cost(8 * n * d * lanes, 16 * n * d),
         name="mid_backward",
-    )(scalars, *[keep_in_hbm(t) for t in (patches, a, b, g, h, cot)], gain, *o, *own[1], *other[1])
+    )(scalars, *[keep_in_hbm(t) for t in (patches, a, b, g, h, cot)], gain, *o, *[keep_in_hbm(t) for t in (*own[1], *other[1])])
 
 
 def head_back_kernel(
-    table, n_out, rows, share, chunk, s_ref, q_ref, k_ref, v_ref, do_ref, o_ref, aux_ref, dwo_ref, normed_ref, *refs
+    in_table, n_src, table, n_out, rows, share, chunk, s_ref, q_ref, k_ref, v_ref, do_ref, o_ref, aux_ref, dwo_ref, gain_ref, normed_ref, *refs
 ):
-    dq_out, dk_out, dv_out = refs[:3]
-    targets = refs[3 : 3 + n_out]
-    normed, dq_buf, dk_buf, dv_buf, pack, sem = refs[3 + n_out :]
+    sources = refs[:n_src]
+    dq_out, dk_out, dv_out, gain_out = refs[n_src : n_src + 4]
+    targets = refs[n_src + 4 : n_src + 4 + n_out]
+    normed, dq_buf, dk_buf, dv_buf, pack, weights, sem, load_sem = refs[n_src + 4 + n_out :]
     heads = head_list(share)
     lane, first, second = lane_halves()
     in_first = lane < HEAD_DIM
@@ -584,6 +587,7 @@
     units = n // UNIT
     load = pltpu.make_async_copy(normed_ref, normed, sem.at[0])
     load.start()
+    loads = start_all(block_copies(in_table, sources, weights, s_ref[WIDE], rows, load_sem))
     minus = [
         -((lane >= 64) & (lane < 67)).astype(f32).astype(bf16),
         -(lane < 3).astype(f32).astype(bf16),
@@ -637,10 +641,16 @@
     pack[0, :, 2 * share : 3 * share] = both[:, 0:share]
     pack[0, :, 3 * share : 4 * share] = both[:, dk_buf.shape[1] : dk_buf.shape[1] + share]
     store_blocks(table, pack, targets, s_ref[WIDE], rows)
+    wait_all(loads)
+    product = weights[0, :, share : 4 * share].astype(f32) * pack[0, :, share : 4 * share]
+    row_sum = jnp.sum(product, axis=1, keepdims=True)
+    gain_out[...] = jnp.broadcast_to(row_sum, (row_sum.shape[0], LANES)).T[:1, :] / gain_ref[...]
     wait_all(copies)
 
 
-def head_backward(scalars, q, k, v, do, o, aux, dwo, which, normed, out, rows, share, chunk=512):
+def head_backward(
+    scalars, q, k, v, do, o, aux, dwo, which, gain, normed, weights, out, rows, share, chunk=512
+):
     n, d = normed.shape
     n_q, lanes = q.shape
     out_table, out_leads = out
@@ -649,32 +659,43 @@
     q_spec, k_spec = once((n_q, lanes)), once((n, lanes))
     any_spec = pl.BlockSpec(memory_space=pl.ANY)
     return pl.pallas_call(
-        functools.partial(head_back_kernel, out_table, len(blocks), rows, share, chunk),
-        out_shape=tuple(jax.ShapeDtypeStruct(shape, bf16) for shape in shapes + blocks),
+        functools.partial(
+            head_back_kernel, weights[0], len(weights[1]), out_table, len(blocks), rows, share, chunk
+        ),
+        out_shape=tuple(jax.ShapeDtypeStruct(shape, bf16) for shape in shapes)
+        + (jax.ShapeDtypeStruct((1, d), f32),)
+        + tuple(jax.ShapeDtypeStruct(shape, bf16) for shape in blocks),
         grid_spec=pltpu.PrefetchScalarGridSpec(
             num_scalar_prefetch=1,
             grid=(1,),
             in_specs=[q_spec, k_spec, k_spec, q_spec, q_spec, q_spec]
             + [
                 pl.BlockSpec((1, d, lanes), lambda i, s: (which, 0, 0), pipeline_mode=pl.Buffered(1)),
+                once((1, d)),
                 any_spec,
-            ],
-            out_specs=[any_spec] * 3 + [once(block) for block in blocks],
+            ]
+            + any_specs(weights[1]),
+            out_specs=[any_spec] * 3 + [once((1, d))] + [once(block) for block in blocks],
             scratch_shapes=[pltpu.VMEM((n, d), bf16)]
             + [pltpu.VMEM(shape, bf16) for shape in shapes]
-            + [pltpu.VMEM((1, d, 4 * share), f32), pltpu.SemaphoreType.DMA((4,))],
+            + [
+                pltpu.VMEM((1, d, 4 * share), f32),
+                pltpu.VMEM((1, d, 4 * share), bf16),
+                pltpu.SemaphoreType.DMA((4,)),
+                pltpu.SemaphoreType.DMA((len(weights[0]),)),
+            ],
         ),
         compiler_params=params(BACK_VMEM),
         cost_estimate=cost(20 * n * n * share, 8 * n * d, n * n * share // 128),
         name="head_backward",
-    )(scalars, *[keep_in_hbm(t) for t in (q, k, v, do, o, aux, dwo)], normed)
+    )(scalars, *[keep_in_hbm(t) for t in (q, k, v)], do, o, keep_in_hbm(aux), dwo, gain, *[keep_in_hbm(t) for t in (normed, *weights[1])])
 
 
 def last_kernel(tables, counts, rows, share, s_ref, x_ref, gain_ref, gm_ref, *refs):
     grads = refs[:6]
     refs = refs[6:]
     sources = [refs[: counts[0]], refs[counts[0] : sum(counts)]]
-    keep_ref, send_ref, gain_out, buf, weights, total, gain, sem = refs[sum(counts) :]
+    keep_ref, send_ref, buf, weights, gain, sem = refs[sum(counts) :]
     i = pl.program_id(0)
     half = pl.num_programs(0) // 2
     d = x_ref.shape[1]
@@ -688,7 +709,6 @@
                 weights[3 * at + j] = padded(
                     buf[at, :, (j + 1) * share : (j + 2) * share], weights.shape[2]
                 )
-        total[...] = jnp.zeros_like(total)
         gain[...] = jnp.broadcast_to(gain_ref[...], (LANES, d)).T[:, :1]
 
     mine = i // half == s_ref[X_HALF]
@@ -703,15 +723,10 @@
                 value = jnp.where(mine, value.astype(f32), 0.0).astype(bf16)
             part = mm(weights[3 * at + j], value, NT)
             back = part if back is None else back + part
-    total[...] += jnp.sum(back * hat, axis=1, keepdims=True)
     scaled = back * gain[...]
     mean = jnp.mean(scaled * hat, axis=0, keepdims=True)
     grad = scale * (scaled - hat * mean) + jnp.where(mine, 0.5, 0.0) * gm_ref[...]
     store_quarters(s_ref[NARROW], grad, keep_ref, send_ref)
-
-    @pl.when(i == pl.num_programs(0) - 1)
-    def _():
-        gain_out[...] = jnp.broadcast_to(total[...], (d, LANES)).T[:1, :]
 
 
 def last_backward(scalars, patches, gain, gm_t, grads, own, other, rows, share, tile=512):
@@ -728,7 +743,6 @@
         out_shape=(
             jax.ShapeDtypeStruct((d // 2, n), bf16),
             jax.ShapeDtypeStruct((d // 2, n), bf16),
-            jax.ShapeDtypeStruct((1, d), f32),
         ),
         grid_spec=pltpu.PrefetchScalarGridSpec(
             num_scalar_prefetch=1,
@@ -741,11 +755,10 @@
             + [own_spec, key_spec, key_spec] * 2
             + any_specs(own[1])
             + any_specs(other[1]),
-            out_specs=[half_spec, half_spec, once((1, d))],
+            out_specs=[half_spec, half_spec],
             scratch_shapes=[
                 pltpu.VMEM((2, d, width), bf16),
                 pltpu.VMEM((6, d, lanes), bf16),
-                pltpu.VMEM((d, 1), f32),
                 pltpu.VMEM((d, 1), f32),
                 pltpu.SemaphoreType.DMA((2, len(own[0]))),
             ],
@@ -753,7 +766,7 @@
         compiler_params=params(LAST_VMEM),
         cost_estimate=cost(2 * n * d * lanes * 5, 10 * n * d),
         name="last_backward",
-    )(scalars, patches, gain, gm_t, *grads, *own[1], *other[1])
+    )(scalars, patches, gain, gm_t, *grads, *[keep_in_hbm(t) for t in (*own[1], *other[1])])
 
 
 def swap_core(value):
@@ -808,16 +821,6 @@
 
 def total(*terms):
     return functools.reduce(jnp.add, [t.astype(f32) for t in terms])
-
-
-def sum_all(value):
-    if not small_slice():
-        return lax.psum(value, ("wide", "narrow"))
-    value = value + swap_core(value)
-    value = value + swap_x(value)
-    for offset in (1, 2, 4):
-        value = value + swap_wide(value, offset)
-    return value
 
 
 def reduce_whole(part):
@@ -869,16 +872,15 @@
         first = [swap_wide(head_shard, 2 * z) for z in (1, 2, 3)]
         first += [swap_wide(head_shard, 1), swap_x(head_shard)]
         ff_early = after(ff_shard, head_shard)
-        first += [swap_wide(ff_early, 1), swap_x(ff_early)]
-        z1, z2, z4, y0, x0, ff_y0, ff_x0 = lax.optimization_barrier(first)
+        first += [swap_wide(ff_early, 1), swap_x(ff_early), swap_x(first[3])]
+        z1, z2, z4, y0, x0, ff_y0, ff_x0, corner = lax.optimization_barrier(first)
         z3 = jnp.concatenate([z1, z2, z4])
         y3, x3 = swap_wide(z3, 1), swap_x(z3)
-        corner = swap_wide(x0, 1)
         own = (OWN_TABLE, [head_shard, z3, y0, y3])
         other = (OTHER_TABLE, [x0, x3, corner, swap_x(y3)])
         ff_late = after(ff_shard, z3)
         ff_z = [swap_wide(ff_late, 2 * z) for z in (1, 2, 3)]
-        early = (y3, corner)
+        early = (y3,)
         own_out = (COLUMN_TABLE, (4, 4))
         other_out = (FLAT_TABLE, (8,))
         ff_out = (FF_COLUMN_TABLE, (4, 2, 2))
@@ -930,8 +932,8 @@
         to_y, to_x = total(to_y, got_x).astype(bf16), total(to_x, got_y).astype(bf16)
         got_y, got_x = swap_wide(to_y, 1), swap_x(to_x)
         do1 = after(do1, to_y, to_x)
-    *grads1, head1 = head_backward(
-        scalars, q1, k1, v1, do1, o1, aux1, dwo, 1, normed, other_out, block, share
+    *grads1, gain1, head1 = head_backward(
+        scalars, q1, k1, v1, do1, o1, aux1, dwo, 1, gain_in, normed, other, other_out, block, share
     )
 
     mlp = total(mlp_keep, after(swap_core(after(mlp_send, do1)), head1))
@@ -961,47 +963,56 @@
         sent = [column[z].astype(bf16) for z in (1, 2, 3)]
         do0 = after(do0, *sent)
         back = [swap_wide(sent[z - 1], 2 * z) for z in (1, 2, 3)]
-    *grads0, head0, head0_y = head_backward(
-        scalars, q0, k0, v0, do0, o0, aux0, dwo, 0, normed, own_out, block, share
+    *grads0, gain0, head0, head0_y = head_backward(
+        scalars, q0, k0, v0, do0, o0, aux0, dwo, 0, gain_in, normed, own, own_out, block, share
     ) + (() if small else (None,))
     dq0, head1_other = lax.optimization_barrier((grads0[0], head1_other))
     if small:
         head_y = total(head0_y, head1_other[1::2]).astype(bf16)
         dq0, head_y, *back = lax.optimization_barrier((dq0, head_y, *back))
         head_y = swap_wide(head_y, 1)
-    grad_keep, grad_send, gain_in_sum = last_backward(
+    sums = jnp.concatenate([gain0 + gain1, stats], axis=1)
+    if small:
+        sums = sums + swap_core(sums)
+        dq0, sums = lax.optimization_barrier((dq0, sums))
+        sums_x = swap_x(sums)
+    grad_keep, grad_send = last_backward(
         scalars, values, gain_in, gm_t, [dq0, *grads0[1:], *grads1], own, other, block, share
     )
 
     if small:
-        grad_keep, grad_send, gain_in_sum, head_y, layer_got = lax.optimization_barrier(
-            (grad_keep, grad_send, gain_in_sum, head_y, layer_got)
+        grad_keep, grad_send, sums_x, head_y, layer_got = lax.optimization_barrier(
+            (grad_keep, grad_send, sums_x, head_y, layer_got)
         )
+        sums = sums + sums_x
+        ff_own = total(column[0], *back)
+    output = jnp.where(
+        x_half == 0,
+        jnp.concatenate([layer_mine, layer_got], axis=1),
+        jnp.concatenate([layer_got, layer_mine], axis=1),
+    )
     grad_got = swap_core(grad_send)
     grad_sent = total(grad_keep[quarter:], grad_got[quarter:]).astype(bf16)
     if small:
+        sums = sums + swap_wide(sums, 1)
         head_column = total(head0, head1_other[::2], head_y)
         head_sent = [head_column[z].astype(bf16) for z in (1, 2, 3)]
-        gain_in_sum, grad_sent = lax.optimization_barrier(
-            (gain_in_sum, grad_sent, *head_sent)
-        )[:2]
+        grad_sent, sums, *head_sent, output, ff_own = lax.optimization_barrier(
+            (grad_sent, sums, *head_sent, output, ff_own)
+        )
+        grad_other = swap_x(grad_sent)
         head_got = [swap_wide(head_sent[z - 1], 2 * z) for z in (1, 2, 3)]
-        ff_own = total(column[0], *back)
+        sums_got = [swap_wide(sums, 2 * z) for z in (1, 2, 3)]
+        grad_other, *got = lax.optimization_barrier((grad_other, *head_got, *sums_got))
+        head_own = total(head_column[0], *got[:3])
+        sums = total(sums, *got[3:])
     else:
         both = total(ff_own_grads[0][0], swap_x(ff_other_grads[0][0])).astype(bf16)
         ff_own = reduce_whole(both)
         head_own = reduce_whole(total(head0[0], head1_other[0]).astype(bf16))
-    output = jnp.where(
-        x_half == 0,
-        jnp.concatenate([layer_mine, layer_got], axis=1),
-        jnp.concatenate([layer_got, layer_mine], axis=1),
-    )
-    grad_patches = total(grad_keep[:quarter], grad_got[:quarter], swap_x(grad_sent))
-
-    sums = sum_all(jnp.concatenate([gain_in_sum, stats], axis=1))
-    if small:
-        sums, *head_got = lax.optimization_barrier((sums, *head_got))
-        head_own = total(head_column[0], *head_got)
+        grad_other = swap_x(grad_sent)
+        sums = lax.psum(sums, ("wide", "narrow"))
+    grad_patches = total(grad_keep[:quarter], grad_got[:quarter], grad_other)
     sums = sums[0]
     total_in, total_mid, totals = sums[:d], sums[d : 2 * d], sums[2 * d : 2 * d + 4]
     rms_values = jnp.sqrt(totals[:3] / (totals[3] * d))

time: 264 us -> 254 us (0.962)
  waiting for transfers between devices: 34.6 us -> 22.7 us
  Pallas kernels: 134 us -> 137 us
    ppermute x13 -> x14, waiting for transfers between devices: 5.79 us -> 0.41 us  [swap_x(): return lax.ppermute(value, 'narrow', [(i, i ^ 2) for i in range(4)])]
    pallas_call x1, Pallas kernels: 8.22 us -> 12 us  [mid_backward(): pl.pallas_call(functools.partial(mid_kernel, (own[0], other[0]), (len(own...]
    ppermute x5, waiting for transfers between devices: 3.29 us -> 0.01 us  [swap_core(): return lax.ppermute(value, 'narrow', [(i, i ^ 1) for i in range(4)])]
    ppermute x26, waiting for transfers between devices: 25.5 us -> 22.3 us  [swap_wide(): return lax.ppermute(value, 'wide', [(i, i ^ offset) for i in range(n)])]
    unnamed x89 -> x106, local copies, waits for them, and re-layouts: 19.2 us -> 18.7 us
    ppermute x13 -> x14, starting transfers between devices: 15.4 us -> 15.7 us  [swap_x(): return lax.ppermute(value, 'narrow', [(i, i ^ 2) for i in range(4)])]
  transfers between devices with their start and end apart: 44 -> 45, of which waited for: 13 -> 10; matrix products, arithmetic and copies ran while one was open for 7% -> 5% of each run, Pallas kernels for 46% -> 49%
where the time goes in v4:
time: 254 us; the launch traced here: 249 us
  Pallas kernels  137 us (54%)
  starting transfers between devices  48.5 us (19%)
  waiting for transfers between devices  22.7 us (9%)
  local copies, waits for them, and re-layouts  22.5 us (9%)
  other arithmetic  15.7 us (6%)
  between operations  3.01 us (1%)
    pallas_call x2, Pallas kernels, head_backward(): pl.pallas_call(functools.partial(head_back_kernel, weights[0], len(weight...  45.2 us
    ppermute x26, starting transfers between devices, swap_wide(): return lax.ppermute(value, 'wide', [(i, i ^ offset) for i in range(n)])  32.6 us
    pallas_call x2, Pallas kernels, head_forward(): pl.pallas_call(functools.partial(head_kernel, tables, counts, rows, share...  32.1 us
    pallas_call x2, Pallas kernels, feed_forward(): pl.pallas_call(kernel, out_shape=out_shape + block_shapes, grid_spec=pltp...  31.8 us
    ppermute x26, waiting for transfers between devices, swap_wide(): return lax.ppermute(value, 'wide', [(i, i ^ offset) for i in range(n)])  22.3 us
    unnamed x106, local copies, waits for them, and re-layouts  18.7 us
    ppermute x14, starting transfers between devices, swap_x(): return lax.ppermute(value, 'narrow', [(i, i ^ 2) for i in range(4)])  15.7 us
    pallas_call x1, Pallas kernels, last_backward(): pl.pallas_call(functools.partial(last_kernel, (own[0], other[0]), (len(ow...  15.6 us
  transfers between devices with their start and end apart: 45, of which 10 were waited for; matrix products, arithmetic and copies ran while one was open for 5% of the time, Pallas kernels for 49%

profile of v4, /device:TPU:0, one launch (start us, length us, event | category | flops | bytes accessed | tf_op | source)
XLA Modules:
  0.0 249.1 jit_solution(10924732103312747699)
XLA Ops:
  0.7 0.9 copy.27
  1.6 1.0 maximum_bitcast_fusion.1.refs_0_.refs_5_.refs_6_
  2.6 3.0 %collective-permute-start.4 = (bf16[1,96,768]{2,1,0:T(8,128)(2,1)S(1)}, bf16[1,96,768]{2,1,0:T(8,128)(2,1)S(1)}, u32[]{:S(2)}, u32[]{:S(2)}) collective-permute-start(bf16[1,96,768]{2,1,0:T(8,128)(2,1)S(1)} %maximum_bitcast_fusion.1.refs_0_.refs_5_.refs_6_), channel_id=1, source_target_pairs={{0,2},{1,3},{2,0},{3,1},{4,6},{5,7},{6,4},{7,5},{8,10},{9,11},{10,... | collective-permute-start | bytes 442376 | tf_op jit(solution)/shard_map/ppermute | solution.py:777
  5.6 1.5 collective-permute-start.3
  7.1 3.6 %collective-permute-start.2 = (bf16[1,96,768]{2,1,0:T(8,128)(2,1)S(1)}, bf16[1,96,768]{2,1,0:T(8,128)(2,1)S(1)}, u32[]{:S(2)}, u32[]{:S(2)}) collective-permute-start(bf16[1,96,768]{2,1,0:T(8,128)(2,1)S(1)} %maximum_bitcast_fusion.1.refs_0_.refs_5_.refs_6_), channel_id=1, source_target_pairs={{0,24},{4,28},{8,16},{12,20},{16,8},{20,12},{24,0},{28,4},{1,25},{... | collective-permute-start | bytes 442376 | tf_op jit(solution)/shard_map/ppermute | solution.py:782
  10.7 1.0 maximum_bitcast_fusion.refs_0_
  12.9 1.0 collective-permute-start
  13.8 1.2 collective-permute-done.2
  15.0 0.8 collective-permute-start.7
  15.9 6.8 %collective-permute-done.1 = bf16[1,96,768]{2,1,0:T(8,128)(2,1)S(1)} collective-permute-done((bf16[1,96,768]{2,1,0:T(8,128)(2,1)S(1)}, bf16[1,96,768]{2,1,0:T(8,128)(2,1)S(1)}, u32[]{:S(2)}, u32[]{:S(2)}) %collective-permute-start.1) | collective-permute-done | bytes 147488 | tf_op jit(solution)/shard_map/ppermute | solution.py:782
  25.7 2.4 collective-permute-start.11
  28.1 2.4 collective-permute-start.10
  31.3 2.6 %collective-permute-done.8.refs_3_.refs_8_.refs_9_ = bf16[3,96,768]{2,1,0:T(8,128)(2,1)S(1)} collective-permute-done((bf16[3,96,768]{2,1,0:T(8,128)(2,1)S(1)}, bf16[3,96,768]{2,1,0:T(8,128)(2,1)S(1)}, u32[]{:S(2)}, u32[]{:S(2)}) %collective-permute-start.8) | collective-permute-done | bytes 442400 | tf_op jit(solution)/shard_map/ppermute | solution.py:782
  34.8 1.9 copy-done
  36.7 16.4 %head_forward.2 = (bf16[2048,768]{1,0:T(8,128)(2,1)S(1)}, bf16[1024,256]{1,0:T(8,128)(2,1)S(1)}, bf16[2048,256]{1,0:T(8,128)(2,1)S(1)}, bf16[2048,256]{1,0:T(8,1...) custom-call(s32[11]{0:T(128)S(1)} %concatenate.33.s_ref, bf16[2048,768]{1,0:T(8,128)(2,1)S(1)} %copy-done, ...), custom_call_target="tpu_custom_call" | custom-call | flops 8053063680 | bytes 12582912 | tf_op jit(solution)/shard_map/head_forward/pallas_call | solution.py:304
  53.1 1.0 copy-done.13
  54.3 1.3 collective-permute-start.13
  57.7 15.7 %head_forward.3 = (bf16[1024,256]{1,0:T(8,128)(2,1)S(1)}, bf16[2048,256]{1,0:T(8,128)(2,1)S(1)}, bf16[2048,256]{1,0:T(8,128)(2,1)S(1)}, bf16[1024,256]{1,0:T(8,1...) custom-call(s32[11]{0:T(128)S(1)} %concatenate.33.s_ref, ...), custom_call_target="tpu_custom_call" | custom-call | flops 8053063680 | bytes 12582912 | tf_op jit(solution)/shard_map/head_forward/pallas_call | solution.py:304
  73.4 1.0 copy-done.11
  74.4 1.0 copy-done.12
  75.4 0.8 copy-done.15
  77.1 1.6 collective-permute-start.19
  79.2 1.3 collective-permute-start.18
  80.6 1.2 copy-done.19
  81.8 16.6 %feed_forward.2 = (bf16[1024,768]{1,0:T(8,128)(2,1)S(1)}, bf16[1024,768]{1,0:T(8,128)(2,1)S(1)}, bf16[1024,768]{1,0:T(8,128)(2,1)S(1)}, bf16[768,1024]{1,0:T(8,1...) custom-call(s32[11]{0:T(128)S(1)} %concatenate.33.s_ref, ...), custom_call_target="tpu_custom_call" | custom-call | flops 7247757312 | bytes 7864320 | tf_op jit(solution)/shard_map/feed_forward/pallas_call | solution.py:470
  98.4 1.2 copy-done.6
  99.6 1.1 copy-done.7
  100.7 1.2 copy-done.8
  101.9 1.1 copy-done.9
  104.1 15.2 %feed_forward.3 = (bf16[1024,768]{1,0:T(8,128)(2,1)S(1)}, bf16[384,1024]{1,0:T(8,128)(2,1)S(1)}, bf16[384,1024]{1,0:T(8,128)(2,1)S(1)}, bf16[2,96,1536]{2,1,0:T(...) custom-call(s32[11]{0:T(128)S(1)} %concatenate.33.s_ref, ...), custom_call_target="tpu_custom_call" | custom-call | flops 7247757312 | bytes 7864320 | tf_op jit(solution)/shard_map/feed_forward/pallas_call | solution.py:470
  119.5 1.3 collective-permute-start.21
  120.7 1.0 collective-permute-start.22
  121.8 1.1 collective-permute-start.27
  123.0 1.1 copy-done.20
  124.1 12.0 %mid_backward.1 = (f32[768,1024]{1,0:T(8,128)}, bf16[1024,256]{1,0:T(8,128)(2,1)}, bf16[1024,256]{1,0:T(8,128)(2,1)S(1)}, f32[2,768,256]{2,1,0:T(8,128)S(1)}, f32[1,768]{1,0:T(1,128)S(1)}) custom-call(s32[11]{0:T(128)S(1)} %concatenate.33.s_ref, bf16[2048,768]{1,0:T(8,128)(2,1)} %x_ref.3, bf16[1024,768]{1,0:T(8,128)(2,1)} %copy-done.2, ...), custom_call_target="tpu_custom_call" | custom-call | flops 1610612736 | bytes 12582912 | tf_op jit(solution)/shard_map/mid_backward/pallas_call | solution.py:539
  137.0 0.8 collective-permute-start.24
  138.0 1.6 collective-permute-start.25
  140.4 22.4 %head_backward.2 = (bf16[1024,256]{1,0:T(8,128)(2,1)S(1)}, bf16[2048,256]{1,0:T(8,128)(2,1)S(1)}, bf16[2048,256]{1,0:T(8,128)(2,1)S(1)}, f32[1,768]{1,0:T(1,128)S(1)}, bf16[8,96,768]{2,1,0:T(8,128)(2,1)S(1)}) custom-call(s32[11]{0:T(128)S(1)} %concatenate.33.s_ref, bf16[1024,256]{1,0:T(8,128)(2,1)} %copy-done.15, bf16[2048,256]{1,0:T(8,128)(2,1)} %copy-done.11, ...), custom_call_target="tpu_custom_call" | custom-call | flops 16106127360 | bytes 12582912 | tf_op jit(solution)/shard_map/head_backward/pallas_call | solution.py:661
  162.8 1.4 collective-permute-start.28
  164.2 1.9 fusion.13
  166.2 2.4 collective-permute-start.31
  168.6 2.0 collective-permute-start.29
  170.7 1.4 select_reduce_fusion
  172.1 1.4 maximum_bitcast_fusion.2
  173.6 22.7 %head_backward.3 = (bf16[1024,256]{1,0:T(8,128)(2,1)S(1)}, bf16[2048,256]{1,0:T(8,128)(2,1)S(1)}, bf16[2048,256]{1,0:T(8,128)(2,1)S(1)}, f32[1,768]{1,0:T(1,128)...) custom-call(s32[11]{0:T(128)S(1)} %concatenate.33.s_ref, bf16[1024,256]{1,0:T(8,128)(2,1)} %copy-done.17, ...), custom_call_target="tpu_custom_call" | custom-call | flops 16106127360 | bytes 12582912 | tf_op jit(solution)/shard_map/head_backward/pallas_call | solution.py:661
  196.5 1.2 collective-permute-start.35
  197.9 1.2 collective-permute-start.34
  199.1 1.2 collective-permute-start.33
  200.4 15.6 %last_backward.1 = (bf16[384,2048]{1,0:T(8,128)(2,1)S(1)}, bf16[384,2048]{1,0:T(8,128)(2,1)}) custom-call(s32[11]{0:T(128)S(1)} %concatenate.33.s_ref, bf16[2048,768]{1,0:T(8,128)(2,1)S(1)} %copy-done.1, f32[1,768]{1,0:T(1,128)S(1)} %broadcast_in_dim.34.gain_ref, f32[768,1024]{1,0:T(8,128)} %get-tuple-element.156.gm_ref, ...), custom_call_target="tpu_custom_call" | custom-call | flops 4026531840 | bytes 15728640 | tf_op jit(solution)/shard_map/last_backward/pallas_call | solution.py:741
  216.6 1.5 fusion.2
  218.9 1.2 maximum_select_fusion
  220.3 1.6 collective-permute-done.37
  221.9 1.4 add_convert_fusion
  223.3 0.9 collective-permute-start.38
  224.3 2.3 collective-permute-start.44
  226.6 2.1 collective-permute-start.42
  228.7 1.1 collective-permute-done.44
  229.8 1.7 collective-permute-start.40
  231.5 1.5 collective-permute-start.41
  233.0 0.8 slice_bitcast_fusion.5
  233.9 2.2 collective-permute-done.39
  236.1 6.0 %collective-permute-done.40 = bf16[96,768]{1,0:T(8,128)(2,1)S(1)} collective-permute-done((bf16[96,768]{1,0:T(8,128)(2,1)S(1)}, bf16[96,768]{1,0:T(8,128)(2,1)S(1)}, u32[]{:S(2)}, u32[]{:S(2)}) %collective-permute-start.40) | collective-permute-done | bytes 147488 | tf_op jit(solution)/shard_map/ppermute | solution.py:782
  244.7 0.8 slice_bitcast_fusion.9
  246.2 2.6 %add_bitcast_fusion = f32[2048,192]{0,1:T(8,128)} fusion(bf16[192,2048]{1,0:T(8,128)(2,1)S(1)} %collective-permute-done.38, bf16[384,2048]{1,0:T(8,128)(2,1)} %collective-permute-done.36, bf16[384,2048]{1,0:T(8,128)(2,1)S(1)} %get-tuple-element.214), kind=kLoop, calls=%fused_computation.1 | loop fusion | flops 1966080 | bytes 3932160 | tf_op jit(solution)/shard_map/transpose | solution.py:1021
  (181 shorter events, 16.6 us)
Async XLA Ops:
  0.6 22.9 %copy-start.40 = (f32[768]{0:T(1024)S(1)}, f32[768]{0:T(1024)}, u32[]{:S(2)}) copy-start(f32[768]{0:T(1024)} %param.14) | copy-start | bytes 9220
  0.7 22.9 %copy-start.41 = (f32[768]{0:T(1024)S(1)}, f32[768]{0:T(1024)}, u32[]{:S(2)}) copy-start(f32[768]{0:T(1024)} %param.15) | copy-start | bytes 9220
  0.7 23.4 %copy-start.43 = (s32[4]{0:T(128)S(1)}, s32[4]{0:T(128)}, u32[]{:S(2)}) copy-start(s32[4]{0:T(128)} %param.25) | copy-start | bytes 52
  0.7 23.5 %copy-start.42 = (s32[4]{0:T(128)S(1)}, s32[4]{0:T(128)}, u32[]{:S(2)}) copy-start(s32[4]{0:T(128)} %param.24) | copy-start | bytes 52
  2.6 32.0 %copy-start.25 = (bf16[1,96,768]{2,1,0:T(8,128)(2,1)}, bf16[1,96,768]{2,1,0:T(8,128)(2,1)S(1)}, u32[]{:S(2)}) copy-start(bf16[1,96,768]{2,1,0:T(8,128)(2,1)S(1)} %maximum_bitcast_fusion.1.refs_0_.refs_5_.refs_6_) | copy-start | bytes 442372
  2.6 10.3 %collective-permute-start.4 = (bf16[1,96,768]{2,1,0:T(8,128)(2,1)S(1)}, bf16[1,96,768]{2,1,0:T(8,128)(2,1)S(1)}, u32[]{:S(2)}, u32[]{:S(2)}) collective-permute-start(bf16[1,96,768]{2,1,0:T(8,128)(2,1)S(1)} %maximum_bitcast_fusion.1.refs_0_.refs_5_.refs_6_), channel_id=1, source_target_pairs={{0,2},{1,3},{2,0},{3,1},{4,6},{5,7},{6,4},{7,5},{8,10},{9,11},{10,... | collective-permute-start | bytes 442376 | tf_op jit(solution)/shard_map/ppermute | solution.py:777
  5.6 7.3 %collective-permute-start.3 = (bf16[1,96,768]{2,1,0:T(8,128)(2,1)S(1)}, bf16[1,96,768]{2,1,0:T(8,128)(2,1)S(1)}, u32[]{:S(2)}, u32[]{:S(2)}) collective-permute-start(bf16[1,96,768]{2,1,0:T(8,128)(2,1)S(1)} %maximum_bitcast_fusion.1.refs_0_.refs_5_.refs_6_), channel_id=1, source_target_pairs={{0,4},{4,0},{8,12},{12,8},{16,20},{20,16},{24,28},{28,24},{1,5},{5... | collective-permute-start | bytes 442376 | tf_op jit(solution)/shard_map/ppermute | solution.py:782
  7.1 7.9 %collective-permute-start.2 = (bf16[1,96,768]{2,1,0:T(8,128)(2,1)S(1)}, bf16[1,96,768]{2,1,0:T(8,128)(2,1)S(1)}, u32[]{:S(2)}, u32[]{:S(2)}) collective-permute-start(bf16[1,96,768]{2,1,0:T(8,128)(2,1)S(1)} %maximum_bitcast_fusion.1.refs_0_.refs_5_.refs_6_), channel_id=1, source_target_pairs={{0,24},{4,28},{8,16},{12,20},{16,8},{20,12},{24,0},{28,4},{1,25},{... | collective-permute-start | bytes 442376 | tf_op jit(solution)/shard_map/ppermute | solution.py:782
  11.7 41.4 %copy-start.30 = (bf16[1,96,1536]{2,1,0:T(8,128)(2,1)}, bf16[1,96,1536]{2,1,0:T(8,128)(2,1)S(1)}, u32[]{:S(2)}) copy-start(bf16[1,96,1536]{2,1,0:T(8,128)(2,1)S(1)} %maximum_bitcast_fusion.refs_0_) | copy-start | bytes 884740
  11.7 11.1 %collective-permute-start.6 = (bf16[1,96,1536]{2,1,0:T(8,128)(2,1)S(1)}, bf16[1,96,1536]{2,1,0:T(8,128)(2,1)S(1)}, u32[]{:S(2)}, u32[]{:S(2)}) collective-permute-start(bf16[1,96,1536]{2,1,0:T(8,128)(2,1)S(1)} %maximum_bitcast_fusion.refs_0_), channel_id=1, source_target_pairs={{0,2},{1,3},{2,0},{3,1},{4,6},{5,7},{6,4},{7,5},{8,10},{9,11},{10,... | collective-permute-start | bytes 884744 | tf_op jit(solution)/shard_map/ppermute | solution.py:777
  12.3 10.5 %collective-permute-start.5 = (bf16[1,96,1536]{2,1,0:T(8,128)(2,1)S(1)}, bf16[1,96,1536]{2,1,0:T(8,128)(2,1)S(1)}, u32[]{:S(2)}, u32[]{:S(2)}) collective-permute-start(bf16[1,96,1536]{2,1,0:T(8,128)(2,1)S(1)} %maximum_bitcast_fusion.refs_0_), channel_id=1, source_target_pairs={{0,4},{4,0},{8,12},{12,8},{16,20},{20,16},{24,28},{28,24},{1,5},{5... | collective-permute-start | bytes 884744 | tf_op jit(solution)/shard_map/ppermute | solution.py:782
  12.8 40.3 %copy-start.34 = (bf16[1,96,768]{2,1,0:T(8,128)(2,1)}, bf16[1,96,768]{2,1,0:T(8,128)(2,1)S(1)}, u32[]{:S(2)}) copy-start(bf16[1,96,768]{2,1,0:T(8,128)(2,1)S(1)} %collective-permute-done.4.refs_1_.refs_4_.refs_0_.refs_10_) | copy-start | bytes 442372
  12.8 9.8 %collective-permute-start.1 = (bf16[1,96,768]{2,1,0:T(8,128)(2,1)S(1)}, bf16[1,96,768]{2,1,0:T(8,128)(2,1)S(1)}, u32[]{:S(2)}, u32[]{:S(2)}) collective-permute-start(bf16[1,96,768]{2,1,0:T(8,128)(2,1)S(1)} %maximum_bitcast_fusion.1.refs_0_.refs_5_.refs_6_), channel_id=1, source_target_pairs={{0,16},{4,20},{8,24},{12,28},{16,0},{20,4},{24,8},{28,12},{1,17},{... | collective-permute-start | bytes 442376 | tf_op jit(solution)/shard_map/ppermute | solution.py:782
  12.8 21.7 %copy-start.35 = (bf16[1,96,768]{2,1,0:T(8,128)(2,1)}, bf16[1,96,768]{2,1,0:T(8,128)(2,1)S(1)}, u32[]{:S(2)}) copy-start(bf16[1,96,768]{2,1,0:T(8,128)(2,1)S(1)} %collective-permute-done.3.refs_2_.refs_7_.refs_8_) | copy-start | bytes 442372
  12.9 9.8 %collective-permute-start = (bf16[1,96,768]{2,1,0:T(8,128)(2,1)S(1)}, bf16[1,96,768]{2,1,0:T(8,128)(2,1)S(1)}, u32[]{:S(2)}, u32[]{:S(2)}) collective-permute-start(bf16[1,96,768]{2,1,0:T(8,128)(2,1)S(1)} %maximum_bitcast_fusion.1.refs_0_.refs_5_.refs_6_), channel_id=1, source_target_pairs={{0,8},{4,12},{8,0},{12,4},{16,24},{20,28},{24,16},{28,20},{1,9},{5... | collective-permute-start | bytes 442376 | tf_op jit(solution)/shard_map/ppermute | solution.py:782
  15.0 7.9 %collective-permute-start.7 = (bf16[1,96,768]{2,1,0:T(8,128)(2,1)S(1)}, bf16[1,96,768]{2,1,0:T(8,128)(2,1)S(1)}, u32[]{:S(2)}, u32[]{:S(2)}) collective-permute-start(bf16[1,96,768]{2,1,0:T(8,128)(2,1)S(1)} %collective-permute-done.3.refs_2_.refs_7_.refs_8_), channel_id=1, source_target_pairs={{0,2},{1,3},{2,0},{3,1},{4,6},{5,7},{6,4},{7,5},{8,10},{9,11},{10,... | collective-permute-start | bytes 442376 | tf_op jit(solution)/shard_map/ppermute | solution.py:777
  22.9 30.3 %copy-start.36 = (bf16[1,96,768]{2,1,0:T(8,128)(2,1)}, bf16[1,96,768]{2,1,0:T(8,128)(2,1)S(1)}, u32[]{:S(2)}) copy-start(bf16[1,96,768]{2,1,0:T(8,128)(2,1)S(1)} %collective-permute-done.7.refs_3_.refs_6_.refs_2_.refs_12_) | copy-start | bytes 442372
  22.9 55.8 %copy-start.45 = (bf16[1,96,1536]{2,1,0:T(8,128)(2,1)}, bf16[1,96,1536]{2,1,0:T(8,128)(2,1)S(1)}, u32[]{:S(2)}) copy-start(bf16[1,96,1536]{2,1,0:T(8,128)(2,1)S(1)} %collective-permute-done.6.refs_0_) | copy-start | bytes 884740
  22.9 30.3 %copy-start.46 = (bf16[1,96,1536]{2,1,0:T(8,128)(2,1)}, bf16[1,96,1536]{2,1,0:T(8,128)(2,1)S(1)}, u32[]{:S(2)}) copy-start(bf16[1,96,1536]{2,1,0:T(8,128)(2,1)S(1)} %collective-permute-done.5.refs_2_) | copy-start | bytes 884740
  22.9 11.0 %collective-permute-start.8 = (bf16[3,96,768]{2,1,0:T(8,128)(2,1)S(1)}, bf16[3,96,768]{2,1,0:T(8,128)(2,1)S(1)}, u32[]{:S(2)}, u32[]{:S(2)}) collective-permute-start(bf16[3,96,768]{2,1,0:T(8,128)(2,1)S(1)} %constant_dynamic-update-slice_fusion.refs_1_.refs_6_.refs_7_), channel_id=1, source_target_pairs={{0,4},{4,0},{8,12},{12,8},{16,20},{20,16},{24,28},{28,24},{1,5},{5... | collective-permute-start | bytes 1327112 | tf_op jit(solution)/shard_map/ppermute | solution.py:782
  25.7 28.5 %collective-permute-start.11 = (bf16[1,96,1536]{2,1,0:T(8,128)(2,1)S(1)}, bf16[1,96,1536]{2,1,0:T(8,128)(2,1)S(1)}, u32[]{:S(2)}, u32[]{:S(2)}) collective-permute-start(bf16[1,96,1536]{2,1,0:T(8,128)(2,1)S(1)} %maximum_bitcast_fusion.refs_0_), channel_id=1, source_target_pairs={{0,24},{4,28},{8,16},{12,20},{16,8},{20,12},{24,0},{28,4},{1,25},{... | collective-permute-start | bytes 884744 | tf_op jit(solution)/shard_map/ppermute | solution.py:782
  28.1 26.1 %collective-permute-start.10 = (bf16[1,96,1536]{2,1,0:T(8,128)(2,1)S(1)}, bf16[1,96,1536]{2,1,0:T(8,128)(2,1)S(1)}, u32[]{:S(2)}, u32[]{:S(2)}) collective-permute-start(bf16[1,96,1536]{2,1,0:T(8,128)(2,1)S(1)} %maximum_bitcast_fusion.refs_0_), channel_id=1, source_target_pairs={{0,16},{4,20},{8,24},{12,28},{16,0},{20,4},{24,8},{28,12},{1,17},{... | collective-permute-start | bytes 884744 | tf_op jit(solution)/shard_map/ppermute | solution.py:782
  30.5 23.7 %collective-permute-start.9 = (bf16[1,96,1536]{2,1,0:T(8,128)(2,1)S(1)}, bf16[1,96,1536]{2,1,0:T(8,128)(2,1)S(1)}, u32[]{:S(2)}, u32[]{:S(2)}) collective-permute-start(bf16[1,96,1536]{2,1,0:T(8,128)(2,1)S(1)} %maximum_bitcast_fusion.refs_0_), channel_id=1, source_target_pairs={{0,8},{4,12},{8,0},{12,4},{16,24},{20,28},{24,16},{28,20},{1,9},{5... | collective-permute-start | bytes 884744 | tf_op jit(solution)/shard_map/ppermute | solution.py:782
  30.8 25.3 %collective-permute-start.14 = (bf16[3,96,768]{2,1,0:T(8,128)(2,1)S(1)}, bf16[3,96,768]{2,1,0:T(8,128)(2,1)S(1)}, u32[]{:S(2)}, u32[]{:S(2)}) collective-permute-start(bf16[3,96,768]{2,1,0:T(8,128)(2,1)S(1)} %constant_dynamic-update-slice_fusion.refs_1_.refs_6_.refs_7_), channel_id=1, source_target_pairs={{0,2},{1,3},{2,0},{3,1},{4,6},{5,7},{6,4},{7,5},{8,10},{9,11},{10,... | collective-permute-start | bytes 1327112 | tf_op jit(solution)/shard_map/ppermute | solution.py:777
  34.0 22.2 %collective-permute-start.15 = (bf16[3,96,768]{2,1,0:T(8,128)(2,1)S(1)}, bf16[3,96,768]{2,1,0:T(8,128)(2,1)S(1)}, u32[]{:S(2)}, u32[]{:S(2)}) collective-permute-start(bf16[3,96,768]{2,1,0:T(8,128)(2,1)S(1)} %collective-permute-done.8.refs_3_.refs_8_.refs_9_), channel_id=1, source_target_pairs={{0,2},{1,3},{2,0},{3,1},{4,6},{5,7},{6,4},{7,5},{8,10},{9,11},{10,... | collective-permute-start | bytes 1327112 | tf_op jit(solution)/shard_map/ppermute | solution.py:777
  54.2 19.2 %copy-start.10 = (bf16[2048,768]{1,0:T(8,128)(2,1)}, bf16[2048,768]{1,0:T(8,128)(2,1)S(1)}, u32[]{:S(2)}) copy-start(bf16[2048,768]{1,0:T(8,128)(2,1)S(1)} %get-tuple-element.141.x_ref.normed_ref) | copy-start | bytes 9437188
  54.2 19.2 %copy-start.14 = (bf16[2048,256]{1,0:T(8,128)(2,1)}, bf16[2048,256]{1,0:T(8,128)(2,1)S(1)}, u32[]{:S(2)}) copy-start(bf16[2048,256]{1,0:T(8,128)(2,1)S(1)} %get-tuple-element.159.v_ref) | copy-start | bytes 3145732
  54.2 19.2 %copy-start.17 = (bf16[1024,256]{1,0:T(8,128)(2,1)}, bf16[1024,256]{1,0:T(8,128)(2,1)S(1)}, u32[]{:S(2)}) copy-start(bf16[1024,256]{1,0:T(8,128)(2,1)S(1)} %get-tuple-element.157.q_ref) | copy-start | bytes 1572868
  54.2 19.2 %copy-start.18 = (bf16[1024,256]{1,0:T(8,128)(2,1)}, bf16[1024,256]{1,0:T(8,128)(2,1)S(1)}, u32[]{:S(2)}) copy-start(bf16[1024,256]{1,0:T(8,128)(2,1)S(1)} %get-tuple-element.194.aux_ref) | copy-start | bytes 1572868
  54.3 22.7 %collective-permute-start.13 = (bf16[3,96,1536]{2,1,0:T(8,128)(2,1)S(1)}, bf16[3,96,1536]{2,1,0:T(8,128)(2,1)S(1)}, u32[]{:S(2)}, u32[]{:S(2)}) collective-permute-start(bf16[3,96,1536]{2,1,0:T(8,128)(2,1)S(1)} %pad_maximum_fusion.refs_1_), channel_id=1, source_target_pairs={{0,2},{1,3},{2,0},{3,1},{4,6},{5,7},{6,4},{7,5},{8,10},{9,11},{10,... | collective-permute-start | bytes 2654216 | tf_op jit(solution)/shard_map/ppermute | solution.py:777
  55.6 21.3 %collective-permute-start.12 = (bf16[3,96,1536]{2,1,0:T(8,128)(2,1)S(1)}, bf16[3,96,1536]{2,1,0:T(8,128)(2,1)S(1)}, u32[]{:S(2)}, u32[]{:S(2)}) collective-permute-start(bf16[3,96,1536]{2,1,0:T(8,128)(2,1)S(1)} %pad_maximum_fusion.refs_1_), channel_id=1, source_target_pairs={{0,4},{4,0},{8,12},{12,8},{16,20},{20,16},{24,28},{28,24},{1,5},{5... | collective-permute-start | bytes 2654216 | tf_op jit(solution)/shard_map/ppermute | solution.py:782
  77.0 21.4 %copy-start.37 = (bf16[3,96,1536]{2,1,0:T(8,128)(2,1)}, bf16[3,96,1536]{2,1,0:T(8,128)(2,1)S(1)}, u32[]{:S(2)}) copy-start(bf16[3,96,1536]{2,1,0:T(8,128)(2,1)S(1)} %collective-permute-done.13.refs_1_) | copy-start | bytes 2654212
  77.0 3.6 %collective-permute-start.16 = (bf16[1024,768]{1,0:T(8,128)(2,1)S(1)}, bf16[1024,768]{1,0:T(8,128)(2,1)S(1)}, u32[]{:S(2)}, u32[]{:S(2)}) collective-permute-start(bf16[1024,768]{1,0:T(8,128)(2,1)S(1)} %get-tuple-element.145.a_ref), channel_id=1, source_target_pairs={{0,1},{1,0},{2,3},{3,2},{4,5},{5,4},{6,7},{7,6},{8,9},{9,8},{10,11... | collective-permute-start | bytes 4718600 | tf_op jit(solution)/shard_map/ppermute | solution.py:773
  77.1 26.0 %collective-permute-start.19 = (bf16[1,96,1536]{2,1,0:T(8,128)(2,1)S(1)}, bf16[1,96,1536]{2,1,0:T(8,128)(2,1)S(1)}, u32[]{:S(2)}, u32[]{:S(2)}) collective-permute-start(bf16[1,96,1536]{2,1,0:T(8,128)(2,1)S(1)} %slice.109), channel_id=1, source_target_pairs={{0,4},{4,0},{8,12},{12,8},{16,20},{20,16},{24,28},{28,24},{1,5},{5... | collective-permute-start | bytes 884744 | tf_op jit(solution)/shard_map/ppermute | solution.py:782
  78.7 24.4 %collective-permute-start.17 = (bf16[1,96,1536]{2,1,0:T(8,128)(2,1)S(1)}, bf16[1,96,1536]{2,1,0:T(8,128)(2,1)S(1)}, u32[]{:S(2)}, u32[]{:S(2)}) collective-permute-start(bf16[1,96,1536]{2,1,0:T(8,128)(2,1)S(1)} %collective-permute-done.6.refs_0_), channel_id=1, source_target_pairs={{0,4},{4,0},{8,12},{12,8},{16,20},{20,16},{24,28},{28,24},{1,5},{5... | collective-permute-start | bytes 884744 | tf_op jit(solution)/shard_map/ppermute | solution.py:782
  79.2 23.8 %collective-permute-start.18 = (bf16[2,96,1536]{2,1,0:T(8,128)(2,1)S(1)}, bf16[2,96,1536]{2,1,0:T(8,128)(2,1)S(1)}, u32[]{:S(2)}, u32[]{:S(2)}) collective-permute-start(bf16[2,96,1536]{2,1,0:T(8,128)(2,1)S(1)} %slice.108), channel_id=1, source_target_pairs={{0,2},{1,3},{2,0},{3,1},{4,6},{5,7},{6,4},{7,5},{8,10},{9,11},{10,... | collective-permute-start | bytes 1769480 | tf_op jit(solution)/shard_map/ppermute | solution.py:777
  104.1 20.0 %copy-start.4 = (f32[1,768]{1,0:T(1,128)S(1)}, f32[1,768]{1,0:T(1,128)}, u32[]{:S(2)}) copy-start(f32[1,768]{1,0:T(1,128)} %broadcast_in_dim.35.gain_ref) | copy-start | bytes 9220
  119.3 3.7 %collective-permute-start.20 = (bf16[1024,768]{1,0:T(8,128)(2,1)S(1)}, bf16[1024,768]{1,0:T(8,128)(2,1)S(1)}, u32[]{:S(2)}, u32[]{:S(2)}) collective-permute-start(bf16[1024,768]{1,0:T(8,128)(2,1)S(1)} %get-tuple-element.154.g_ref), channel_id=1, source_target_pairs={{0,1},{1,0},{2,3},{3,2},{4,5},{5,4},{6,7},{7,6},{8,9},{9,8},{10,11... | collective-permute-start | bytes 4718600 | tf_op jit(solution)/shard_map/ppermute | solution.py:773
  119.5 16.7 %collective-permute-start.21 = (bf16[2,96,1536]{2,1,0:T(8,128)(2,1)S(1)}, bf16[2,96,1536]{2,1,0:T(8,128)(2,1)S(1)}, u32[]{:S(2)}, u32[]{:S(2)}) collective-permute-start(bf16[2,96,1536]{2,1,0:T(8,128)(2,1)S(1)} %get-tuple-element.166), channel_id=1, source_target_pairs={{0,2},{1,3},{2,0},{3,1},{4,6},{5,7},{6,4},{7,5},{8,10},{9,11},{10,... | collective-permute-start | bytes 1769480 | tf_op jit(solution)/shard_map/ppermute | solution.py:777
  120.7 16.2 %collective-permute-start.22 = (bf16[2,96,1536]{2,1,0:T(8,128)(2,1)S(1)}, bf16[2,96,1536]{2,1,0:T(8,128)(2,1)S(1)}, u32[]{:S(2)}, u32[]{:S(2)}) collective-permute-start(bf16[2,96,1536]{2,1,0:T(8,128)(2,1)S(1)} %get-tuple-element.167), channel_id=1, source_target_pairs={{0,4},{4,0},{8,12},{12,8},{16,20},{20,16},{24,28},{28,24},{1,5},{5... | collective-permute-start | bytes 1769480 | tf_op jit(solution)/shard_map/ppermute | solution.py:782
  121.8 41.0 %collective-permute-start.27 = (bf16[2,96,1536]{2,1,0:T(8,128)(2,1)S(1)}, bf16[2,96,1536]{2,1,0:T(8,128)(2,1)S(1)}, u32[]{:S(2)}, u32[]{:S(2)}) collective-permute-start(bf16[2,96,1536]{2,1,0:T(8,128)(2,1)S(1)} %get-tuple-element.188), channel_id=1, source_target_pairs={{0,4},{4,0},{8,12},{12,8},{16,20},{20,16},{24,28},{28,24},{1,5},{5... | collective-permute-start | bytes 1769480 | tf_op jit(solution)/shard_map/ppermute | solution.py:782
  137.0 27.1 %collective-permute-start.24 = (bf16[2,96,1536]{2,1,0:T(8,128)(2,1)S(1)}, bf16[2,96,1536]{2,1,0:T(8,128)(2,1)S(1)}, u32[]{:S(2)}, u32[]{:S(2)}) collective-permute-start(bf16[2,96,1536]{2,1,0:T(8,128)(2,1)S(1)} %add_convert_fusion.2), channel_id=1, source_target_pairs={{0,2},{1,3},{2,0},{3,1},{4,6},{5,7},{6,4},{7,5},{8,10},{9,11},{10,... | collective-permute-start | bytes 1769480 | tf_op jit(solution)/shard_map/ppermute | solution.py:777
  138.0 26.2 %collective-permute-start.25 = (bf16[2,96,1536]{2,1,0:T(8,128)(2,1)S(1)}, bf16[2,96,1536]{2,1,0:T(8,128)(2,1)S(1)}, u32[]{:S(2)}, u32[]{:S(2)}) collective-permute-start(bf16[2,96,1536]{2,1,0:T(8,128)(2,1)S(1)} %add_convert_fusion.3), channel_id=1, source_target_pairs={{0,4},{4,0},{8,12},{12,8},{16,20},{20,16},{24,28},{28,24},{1,5},{5... | collective-permute-start | bytes 1769480 | tf_op jit(solution)/shard_map/ppermute | solution.py:782
  139.6 24.6 %collective-permute-start.26 = (bf16[2,96,1536]{2,1,0:T(8,128)(2,1)S(1)}, bf16[2,96,1536]{2,1,0:T(8,128)(2,1)S(1)}, u32[]{:S(2)}, u32[]{:S(2)}) collective-permute-start(bf16[2,96,1536]{2,1,0:T(8,128)(2,1)S(1)} %get-tuple-element.187), channel_id=1, source_target_pairs={{0,2},{1,3},{2,0},{3,1},{4,6},{5,7},{6,4},{7,5},{8,10},{9,11},{10,... | collective-permute-start | bytes 1769480 | tf_op jit(solution)/shard_map/ppermute | solution.py:777
  140.4 30.3 %collective-permute-start.23 = (bf16[384,1024]{1,0:T(8,128)(2,1)S(1)}, bf16[384,1024]{1,0:T(8,128)(2,1)S(1)}, u32[]{:S(2)}, u32[]{:S(2)}) collective-permute-start(bf16[384,1024]{1,0:T(8,128)(2,1)S(1)} %get-tuple-element.175), channel_id=1, source_target_pairs={{0,1},{1,0},{2,3},{3,2},{4,5},{5,4},{6,7},{7,6},{8,9},{9,8},{10,11... | collective-permute-start | bytes 2359304 | tf_op jit(solution)/shard_map/ppermute | solution.py:773
  162.8 33.6 %collective-permute-start.28 = (bf16[8,96,768]{2,1,0:T(8,128)(2,1)S(1)}, bf16[8,96,768]{2,1,0:T(8,128)(2,1)S(1)}, u32[]{:S(2)}, u32[]{:S(2)}) collective-permute-start(bf16[8,96,768]{2,1,0:T(8,128)(2,1)S(1)} %get-tuple-element.181), channel_id=1, source_target_pairs={{0,2},{1,3},{2,0},{3,1},{4,6},{5,7},{6,4},{7,5},{8,10},{9,11},{10,... | collective-permute-start | bytes 3538952 | tf_op jit(solution)/shard_map/ppermute | solution.py:777
  166.2 31.6 %collective-permute-start.31 = (bf16[96,1536]{1,0:T(8,128)(2,1)S(1)}, bf16[96,1536]{1,0:T(8,128)(2,1)S(1)}, u32[]{:S(2)}, u32[]{:S(2)}) collective-permute-start(bf16[96,1536]{1,0:T(8,128)(2,1)S(1)} %get-tuple-element.271), channel_id=1, source_target_pairs={{0,24},{4,28},{8,16},{12,20},{16,8},{20,12},{24,0},{28,4},{1,25},{... | collective-permute-start | bytes 884744 | tf_op jit(solution)/shard_map/ppermute | solution.py:782
  168.6 29.2 %collective-permute-start.30 = (bf16[96,1536]{1,0:T(8,128)(2,1)S(1)}, bf16[96,1536]{1,0:T(8,128)(2,1)S(1)}, u32[]{:S(2)}, u32[]{:S(2)}) collective-permute-start(bf16[96,1536]{1,0:T(8,128)(2,1)S(1)} %get-tuple-element.272), channel_id=1, source_target_pairs={{0,16},{4,20},{8,24},{12,28},{16,0},{20,4},{24,8},{28,12},{1,17},{... | collective-permute-start | bytes 884744 | tf_op jit(solution)/shard_map/ppermute | solution.py:782
  168.6 29.2 %collective-permute-start.29 = (bf16[96,1536]{1,0:T(8,128)(2,1)S(1)}, bf16[96,1536]{1,0:T(8,128)(2,1)S(1)}, u32[]{:S(2)}, u32[]{:S(2)}) collective-permute-start(bf16[96,1536]{1,0:T(8,128)(2,1)S(1)} %get-tuple-element.273), channel_id=1, source_target_pairs={{0,8},{4,12},{8,0},{12,4},{16,24},{20,28},{24,16},{28,20},{1,9},{5... | collective-permute-start | bytes 884744 | tf_op jit(solution)/shard_map/ppermute | solution.py:782
  173.6 26.8 %copy-start.1 = (bf16[2048,768]{1,0:T(8,128)(2,1)S(1)}, bf16[2048,768]{1,0:T(8,128)(2,1)}, u32[]{:S(2)}) copy-start(bf16[2048,768]{1,0:T(8,128)(2,1)} %x_ref.3) | copy-start | bytes 9437188
  196.4 2.7 %collective-permute-start.32 = (f32[1,1664]{1,0:T(1,128)S(1)}, f32[1,1664]{1,0:T(1,128)S(1)}, u32[]{:S(2)}, u32[]{:S(2)}) collective-permute-start(f32[1,1664]{1,0:T(1,128)S(1)} %pad_maximum_fusion.1), channel_id=1, source_target_pairs={{0,1},{1,0},{2,3},{3,2},{4,5},{5,4},{6,7},{7,6},{8,9},{9,8},{10,11... | collective-permute-start | bytes 19976 | tf_op jit(solution)/shard_map/ppermute | solution.py:773
  196.5 19.6 %copy-start.21 = (bf16[8,96,768]{2,1,0:T(8,128)(2,1)}, bf16[8,96,768]{2,1,0:T(8,128)(2,1)S(1)}, u32[]{:S(2)}) copy-start(bf16[8,96,768]{2,1,0:T(8,128)(2,1)S(1)} %collective-permute-done.28) | copy-start | bytes 3538948
  196.5 19.6 %collective-permute-start.35 = (bf16[192,1024]{1,0:T(8,128)(2,1)S(1)}, bf16[192,1024]{1,0:T(8,128)(2,1)S(1)}, u32[]{:S(2)}, u32[]{:S(2)}) collective-permute-start(bf16[192,1024]{1,0:T(8,128)(2,1)S(1)} %get-tuple-element.213), channel_id=1, source_target_pairs={{0,2},{1,3},{2,0},{3,1},{4,6},{5,7},{6,4},{7,5},{8,10},{9,11},{10,... | collective-permute-start | bytes 1179656 | tf_op jit(solution)/shard_map/ppermute | solution.py:777
  197.9 18.1 %collective-permute-start.34 = (bf16[4,96,768]{2,1,0:T(8,128)(2,1)S(1)}, bf16[4,96,768]{2,1,0:T(8,128)(2,1)S(1)}, u32[]{:S(2)}, u32[]{:S(2)}) collective-permute-start(bf16[4,96,768]{2,1,0:T(8,128)(2,1)S(1)} %add_convert_fusion.1), channel_id=1, source_target_pairs={{0,4},{4,0},{8,12},{12,8},{16,20},{20,16},{24,28},{28,24},{1,5},{5... | collective-permute-start | bytes 1769480 | tf_op jit(solution)/shard_map/ppermute | solution.py:782
  199.1 16.9 %collective-permute-start.33 = (f32[1,1664]{1,0:T(1,128)S(1)}, f32[1,1664]{1,0:T(1,128)S(1)}, u32[]{:S(2)}, u32[]{:S(2)}) collective-permute-start(f32[1,1664]{1,0:T(1,128)S(1)} %fusion.11), channel_id=1, source_target_pairs={{0,2},{1,3},{2,0},{3,1},{4,6},{5,7},{6,4},{7,5},{8,10},{9,11},{10,... | collective-permute-start | bytes 19976 | tf_op jit(solution)/shard_map/ppermute | solution.py:777
  216.6 5.3 %collective-permute-start.36 = (bf16[384,2048]{1,0:T(8,128)(2,1)}, bf16[384,2048]{1,0:T(8,128)(2,1)}, u32[]{:S(2)}, u32[]{:S(2)}) collective-permute-start(bf16[384,2048]{1,0:T(8,128)(2,1)} %get-tuple-element.215), channel_id=1, source_target_pairs={{0,1},{1,0},{2,3},{3,2},{4,5},{5,4},{6,7},{7,6},{8,9},{9,8},{10,11... | collective-permute-start | bytes 4718600 | tf_op jit(solution)/shard_map/ppermute | solution.py:773
  218.2 3.7 %collective-permute-start.37 = (f32[1,1664]{1,0:T(1,128)S(1)}, f32[1,1664]{1,0:T(1,128)S(1)}, u32[]{:S(2)}, u32[]{:S(2)}) collective-permute-start(f32[1,1664]{1,0:T(1,128)S(1)} %add.138), channel_id=1, source_target_pairs={{0,4},{4,0},{8,12},{12,8},{16,20},{20,16},{24,28},{28,24},{1,5},{5... | collective-permute-start | bytes 19976 | tf_op jit(solution)/shard_map/ppermute | solution.py:782
  223.3 18.9 %collective-permute-start.38 = (bf16[192,2048]{1,0:T(8,128)(2,1)S(1)}, bf16[192,2048]{1,0:T(8,128)(2,1)S(1)}, u32[]{:S(2)}, u32[]{:S(2)}) collective-permute-start(bf16[192,2048]{1,0:T(8,128)(2,1)S(1)} %add_convert_fusion), channel_id=1, source_target_pairs={{0,2},{1,3},{2,0},{3,1},{4,6},{5,7},{6,4},{7,5},{8,10},{9,11},{10,... | collective-permute-start | bytes 2359304 | tf_op jit(solution)/shard_map/ppermute | solution.py:777
  224.3 5.5 %collective-permute-start.44 = (f32[1,1664]{1,0:T(1,128)S(1)}, f32[1,1664]{1,0:T(1,128)S(1)}, u32[]{:S(2)}, u32[]{:S(2)}) collective-permute-start(f32[1,1664]{1,0:T(1,128)S(1)} %add.139), channel_id=1, source_target_pairs={{0,24},{4,28},{8,16},{12,20},{16,8},{20,12},{24,0},{28,4},{1,25},{... | collective-permute-start | bytes 19976 | tf_op jit(solution)/shard_map/ppermute | solution.py:782
  226.6 5.0 %collective-permute-start.43 = (f32[1,1664]{1,0:T(1,128)S(1)}, f32[1,1664]{1,0:T(1,128)S(1)}, u32[]{:S(2)}, u32[]{:S(2)}) collective-permute-start(f32[1,1664]{1,0:T(1,128)S(1)} %add.139), channel_id=1, source_target_pairs={{0,16},{4,20},{8,24},{12,28},{16,0},{20,4},{24,8},{28,12},{1,17},{... | collective-permute-start | bytes 19976 | tf_op jit(solution)/shard_map/ppermute | solution.py:782
  226.6 7.3 %collective-permute-start.42 = (f32[1,1664]{1,0:T(1,128)S(1)}, f32[1,1664]{1,0:T(1,128)S(1)}, u32[]{:S(2)}, u32[]{:S(2)}) collective-permute-start(f32[1,1664]{1,0:T(1,128)S(1)} %add.139), channel_id=1, source_target_pairs={{0,8},{4,12},{8,0},{12,4},{16,24},{20,28},{24,16},{28,20},{1,9},{5... | collective-permute-start | bytes 19976 | tf_op jit(solution)/shard_map/ppermute | solution.py:782
  228.6 7.5 %collective-permute-start.39 = (bf16[96,768]{1,0:T(8,128)(2,1)S(1)}, bf16[96,768]{1,0:T(8,128)(2,1)S(1)}, u32[]{:S(2)}, u32[]{:S(2)}) collective-permute-start(bf16[96,768]{1,0:T(8,128)(2,1)S(1)} %get-tuple-element.226), channel_id=1, source_target_pairs={{0,8},{4,12},{8,0},{12,4},{16,24},{20,28},{24,16},{28,20},{1,9},{5... | collective-permute-start | bytes 442376 | tf_op jit(solution)/shard_map/ppermute | solution.py:782
  229.8 12.3 %collective-permute-start.40 = (bf16[96,768]{1,0:T(8,128)(2,1)S(1)}, bf16[96,768]{1,0:T(8,128)(2,1)S(1)}, u32[]{:S(2)}, u32[]{:S(2)}) collective-permute-start(bf16[96,768]{1,0:T(8,128)(2,1)S(1)} %get-tuple-element.227), channel_id=1, source_target_pairs={{0,16},{4,20},{8,24},{12,28},{16,0},{20,4},{24,8},{28,12},{1,17},{... | collective-permute-start | bytes 442376 | tf_op jit(solution)/shard_map/ppermute | solution.py:782
  231.5 10.6 %collective-permute-start.41 = (bf16[96,768]{1,0:T(8,128)(2,1)S(1)}, bf16[96,768]{1,0:T(8,128)(2,1)S(1)}, u32[]{:S(2)}, u32[]{:S(2)}) collective-permute-start(bf16[96,768]{1,0:T(8,128)(2,1)S(1)} %get-tuple-element.228), channel_id=1, source_target_pairs={{0,24},{4,28},{8,16},{12,20},{16,8},{20,12},{24,0},{28,4},{1,25},{... | collective-permute-start | bytes 442376 | tf_op jit(solution)/shard_map/ppermute | solution.py:782
  (30 other events, 74.5 us)
